TPU v7x, 512 devices: a whole 4x8x8 slice. The times are simulated.
512 devices in a mesh: frame: 16 (over y_hi, z), row: 32 (over y_lo, x, core).
Axes of the slice: x: 4, y: 8 (y_hi: 2, y_lo: 4; y = y_hi * 4 + y_lo), z: 8, core: 2. Of those that a mesh axis runs over, the one named last changes fastest.
Arguments:
- fine: bfloat16 [32, 320, 128, 128], P('frame', None, 'row'), may hold values from -6 to 6
- coarse: bfloat16 [4, 256, 1280], P(None, 'row', 'frame'), may hold values from -6 to 6
- w_qkv: bfloat16 [3, 1280, 1280], P(None, None, 'frame'), may hold values from -0.15625 to 0.15625
- w_out: bfloat16 [1280, 1280], P('frame'), may hold values from -0.15625 to 0.15625
- w_up: bfloat16 [1280, 320], P('frame'), may hold values from -0.15625 to 0.15625
- gain_one: float32 [320], replicated, may hold values from 0.1 to 1.9
- conv_space: bfloat16 [3, 3, 320, 320], replicated, may hold values from -0.109375 to 0.109375
- gain_two: float32 [320], replicated, may hold values from 0.1 to 1.9
- conv_time: bfloat16 [3, 320, 320], replicated, may hold values from -0.1875 to 0.1875
Outputs:
- result: bfloat16 [32, 320, 128, 128], P('frame', None, 'row')
All inputs are finite; a program needn't handle non-finite values.
Results may differ from a plain program's by a relative error of at most 0.013.
Values may be sent and summed in bfloat16 or wider, within the bound.
No kernel may reach another device: no remote copies, remote signals or barrier semaphores. Data moves between devices by JAX's collectives and lax.ppermute only.
A program may use at most 64 MiB of HBM per device.

v0:
```python
import math

import jax
import jax.numpy as jnp
from jax import lax
from jax.sharding import PartitionSpec as P

HD = 80


def in_order(blocks, dim):
    shape = list(blocks.shape[1:])
    shape[dim] *= blocks.shape[0]
    return jnp.moveaxis(blocks, 0, dim).reshape(shape)


def copy_for_each(array, axis):
    devices = lax.axis_size(axis)
    return lax.all_to_all(
        jnp.broadcast_to(array[None], (devices, *array.shape)), axis, 0, 0, tiled=True
    )


def collect(array, axis, dim):
    return in_order(copy_for_each(array, axis), dim)


def cut_along(array, dim, devices):
    before, after = (array.shape[:dim], array.shape[dim + 1 :])
    return jnp.moveaxis(array.reshape(*before, devices, -1, *after), dim, 0)


def summed_on_arrival(array, axis, dim):
    blocks = cut_along(array, dim, lax.axis_size(axis))
    arrived = lax.all_to_all(blocks, axis, split_axis=0, concat_axis=0, tiled=True)
    return arrived.sum(axis=0)


def over_copies(array, axis):
    return copy_for_each(array, axis).sum(axis=0)


def from_partner(value, axis, apart):
    mask = 2**apart
    pairs = [(source, source ^ mask) for source in range(lax.axis_size(axis))]
    return lax.ppermute(value, axis, pairs)


def with_halo(cells, sides, width):
    for axis, dim in sides:
        count = lax.axis_size(axis)
        ends = count - 1
        head = lax.slice_in_dim(cells, 0, width, axis=dim)
        tail = lax.slice_in_dim(cells, cells.shape[dim] - width, cells.shape[dim], axis=dim)
        cells = jnp.concatenate(
            [
                lax.ppermute(tail, axis, [(i, (i + 1) % count) for i in range(ends)]),
                cells,
                lax.ppermute(head, axis, [((i + 1) % count, i) for i in range(ends)]),
            ],
            axis=dim,
        )
    return cells


def norm_silu(values, gain):
    square = jnp.mean(values * values, axis=1, keepdims=True)
    scaled = values * lax.rsqrt(square + 1e-06) * gain[None, :, None, None]
    return jax.nn.silu(scaled).astype(jnp.bfloat16)


def convolve_space(extended, conv_space):
    padded = jnp.pad(extended, ((0, 0), (0, 0), (0, 0), (1, 1)))
    rows_here = extended.shape[2] - 2
    width = extended.shape[3]
    spatial = None
    for offset_y in range(3):
        for offset_x in range(3):
            window = padded[:, :, offset_y : offset_y + rows_here, offset_x : offset_x + width]
            term = jnp.einsum(
                "fcrw,cd->fdrw",
                window,
                conv_space[offset_y, offset_x],
                preferred_element_type=jnp.float32,
            )
            spatial = term if spatial is None else spatial + term
    return spatial


def local(fine, coarse, w_qkv, w_out, w_up, gain_one, conv_space, gain_two, conv_time):
    frame_count = lax.axis_size("frame")
    f_dev = fine.shape[0]
    width = fine.shape[3]
    cf_count, p_dev, c_dev = coarse.shape
    heads_local = w_qkv.shape[2] // HD
    qkv = jnp.einsum(
        "fpc,icd->ifpd", collect(coarse, "frame", 2), w_qkv, preferred_element_type=jnp.float32
    ).astype(jnp.bfloat16)
    query = qkv[0].reshape(cf_count, p_dev, heads_local, HD)
    keys = qkv[1].reshape(cf_count, p_dev, heads_local, HD)
    values = qkv[2].reshape(cf_count, p_dev, heads_local, HD)
    scores = jnp.einsum(
        "fphd,gphd->phfg", query, keys, preferred_element_type=jnp.float32
    ) / math.sqrt(HD)
    probs = jax.nn.softmax(scores, axis=-1).astype(jnp.bfloat16)
    attn = jnp.einsum("phfg,gphd->fphd", probs, values, preferred_element_type=jnp.float32).astype(
        jnp.bfloat16
    )
    attn = attn.reshape(cf_count * p_dev, heads_local * HD)
    partial_out = jnp.dot(attn, w_out, preferred_element_type=jnp.float32).reshape(
        cf_count, p_dev, -1
    )
    share = summed_on_arrival(partial_out, "frame", 2)
    coarse_out = (coarse.astype(jnp.float32) + share).astype(jnp.bfloat16)
    up_partial = jnp.einsum("fpc,cd->fpd", coarse_out, w_up, preferred_element_type=jnp.float32)
    up_cells = over_copies(up_partial, "frame").astype(jnp.bfloat16)
    partner = from_partner(up_cells, "row", 0)
    is_even = lax.axis_index("row") % 2 == 0
    coarse_row = jnp.where(
        is_even,
        jnp.concatenate([up_cells, partner], axis=1),
        jnp.concatenate([partner, up_cells], axis=1),
    )
    global_frames = lax.axis_index("frame") * f_dev + jnp.arange(f_dev, dtype=jnp.int32)
    target = global_frames * cf_count // (f_dev * frame_count)
    select = (target[:, None] == jnp.arange(cf_count, dtype=jnp.int32)[None, :]).astype(jnp.float32)
    picked = jnp.einsum("tk,kwc->tcw", select, coarse_row.astype(jnp.float32))
    widened = jnp.repeat(picked, width // picked.shape[2], axis=2)
    merged = (fine.astype(jnp.float32) + widened[:, :, None, :]).astype(jnp.bfloat16)
    first = norm_silu(merged.astype(jnp.float32), gain_one)
    extended = with_halo(first, (("row", 2),), 1)
    second = norm_silu(convolve_space(extended, conv_space), gain_two)
    second_ext = with_halo(second, (("frame", 0),), 1)
    temporal = None
    for offset in range(3):
        term = jnp.einsum(
            "fcrw,cd->fdrw",
            second_ext[offset : offset + f_dev],
            conv_time[offset],
            preferred_element_type=jnp.float32,
        )
        temporal = term if temporal is None else temporal + term
    return (merged.astype(jnp.float32) + temporal).astype(jnp.bfloat16)


def solution(mesh):
    return jax.shard_map(
        local,
        mesh=mesh,
        in_specs=(
            P("frame", None, "row", None),
            P(None, "row", "frame"),
            P(None, None, "frame"),
            P("frame", None),
            P("frame", None),
            P(),
            P(),
            P(),
            P(),
        ),
        out_specs=P("frame", None, "row", None),
        check_vma=False,
    )
```

profile of v0, /device:TPU:55, one launch (start us, length us, event | category | flops | bytes accessed | tf_op | source)
XLA Modules:
  0.0 126.6 jit_solution(5074941928840200985)
XLA Ops:
  0.0 1.4 %broadcast_in_dim.6 = bf16[16,4,8,80]{3,2,1,0:T(8,128)(2,1)} broadcast(bf16[4,8,80]{2,1,0:T(8,128)(2,1)} %param.10), dimensions={1,2,3} | broadcast | bytes 87040 | tf_op jit(solution)/shard_map/broadcast_in_dim | solution.py:20
  1.4 15.1 %all-to-all-start = ((bf16[16,4,8,80]{3,2,1,0:T(8,128)(2,1)}), bf16[16,4,8,80]{3,2,1,0:T(8,128)(2,1)S(1)}, u32[]{:S(2)}, u32[]{:S(2)}) async-start(bf16[16,4,8,80]{3,2,1,0:T(8,128)(2,1)} %broadcast_in_dim.6), calls=%async_computation | async-start | bytes 262144 | tf_op jit(solution)/shard_map/all_to_all | solution.py:19
  16.6 1.1 copy.111
  17.7 5.6 %all-to-all-done = bf16[16,4,8,80]{3,2,1,0:T(8,128)(2,1)S(1)} async-done(((bf16[16,4,8,80]{3,2,1,0:T(8,128)(2,1)}), bf16[16,4,8,80]{3,2,1,0:T(8,128)(2,1)S(1)}, u32[]{:S(2)}, u32[]{:S(2)}) %all-to-all-start) | async-done | bytes 81952 | tf_op jit(solution)/shard_map/all_to_all | solution.py:19
  23.3 0.1 copy.73
  23.4 0.2 reshape.85
  23.6 0.0 copy-start.4
  23.6 0.0 copy-start.5
  23.6 0.3 fusion.28
  23.9 0.2 fusion.105
  24.1 0.5 convolution_bitcast_fusion
  24.6 0.2 copy.79
  24.8 15.7 %all_to_all.15 = f32[16,4,8,80]{3,2,1,0:T(8,128)S(1)} all-to-all(f32[16,4,8,80]{3,2,1,0:T(8,128)S(1)} %copy.79), channel_id=1, replica_groups=mesh['frame'=16,'row'=32] {'frame'}, dimensions={0} | all-to-all | bytes 327680 | tf_op jit(solution)/shard_map/all_to_all | solution.py:35
  40.6 0.1 fusion.76
  40.7 1.0 broadcast_in_dim.7
  41.7 10.2 %all-to-all-start.2 = ((f32[16,4,8,320]{3,2,1,0:T(8,128)}), f32[16,4,8,320]{3,2,1,0:T(8,128)S(1)}, u32[]{:S(2)}, u32[]{:S(2)}) async-start(f32[16,4,8,320]{3,2,1,0:T(8,128)} %broadcast_in_dim.7), calls=%async_computation.2 | async-start | bytes 1572864 | tf_op jit(solution)/shard_map/all_to_all | solution.py:19
  51.9 17.8 %all-to-all-done.2 = f32[16,4,8,320]{3,2,1,0:T(8,128)S(1)} async-done(((f32[16,4,8,320]{3,2,1,0:T(8,128)}), f32[16,4,8,320]{3,2,1,0:T(8,128)S(1)}, u32[]{:S(2)}, u32[]{:S(2)}) %all-to-all-start.2) | async-done | bytes 655392 | tf_op jit(solution)/shard_map/all_to_all | solution.py:19
  69.6 0.1 reduce_sum.47
  69.7 0.0 copy-start.6
  69.7 5.9 %collective-permute-start = (bf16[4,8,320]{2,1,0:T(8,128)(2,1)S(1)}, bf16[4,8,320]{2,1,0:T(8,128)(2,1)S(1)}, u32[]{:S(2)}, u32[]{:S(2)}) collective-permute-start(bf16[4,8,320]{2,1,0:T(8,128)(2,1)S(1)} %reduce_sum.47), channel_id=1, source_target_pairs={{0,1},{1,0},{2,3},{3,2},{4,5},{5,4},{6,7},{7,6},{8,9},{9,8},{10,11... | collective-permute-start | bytes 61448 | tf_op jit(solution)/shard_map/ppermute | solution.py:46
  75.6 0.8 collective-permute-done
  76.4 0.2 convolution_bitcast_fusion.1
  76.7 0.2 copy.82
  76.9 0.1 fusion.16
  77.1 0.5 fusion.23
  77.6 5.4 %collective-permute-start.1 = (bf16[2,320,1,128]{3,1,2,0:T(8,128)(2,1)S(1)}, bf16[2,320,1,128]{3,1,2,0:T(8,128)(2,1)S(1)}, u32[]{:S(2)}, u32[]{:S(2)}) collective-permute-start(bf16[2,320,1,128]{3,1,2,0:T(8,128)(2,1)S(1)} %get-tuple-element.7), channel_id=1, source_target_pairs={{0,1},{1,2},{2,3},{3,4},{4,5},{5,6},{6,7},{7,8},{8,9},{9,10},{10,1... | collective-permute-start | bytes 491528 | tf_op jit(solution)/shard_map/ppermute | solution.py:57
  82.9 1.9 %collective-permute-start.2 = (bf16[2,320,1,128]{3,1,2,0:T(8,128)(2,1)S(1)}, bf16[2,320,1,128]{3,1,2,0:T(8,128)(2,1)S(1)}, u32[]{:S(2)}, u32[]{:S(2)}) collective-permute-start(bf16[2,320,1,128]{3,1,2,0:T(8,128)(2,1)S(1)} %get-tuple-element.8), channel_id=1, source_target_pairs={{1,0},{2,1},{3,2},{4,3},{5,4},{6,5},{7,6},{8,7},{9,8},{10,9},{11,1... | collective-permute-start | bytes 491528 | tf_op jit(solution)/shard_map/ppermute | solution.py:59
  84.9 0.5 fusion.58
  85.4 6.3 %collective-permute-done.2 = bf16[2,320,1,128]{3,1,2,0:T(8,128)(2,1)S(1)} collective-permute-done((bf16[2,320,1,128]{3,1,2,0:T(8,128)(2,1)S(1)}, bf16[2,320,1,128]{3,1,2,0:T(8,128)(2,1)S(1)}, u32[]{:S(2)}, u32[]{:S(2)}) %collective-permute-start.2) | collective-permute-done | bytes 163872 | tf_op jit(solution)/shard_map/ppermute | solution.py:59
  91.7 1.0 fusion.6
  92.7 0.5 fusion.42
  93.2 0.7 fusion.44
  93.9 0.7 fusion.35
  94.6 0.5 fusion.39
  95.1 0.5 fusion.46
  95.6 0.6 fusion.14
  96.2 0.5 fusion.37
  96.7 0.0 copy-start.7
  96.8 0.9 multiply_reduce_fusion
  97.7 0.5 fusion.27
  98.2 5.5 %collective-permute-start.4 = (bf16[1,320,4,128]{3,1,2,0:T(8,128)(2,1)S(1)}, bf16[1,320,4,128]{3,1,2,0:T(8,128)(2,1)S(1)}, u32[]{:S(2)}, u32[]{:S(2)}) collective-permute-start(bf16[1,320,4,128]{3,1,2,0:T(8,128)(2,1)S(1)} %get-tuple-element.6), channel_id=1, source_target_pairs={{32,0},{64,32},{96,64},{128,96},{160,128},{192,160},{224,192},{256... | collective-permute-start | bytes 983048 | tf_op jit(solution)/shard_map/ppermute | solution.py:59
  103.8 1.9 %collective-permute-start.3 = (bf16[1,320,4,128]{3,1,2,0:T(8,128)(2,1)S(1)}, bf16[1,320,4,128]{3,1,2,0:T(8,128)(2,1)S(1)}, u32[]{:S(2)}, u32[]{:S(2)}) collective-permute-start(bf16[1,320,4,128]{3,1,2,0:T(8,128)(2,1)S(1)} %get-tuple-element.5), channel_id=1, source_target_pairs={{0,32},{32,64},{64,96},{96,128},{128,160},{160,192},{192,224},{224... | collective-permute-start | bytes 983048 | tf_op jit(solution)/shard_map/ppermute | solution.py:57
  105.7 0.5 fusion.51
  106.2 8.4 %collective-permute-done.4 = bf16[1,320,4,128]{3,1,2,0:T(8,128)(2,1)S(1)} collective-permute-done((bf16[1,320,4,128]{3,1,2,0:T(8,128)(2,1)S(1)}, bf16[1,320,4,128]{3,1,2,0:T(8,128)(2,1)S(1)}, u32[]{:S(2)}, u32[]{:S(2)}) %collective-permute-start.4) | collective-permute-done | bytes 327712 | tf_op jit(solution)/shard_map/ppermute | solution.py:59
  114.6 0.5 fusion.32
  115.1 9.5 %collective-permute-done.3 = bf16[1,320,4,128]{3,1,2,0:T(8,128)(2,1)S(1)} collective-permute-done((bf16[1,320,4,128]{3,1,2,0:T(8,128)(2,1)S(1)}, bf16[1,320,4,128]{3,1,2,0:T(8,128)(2,1)S(1)}, u32[]{:S(2)}, u32[]{:S(2)}) %collective-permute-start.3) | collective-permute-done | bytes 327712 | tf_op jit(solution)/shard_map/ppermute | solution.py:57
  124.6 0.6 fusion.15
  125.3 1.3 %copy.95 = bf16[2,320,4,128]{3,2,1,0:T(4,128)(2,1)} copy(bf16[2,320,4,128]{3,1,2,0:T(8,128)(2,1)S(1)} %fusion.15) | data formatting | bytes 1310720 | tf_op jit(solution)/shard_map/convert_element_type | solution.py:143
  (23 shorter events, 0.2 us)
Async XLA Ops:
  0.0 23.6 %copy-start = (bf16[3,1280,80]{1,2,0:T(8,128)(2,1)S(1)}, bf16[3,1280,80]{1,2,0:T(8,128)(2,1)}, u32[]{:S(2)}) copy-start(bf16[3,1280,80]{1,2,0:T(8,128)(2,1)} %param.11) | copy-start | bytes 1843204
  1.4 21.9 %all-to-all-start = ((bf16[16,4,8,80]{3,2,1,0:T(8,128)(2,1)}), bf16[16,4,8,80]{3,2,1,0:T(8,128)(2,1)S(1)}, u32[]{:S(2)}, u32[]{:S(2)}) async-start(bf16[16,4,8,80]{3,2,1,0:T(8,128)(2,1)} %broadcast_in_dim.6), calls=%async_computation | async-start | bytes 262144 | tf_op jit(solution)/shard_map/all_to_all | solution.py:19
  23.6 17.0 %copy-start.4 = (bf16[80,320]{1,0:T(8,128)(2,1)S(1)}, bf16[80,320]{1,0:T(8,128)(2,1)}, u32[]{:S(2)}) copy-start(bf16[80,320]{1,0:T(8,128)(2,1)} %param.13) | copy-start | bytes 153604
  23.6 17.0 %copy-start.5 = (bf16[4,8,80]{2,1,0:T(8,128)(2,1)S(1)}, bf16[4,8,80]{2,1,0:T(8,128)(2,1)}, u32[]{:S(2)}) copy-start(bf16[4,8,80]{2,1,0:T(8,128)(2,1)} %param.10) | copy-start | bytes 15364
  41.7 28.0 %all-to-all-start.2 = ((f32[16,4,8,320]{3,2,1,0:T(8,128)}), f32[16,4,8,320]{3,2,1,0:T(8,128)S(1)}, u32[]{:S(2)}, u32[]{:S(2)}) async-start(f32[16,4,8,320]{3,2,1,0:T(8,128)} %broadcast_in_dim.7), calls=%async_computation.2 | async-start | bytes 1572864 | tf_op jit(solution)/shard_map/all_to_all | solution.py:19
  51.9 25.0 %copy-start.1 = (bf16[2,320,4,128]{3,2,1,0:T(4,128)(2,1)S(1)}, bf16[2,320,4,128]{3,2,1,0:T(4,128)(2,1)}, u32[]{:S(2)}) copy-start(bf16[2,320,4,128]{3,2,1,0:T(4,128)(2,1)} %param.9) | copy-start | bytes 1966084
  69.7 7.4 %copy-start.6 = (f32[320]{0:T(512)S(1)}, f32[320]{0:T(512)}, u32[]{:S(2)}) copy-start(f32[320]{0:T(512)} %param.14) | copy-start | bytes 3844
  69.7 6.7 %collective-permute-start = (bf16[4,8,320]{2,1,0:T(8,128)(2,1)S(1)}, bf16[4,8,320]{2,1,0:T(8,128)(2,1)S(1)}, u32[]{:S(2)}, u32[]{:S(2)}) collective-permute-start(bf16[4,8,320]{2,1,0:T(8,128)(2,1)S(1)} %reduce_sum.47), channel_id=1, source_target_pairs={{0,1},{1,0},{2,3},{3,2},{4,5},{5,4},{6,7},{7,6},{8,9},{9,8},{10,11... | collective-permute-start | bytes 61448 | tf_op jit(solution)/shard_map/ppermute | solution.py:46
  77.0 7.9 %copy-start.2 = (bf16[3,3,320,320]{3,2,1,0:T(8,128)(2,1)S(1)}, bf16[3,3,320,320]{3,2,1,0:T(8,128)(2,1)}, u32[]{:S(2)}) copy-start(bf16[3,3,320,320]{3,2,1,0:T(8,128)(2,1)} %param.15) | copy-start | bytes 5529604
  77.6 7.9 %collective-permute-start.1 = (bf16[2,320,1,128]{3,1,2,0:T(8,128)(2,1)S(1)}, bf16[2,320,1,128]{3,1,2,0:T(8,128)(2,1)S(1)}, u32[]{:S(2)}, u32[]{:S(2)}) collective-permute-start(bf16[2,320,1,128]{3,1,2,0:T(8,128)(2,1)S(1)} %get-tuple-element.7), channel_id=1, source_target_pairs={{0,1},{1,2},{2,3},{3,4},{4,5},{5,6},{6,7},{7,8},{8,9},{9,10},{10,1... | collective-permute-start | bytes 491528 | tf_op jit(solution)/shard_map/ppermute | solution.py:57
  82.9 8.7 %collective-permute-start.2 = (bf16[2,320,1,128]{3,1,2,0:T(8,128)(2,1)S(1)}, bf16[2,320,1,128]{3,1,2,0:T(8,128)(2,1)S(1)}, u32[]{:S(2)}, u32[]{:S(2)}) collective-permute-start(bf16[2,320,1,128]{3,1,2,0:T(8,128)(2,1)S(1)} %get-tuple-element.8), channel_id=1, source_target_pairs={{1,0},{2,1},{3,2},{4,3},{5,4},{6,5},{7,6},{8,7},{9,8},{10,9},{11,1... | collective-permute-start | bytes 491528 | tf_op jit(solution)/shard_map/ppermute | solution.py:59
  96.7 0.9 copy-start.7
  97.7 8.0 %copy-start.3 = (bf16[3,320,320]{2,1,0:T(8,128)(2,1)S(1)}, bf16[3,320,320]{2,1,0:T(8,128)(2,1)}, u32[]{:S(2)}) copy-start(bf16[3,320,320]{2,1,0:T(8,128)(2,1)} %param.17) | copy-start | bytes 1843204
  98.2 16.4 %collective-permute-start.4 = (bf16[1,320,4,128]{3,1,2,0:T(8,128)(2,1)S(1)}, bf16[1,320,4,128]{3,1,2,0:T(8,128)(2,1)S(1)}, u32[]{:S(2)}, u32[]{:S(2)}) collective-permute-start(bf16[1,320,4,128]{3,1,2,0:T(8,128)(2,1)S(1)} %get-tuple-element.6), channel_id=1, source_target_pairs={{32,0},{64,32},{96,64},{128,96},{160,128},{192,160},{224,192},{256... | collective-permute-start | bytes 983048 | tf_op jit(solution)/shard_map/ppermute | solution.py:59
  103.8 20.9 %collective-permute-start.3 = (bf16[1,320,4,128]{3,1,2,0:T(8,128)(2,1)S(1)}, bf16[1,320,4,128]{3,1,2,0:T(8,128)(2,1)S(1)}, u32[]{:S(2)}, u32[]{:S(2)}) collective-permute-start(bf16[1,320,4,128]{3,1,2,0:T(8,128)(2,1)S(1)} %get-tuple-element.5), channel_id=1, source_target_pairs={{0,32},{32,64},{64,96},{96,128},{128,160},{160,192},{192,224},{224... | collective-permute-start | bytes 983048 | tf_op jit(solution)/shard_map/ppermute | solution.py:57
where the time goes:
time: 127 us
  waiting for transfers between devices  48.3 us (38%)
  starting transfers between devices  46 us (36%)
  blocking collectives  15.7 us (12%)
  matrix products  8.44 us (7%)
  local copies, waits for them, and re-layouts  5.59 us (4%)
  other arithmetic  2.17 us (2%)
    all_to_all x2, starting transfers between devices, copy_for_each(): lax.all_to_all(jnp.broadcast_to(array[None], (devices, *array.shape)), ax...  25.3 us
    all_to_all x2, waiting for transfers between devices, copy_for_each(): lax.all_to_all(jnp.broadcast_to(array[None], (devices, *array.shape)), ax...  23.4 us
    all_to_all x1, blocking collectives, summed_on_arrival(): lax.all_to_all(blocks, axis, split_axis=0, concat_axis=0, tiled=True)  15.7 us
    ppermute x2, waiting for transfers between devices, with_halo(): lax.ppermute(head, axis, [((i + 1) % count, i) for i in range(ends)])  14.6 us
    ppermute x2, waiting for transfers between devices, with_halo(): lax.ppermute(tail, axis, [(i, (i + 1) % count) for i in range(ends)])  9.51 us
    ppermute x2, starting transfers between devices, with_halo(): lax.ppermute(head, axis, [((i + 1) % count, i) for i in range(ends)])  7.47 us
    ppermute x2, starting transfers between devices, with_halo(): lax.ppermute(tail, axis, [(i, (i + 1) % count) for i in range(ends)])  7.3 us
    ppermute x1, starting transfers between devices, from_partner(): return lax.ppermute(value, axis, pairs)  5.89 us
  transfers between devices with their start and end apart: 7, of which 6 were waited for; matrix products, arithmetic and copies ran while one was open for 2% of the time, Pallas kernels for 0%

commit v1 on v0

v1 whole, which is shorter than its diff:
```python
import math

import jax
import jax.numpy as jnp
from jax import lax
from jax.experimental import pallas as pl
from jax.sharding import PartitionSpec as P

HD = 80


def send_all(message, axis, count, groups=None):
    copies = jnp.broadcast_to(message[None], (count, *message.shape))
    return lax.all_to_all(copies, axis, 0, 0, tiled=True, axis_index_groups=groups)


def project(both, folded, w_up, wanted):
    cf, cells, width = both.shape[1:]

    def body(both_ref, folded_ref, up_ref, out_ref):
        attn = both_ref[0].reshape(cf * cells, width)
        inputs = both_ref[1].reshape(cf * cells, width)
        partial = lax.dot_general(
            attn, folded_ref[...], (((1,), (1,)), ((), ())), preferred_element_type=jnp.float32
        )
        partial += jnp.dot(inputs, up_ref[...], preferred_element_type=jnp.float32)
        partial = partial.astype(jnp.bfloat16)
        for place, source in enumerate(wanted):
            out_ref[place] = partial[source * cells : (source + 1) * cells]

    return pl.pallas_call(
        body,
        out_shape=jax.ShapeDtypeStruct((len(wanted), cells, w_up.shape[1]), jnp.bfloat16),
        name="project",
    )(both, folded, w_up)


def norm_silu(values, gain):
    square = jnp.mean(values * values, axis=2, keepdims=True)
    scaled = values * lax.rsqrt(square + 1e-06) * gain[None, None, :, None]
    return jax.nn.silu(scaled)


def fine_stage(ext, up, gain_one, conv_space, gain_two, conv_time, valid):
    above, below, before, after = valid
    width = ext.shape[3]
    wide = jnp.repeat(jnp.swapaxes(up, 2, 3).astype(jnp.float32), width // up.shape[2], axis=3)
    spread = jnp.concatenate([wide[:, :1], *([wide[:, 1:2]] * 4), wide[:, 2:]], axis=1)
    merged = (ext.astype(jnp.float32) + spread).astype(jnp.bfloat16)
    first = norm_silu(merged.astype(jnp.float32), gain_one)
    row_mask = jnp.stack([above, *([jnp.ones_like(above)] * 4), below])
    first = (first * row_mask[None, :, None, None]).astype(jnp.bfloat16)
    padded = jnp.pad(first, ((0, 0), (0, 0), (0, 0), (1, 1)))
    spatial = None
    for dy in range(3):
        for dx in range(3):
            term = jnp.einsum(
                "frcw,cd->frdw",
                padded[:, dy : dy + 4, :, dx : dx + width],
                conv_space[dy, dx],
                preferred_element_type=jnp.float32,
            )
            spatial = term if spatial is None else spatial + term
    second = norm_silu(spatial, gain_two)
    frame_mask = jnp.stack([before, jnp.ones_like(before), jnp.ones_like(before), after])
    second = (second * frame_mask[:, None, None, None]).astype(jnp.bfloat16)
    temporal = None
    for k in range(3):
        term = jnp.einsum(
            "frcw,cd->frdw", second[k : k + 2], conv_time[k], preferred_element_type=jnp.float32
        )
        temporal = term if temporal is None else temporal + term
    result = (merged[1:3, 1:5].astype(jnp.float32) + temporal).astype(jnp.bfloat16)
    return jnp.swapaxes(result, 1, 2)


def local(fine, coarse, w_qkv, w_out, w_up, gain_one, conv_space, gain_two, conv_time):
    frames = lax.axis_size("frame")
    rows = lax.axis_size("row")
    frame = lax.axis_index("frame")
    row = lax.axis_index("row")
    even = row % 2 == 0
    cf, cells, c_dev = coarse.shape
    fine_c = w_up.shape[1]
    tokens = cf * cells
    share = 8
    columns = fine_c // share
    groups = [list(range(k, k + share)) for k in range(0, rows, share)]
    partner = [(i, i ^ 1) for i in range(rows)]
    across = [(i, i + 1) for i in range(1, rows - 1, 2)]
    across += [(b, a) for a, b in across]

    up_slice = lax.dynamic_slice_in_dim(w_up, (row % share) * columns, columns, 1)
    message = jnp.concatenate([coarse.reshape(tokens, c_dev), up_slice.T], axis=0)
    arrived = send_all(message, "frame", frames)
    whole = jnp.swapaxes(arrived, 0, 1).reshape(tokens + columns, frames * c_dev)

    folded_slice = jnp.einsum(
        "jk,dk->jd", whole[tokens:], w_out, preferred_element_type=jnp.float32
    ).astype(jnp.bfloat16)
    folded = send_all(folded_slice, "row", share, groups).reshape(fine_c, c_dev)

    heads = w_qkv.shape[2] // HD
    qkv = jnp.einsum("tc,icd->itd", whole[:tokens], w_qkv, preferred_element_type=jnp.float32)
    qkv = qkv.astype(jnp.bfloat16).reshape(3, cf, cells, heads, HD)
    query, keys, values = qkv[0], qkv[1], qkv[2]
    scores = jnp.einsum(
        "fphd,gphd->phfg", query, keys, preferred_element_type=jnp.float32
    ) / math.sqrt(HD)
    probs = jax.nn.softmax(scores, axis=-1).astype(jnp.bfloat16)
    attn = jnp.einsum("phfg,gphd->fphd", probs, values, preferred_element_type=jnp.float32)
    attn = attn.astype(jnp.bfloat16).reshape(cf, cells, heads * HD)

    mine = jnp.stack([attn, coarse])
    other = lax.ppermute(mine, "row", partner)
    both = jnp.concatenate([jnp.where(even, mine, other), jnp.where(even, other, mine)], axis=2)

    per = frames // cf
    wanted = []
    for f in range(frames):
        wanted.append(max(f - 1, 0) // per)
        wanted.append(min(f + 1, frames - 1) // per)
    outgoing = project(both, folded, w_up, wanted).reshape(frames, 2, 2 * cells, fine_c)
    summed = lax.all_to_all(outgoing, "frame", 0, 0, tiled=True)
    up_own = jnp.sum(summed.astype(jnp.float32), axis=0).astype(jnp.bfloat16)
    up_next = lax.ppermute(up_own, "row", across)

    here = jnp.where(frame % per == 0, up_own[1], up_own[0])
    next_here = jnp.where(frame % per == 0, up_next[1], up_next[0])
    own4 = jnp.stack([up_own[0], here, here, up_own[1]])
    next4 = jnp.stack([up_next[0], next_here, next_here, up_next[1]])
    up = jnp.stack([jnp.where(even, next4, own4), own4, jnp.where(even, own4, next4)], axis=1)

    rows_first = jnp.swapaxes(fine, 1, 2)
    ahead = [(i, i + 1) for i in range(frames - 1)]
    back = [(i + 1, i) for i in range(frames - 1)]
    left = lax.ppermute(rows_first[1:], "frame", ahead)
    right = lax.ppermute(rows_first[:1], "frame", back)
    four = jnp.concatenate([left, rows_first, right], axis=0)
    top, bottom = four[:, :1], four[:, 3:]
    in_pair = lax.ppermute(jnp.where(even, bottom, top), "row", partner)
    beyond = lax.ppermute(jnp.where(even, top, bottom), "row", across)
    ext = jnp.concatenate(
        [jnp.where(even, beyond, in_pair), four, jnp.where(even, in_pair, beyond)], axis=1
    )
    valid = (row > 0, row < rows - 1, frame > 0, frame < frames - 1)
    valid = tuple(v.astype(jnp.float32) for v in valid)
    return fine_stage(ext, up, gain_one, conv_space, gain_two, conv_time, valid)


def solution(mesh):
    return jax.shard_map(
        local,
        mesh=mesh,
        in_specs=(
            P("frame", None, "row", None),
            P(None, "row", "frame"),
            P(None, None, "frame"),
            P("frame", None),
            P("frame", None),
            P(),
            P(),
            P(),
            P(),
        ),
        out_specs=P("frame", None, "row", None),
        check_vma=False,
    )
```

time: 127 us -> 119 us (0.937)
  the two profiles are of different devices: /device:TPU:55 before, /device:TPU:8 now
where the time goes in v1:
time: 119 us; the launch traced here: 118 us
  starting transfers between devices  48.2 us (41%)
  waiting for transfers between devices  31.8 us (27%)
  local copies, waits for them, and re-layouts  15.2 us (13%)
  matrix products  13.2 us (11%)
  other arithmetic  7 us (6%)
  Pallas kernels  1.82 us (2%)
    all_to_all x2, starting transfers between devices, send_all(): lax.all_to_all(copies, axis, 0, 0, tiled=True, axis_index_groups=groups)  20.6 us
    all_to_all x2, waiting for transfers between devices, send_all(): lax.all_to_all(copies, axis, 0, 0, tiled=True, axis_index_groups=groups)  20.2 us
    dot_general x9, matrix products, fine_stage(): jnp.einsum('frcw,cd->frdw', padded[:, dy:dy + 4, :, dx:dx + width], conv_...  10.6 us
    ppermute x1, starting transfers between devices, local(): beyond = lax.ppermute(jnp.where(even, top, bottom), 'row', across)  9.2 us
    unnamed x24, local copies, waits for them, and re-layouts  8.19 us
    ppermute x1, waiting for transfers between devices, local(): beyond = lax.ppermute(jnp.where(even, top, bottom), 'row', across)  7.47 us
    all_to_all x1, starting transfers between devices, local(): summed = lax.all_to_all(outgoing, 'frame', 0, 0, tiled=True)  5.82 us
    ppermute x1, starting transfers between devices, local(): left = lax.ppermute(rows_first[1:], 'frame', ahead)  4.3 us
  transfers between devices with their start and end apart: 9, of which 4 were waited for; matrix products, arithmetic and copies ran while one was open for 4% of the time, Pallas kernels for 0%

profile of v1, /device:TPU:8, one launch (start us, length us, event | category | flops | bytes accessed | tf_op | source)
XLA Modules:
  0.0 117.7 jit_solution(7400985990929974202)
XLA Ops:
  0.0 1.3 %copy.168 = bf16[2,320,4,128]{3,1,2,0:T(8,128)(2,1)S(1)} copy(bf16[2,320,4,128]{3,2,1,0:T(4,128)(2,1)} %param.9) | data formatting | bytes 1310720 | tf_op args[0]
  1.3 4.3 %collective-permute-start = (bf16[1,4,320,128]{3,2,1,0:T(8,128)(2,1)S(1)}, bf16[1,4,320,128]{3,2,1,0:T(8,128)(2,1)S(1)}, u32[]{:S(2)}, u32[]{:S(2)}) collective-permute-start(bf16[1,4,320,128]{3,2,1,0:T(8,128)(2,1)S(1)} %get-tuple-element.14), channel_id=1, source_target_pairs={{0,32},{32,64},{64,96},{96,128},{128,160},{160,192},{192,224},{224... | collective-permute-start | bytes 983048 | tf_op jit(solution)/shard_map/ppermute | solution.py:137
  5.6 1.3 %collective-permute-start.1 = (bf16[1,4,320,128]{3,2,1,0:T(8,128)(2,1)S(1)}, bf16[1,4,320,128]{3,2,1,0:T(8,128)(2,1)S(1)}, u32[]{:S(2)}, u32[]{:S(2)}) collective-permute-start(bf16[1,4,320,128]{3,2,1,0:T(8,128)(2,1)S(1)} %get-tuple-element.15), channel_id=1, source_target_pairs={{32,0},{64,32},{96,64},{128,96},{160,128},{192,160},{224,192},{256... | collective-permute-start | bytes 983048 | tf_op jit(solution)/shard_map/ppermute | solution.py:138
  6.9 0.9 dynamic-slice_bitcast_fusion
  8.1 0.8 broadcast_in_dim.6
  8.9 16.2 %all-to-all-start = ((bf16[16,72,80]{2,1,0:T(8,128)(2,1)}), bf16[16,72,80]{2,1,0:T(8,128)(2,1)S(1)}, u32[]{:S(2)}, u32[]{:S(2)}) async-start(bf16[16,72,80]{2,1,0:T(8,128)(2,1)} %broadcast_in_dim.6), calls=%async_computation | async-start | bytes 589824 | tf_op jit(solution)/shard_map/all_to_all | solution.py:14
  25.2 15.1 %all-to-all-done = bf16[16,72,80]{2,1,0:T(8,128)(2,1)S(1)} async-done(((bf16[16,72,80]{2,1,0:T(8,128)(2,1)}), bf16[16,72,80]{2,1,0:T(8,128)(2,1)S(1)}, u32[]{:S(2)}, u32[]{:S(2)}) %all-to-all-start) | async-done | bytes 184352 | tf_op jit(solution)/shard_map/all_to_all | solution.py:14
  40.5 0.2 slice.151
  40.9 0.3 fusion.28
  41.4 0.3 fusion.65
  41.8 1.9 %collective-permute-start.4 = (bf16[2,4,8,80]{3,2,1,0:T(8,128)(2,1)S(1)}, bf16[2,4,8,80]{3,2,1,0:T(8,128)(2,1)S(1)}, u32[]{:S(2)}, u32[]{:S(2)}) collective-permute-start(bf16[2,4,8,80]{3,2,1,0:T(8,128)(2,1)S(1)} %pad_maximum_fusion.7), channel_id=1, source_target_pairs={{0,1},{1,0},{2,3},{3,2},{4,5},{5,4},{6,7},{7,6},{8,9},{9,8},{10,11... | collective-permute-start | bytes 30728 | tf_op jit(solution)/shard_map/ppermute | solution.py:115
  43.9 0.7 broadcast_in_dim.7
  44.6 4.4 %all-to-all-start.1 = ((bf16[8,40,80]{2,1,0:T(8,128)(2,1)}), bf16[8,40,80]{2,1,0:T(8,128)(2,1)S(1)}, u32[]{:S(2)}, u32[]{:S(2)}) async-start(bf16[8,40,80]{2,1,0:T(8,128)(2,1)} %broadcast_in_dim.7), calls=%async_computation.1 | async-start | bytes 163840 | tf_op jit(solution)/shard_map/all_to_all | solution.py:14
  49.0 0.6 pad_maximum_fusion.5.both_ref
  49.6 5.1 %all-to-all-done.1 = bf16[8,40,80]{2,1,0:T(8,128)(2,1)S(1)} async-done(((bf16[8,40,80]{2,1,0:T(8,128)(2,1)}), bf16[8,40,80]{2,1,0:T(8,128)(2,1)S(1)}, u32[]{:S(2)}, u32[]{:S(2)}) %all-to-all-start.1) | async-done | bytes 51232 | tf_op jit(solution)/shard_map/all_to_all | solution.py:14
  54.7 0.6 copy-done.5
  55.3 1.8 %project.1 = bf16[32,16,320]{2,1,0:T(8,128)(2,1)} custom-call(bf16[2,4,16,80]{3,2,1,0:T(8,128)(2,1)} %pad_maximum_fusion.5.both_ref, bf16[320,80]{1,0:T(8,128)(2,1)} %bitcast.179, bf16[80,320]{1,0:T(8,128)(2,1)} %up_ref.1), custom_call_target="tpu_custom_call" | custom-call | tf_op jit(solution)/shard_map/project/pallas_call | solution.py:31
  57.1 5.8 %all-to-all-start.2 = ((bf16[16,2,16,320]{3,2,1,0:T(8,128)(2,1)}), bf16[16,2,16,320]{3,2,1,0:T(8,128)(2,1)S(1)}, u32[]{:S(2)}, u32[]{:S(2)}) async-start(bf16[16,2,16,320]{3,2,1,0:T(8,128)(2,1)} %bitcast.176), calls=%async_computation.2 | async-start | bytes 786432 | tf_op jit(solution)/shard_map/all_to_all | solution.py:124
  63.0 1.9 %collective-permute-start.3 = (bf16[4,1,320,128]{3,2,1,0:T(8,128)(2,1)S(1)}, bf16[4,1,320,128]{3,2,1,0:T(8,128)(2,1)S(1)}, u32[]{:S(2)}, u32[]{:S(2)}) collective-permute-start(bf16[4,1,320,128]{3,2,1,0:T(8,128)(2,1)S(1)} %broadcast_select_fusion.2), channel_id=1, source_target_pairs={{0,1},{1,0},{2,3},{3,2},{4,5},{5,4},{6,7},{7,6},{8,9},{9,8},{10,11... | collective-permute-start | bytes 983048 | tf_op jit(solution)/shard_map/ppermute | solution.py:141
  64.9 9.2 %collective-permute-start.2 = (bf16[4,1,320,128]{3,2,1,0:T(8,128)(2,1)S(1)}, bf16[4,1,320,128]{3,2,1,0:T(8,128)(2,1)S(1)}, u32[]{:S(2)}, u32[]{:S(2)}) collective-permute-start(bf16[4,1,320,128]{3,2,1,0:T(8,128)(2,1)S(1)} %get-tuple-element.7), channel_id=1, source_target_pairs={{1,2},{3,4},{5,6},{7,8},{9,10},{11,12},{13,14},{15,16},{17,18},{19... | collective-permute-start | bytes 983048 | tf_op jit(solution)/shard_map/ppermute | solution.py:142
  74.3 7.5 %collective-permute-done.2 = bf16[4,1,320,128]{3,2,1,0:T(8,128)(2,1)S(1)} collective-permute-done((bf16[4,1,320,128]{3,2,1,0:T(8,128)(2,1)S(1)}, bf16[4,1,320,128]{3,2,1,0:T(8,128)(2,1)S(1)}, u32[]{:S(2)}, u32[]{:S(2)}) %collective-permute-start.2) | collective-permute-done | bytes 327712 | tf_op jit(solution)/shard_map/ppermute | solution.py:142
  81.8 0.9 broadcast_select_fusion.1
  82.8 3.1 %collective-permute-start.5 = (bf16[2,16,320]{2,1,0:T(8,128)(2,1)S(1)}, bf16[2,16,320]{2,1,0:T(8,128)(2,1)S(1)}, u32[]{:S(2)}, u32[]{:S(2)}) collective-permute-start(bf16[2,16,320]{2,1,0:T(8,128)(2,1)S(1)} %reduce_sum.40), channel_id=1, source_target_pairs={{1,2},{3,4},{5,6},{7,8},{9,10},{11,12},{13,14},{15,16},{17,18},{19... | collective-permute-start | bytes 61448 | tf_op jit(solution)/shard_map/ppermute | solution.py:126
  85.9 4.1 %collective-permute-done.5 = bf16[2,16,320]{2,1,0:T(8,128)(2,1)S(1)} collective-permute-done((bf16[2,16,320]{2,1,0:T(8,128)(2,1)S(1)}, bf16[2,16,320]{2,1,0:T(8,128)(2,1)S(1)}, u32[]{:S(2)}, u32[]{:S(2)}) %collective-permute-start.5) | collective-permute-done | bytes 20512 | tf_op jit(solution)/shard_map/ppermute | solution.py:126
  90.1 0.2 broadcast_bitcast_fusion
  90.3 0.9 slice.196
  91.3 1.5 %fusion.96 = (f32[4,2,320,128]{2,3,1,0:T(8,128)}, f32[4,2,320,128]{2,3,1,0:T(8,128)S(1)}) fusion(f32[4,3,320,128]{2,3,1,0:T(8,128)S(1)} %broadcast_bitcast_fusion), kind=kLoop, calls=%fused_computation.129 | loop fusion | bytes 5242880 | tf_op jit(solution)/shard_map/slice | solution.py:48
  92.8 1.4 %copy.124 = f32[4,1,320,128]{3,2,1,0:T(8,128)S(1)} copy(f32[4,1,320,128]{2,3,1,0:T(8,128)} %slice.196) | data formatting | bytes 1310720
  94.2 2.9 %copy.123 = f32[4,2,320,128]{3,2,1,0:T(8,128)} copy(f32[4,2,320,128]{2,3,1,0:T(8,128)} %get-tuple-element.10) | data formatting | bytes 2621440
  97.1 1.5 %copy.125 = f32[4,2,320,128]{3,2,1,0:T(8,128)} copy(f32[4,2,320,128]{2,3,1,0:T(8,128)S(1)} %get-tuple-element.11) | data formatting | bytes 2621440
  98.7 2.7 %fusion.1 = (f32[4,6,128]{2,1,0:T(8,128)S(1)}, bf16[4,6,320,128]{3,2,1,0:T(8,128)(2,1)S(1)}) fusion(f32[4,2,320,128]{3,2,1,0:T(8,128)} %copy.125, f32[4,1,320,128]{3,2,1,0:T(8,128)S(1)} %copy.124, f32[4,2,320,128]{3,2,1,0:T(8,128)} %copy.123, bf16[4,1,320,128]{3,2,1,0:T(8,128)(2,1)} %get-tuple-element.13, bf16[1,4,320,128]{3,2,1,0:T(8,128)(2,1)} %copy-done.3, ...), kind=kLoop, calls=%fused_computation.9 | loop fusion | flops 12776448 | bytes 7221248 | tf_op jit(solution)/shard_map/reduce_sum | solution.py:39
  101.4 1.4 %fusion.9 = bf16[4,6,320,128]{3,2,1,0:T(8,128)(2,1)S(1)} fusion(bf16[4,6,320,128]{3,2,1,0:T(8,128)(2,1)S(1)} %get-tuple-element.6, f32[6]{0:T(128)S(1)} %pad_maximum_fusion.8, f32[320]{0:T(512)S(1)} %copy-done.8, f32[4,6,128]{2,1,0:T(8,128)S(1)} %add_rsqrt_fusion), kind=kLoop, calls=%fused_computation.17 | loop fusion | flops 8847360 | bytes 3945752 | tf_op jit(solution)/shard_map/convert_element_type | solution.py:52
  102.7 0.2 copy-done.1
  102.9 1.0 fusion.18
  104.0 1.0 fusion.19
  105.0 1.0 fusion.20
  106.1 1.0 fusion.21
  107.1 0.9 fusion.22
  108.0 0.9 fusion.24
  108.8 0.9 fusion.26
  109.7 1.0 fusion.17
  110.7 2.9 %multiply_reduce_fusion = (f32[4,4,128]{2,1,0:T(4,128)S(1)}, f32[4,4,128,320]{2,3,1,0:T(8,128)S(1)}) fusion(bf16[4,6,320,128]{3,2,1,0:T(8,128)(2,1)S(1)} %fusion.9, bf16[3,3,320,320]{3,2,1,0:T(8,128)(2,1)} %param.15, f32[4,4,128,320]{2,3,1,0:T(8,128)S(1)} %fusion.22, f32[4,4,128,320]{2,3,1,0:T(8,128)S(1)} %fusion.21, f32[4,4,128,320]{2,3,1,0:T(8,128)S(1)} %fusion.20, ...), kind=kOutput, calls=%fused_computation.26 | convolution fusion | flops 425981952 | bytes 25812992 | tf_op jit(solution)/shard_map/frcw,cd->frdw/dot_general | solution.py:57
  113.7 0.9 fusion.15
  114.6 0.2 copy-done.4
  114.8 0.5 fusion.34
  115.3 0.5 convolution_add_fusion.1
  115.8 0.5 fusion.31
  116.4 1.3 %copy.109 = bf16[2,320,4,128]{3,2,1,0:T(4,128)(2,1)} copy(bf16[2,320,4,128]{3,1,2,0:T(8,128)(2,1)S(1)} %fusion.31) | data formatting | bytes 1310720 | tf_op jit(solution)/shard_map/transpose | solution.py:74
  (51 shorter events, 1.5 us)
Async XLA Ops:
  0.0 40.9 %copy-start = (bf16[3,1280,80]{1,2,0:T(8,128)(2,1)S(1)}, bf16[3,1280,80]{1,2,0:T(8,128)(2,1)}, u32[]{:S(2)}) copy-start(bf16[3,1280,80]{1,2,0:T(8,128)(2,1)} %param.11) | copy-start | bytes 1843204
  0.0 7.8 %copy-start.7 = (bf16[4,8,80]{2,1,0:T(8,128)(2,1)S(1)}, bf16[4,8,80]{2,1,0:T(8,128)(2,1)}, u32[]{:S(2)}) copy-start(bf16[4,8,80]{2,1,0:T(8,128)(2,1)} %param.10) | copy-start | bytes 15364
  1.3 23.8 %collective-permute-start = (bf16[1,4,320,128]{3,2,1,0:T(8,128)(2,1)S(1)}, bf16[1,4,320,128]{3,2,1,0:T(8,128)(2,1)S(1)}, u32[]{:S(2)}, u32[]{:S(2)}) collective-permute-start(bf16[1,4,320,128]{3,2,1,0:T(8,128)(2,1)S(1)} %get-tuple-element.14), channel_id=1, source_target_pairs={{0,32},{32,64},{64,96},{96,128},{128,160},{160,192},{192,224},{224... | collective-permute-start | bytes 983048 | tf_op jit(solution)/shard_map/ppermute | solution.py:137
  5.6 19.5 %collective-permute-start.1 = (bf16[1,4,320,128]{3,2,1,0:T(8,128)(2,1)S(1)}, bf16[1,4,320,128]{3,2,1,0:T(8,128)(2,1)S(1)}, u32[]{:S(2)}, u32[]{:S(2)}) collective-permute-start(bf16[1,4,320,128]{3,2,1,0:T(8,128)(2,1)S(1)} %get-tuple-element.15), channel_id=1, source_target_pairs={{32,0},{64,32},{96,64},{128,96},{160,128},{192,160},{224,192},{256... | collective-permute-start | bytes 983048 | tf_op jit(solution)/shard_map/ppermute | solution.py:138
  8.9 31.5 %all-to-all-start = ((bf16[16,72,80]{2,1,0:T(8,128)(2,1)}), bf16[16,72,80]{2,1,0:T(8,128)(2,1)S(1)}, u32[]{:S(2)}, u32[]{:S(2)}) async-start(bf16[16,72,80]{2,1,0:T(8,128)(2,1)} %broadcast_in_dim.6), calls=%async_computation | async-start | bytes 589824 | tf_op jit(solution)/shard_map/all_to_all | solution.py:14
  25.1 18.6 %copy-start.6 = (bf16[80,1280]{1,0:T(8,128)(2,1)S(1)}, bf16[80,1280]{1,0:T(8,128)(2,1)}, u32[]{:S(2)}) copy-start(bf16[80,1280]{1,0:T(8,128)(2,1)} %param.12) | copy-start | bytes 614404
  25.1 16.1 %copy-start.2 = (bf16[1,4,320,128]{3,2,1,0:T(8,128)(2,1)}, bf16[1,4,320,128]{3,2,1,0:T(8,128)(2,1)S(1)}, u32[]{:S(2)}) copy-start(bf16[1,4,320,128]{3,2,1,0:T(8,128)(2,1)S(1)} %collective-permute-done) | copy-start | bytes 983044
  25.1 16.1 %copy-start.3 = (bf16[1,4,320,128]{3,2,1,0:T(8,128)(2,1)}, bf16[1,4,320,128]{3,2,1,0:T(8,128)(2,1)S(1)}, u32[]{:S(2)}) copy-start(bf16[1,4,320,128]{3,2,1,0:T(8,128)(2,1)S(1)} %collective-permute-done.1) | copy-start | bytes 983044
  41.8 7.2 %collective-permute-start.4 = (bf16[2,4,8,80]{3,2,1,0:T(8,128)(2,1)S(1)}, bf16[2,4,8,80]{3,2,1,0:T(8,128)(2,1)S(1)}, u32[]{:S(2)}, u32[]{:S(2)}) collective-permute-start(bf16[2,4,8,80]{3,2,1,0:T(8,128)(2,1)S(1)} %pad_maximum_fusion.7), channel_id=1, source_target_pairs={{0,1},{1,0},{2,3},{3,2},{4,5},{5,4},{6,7},{7,6},{8,9},{9,8},{10,11... | collective-permute-start | bytes 30728 | tf_op jit(solution)/shard_map/ppermute | solution.py:115
  44.6 10.1 %all-to-all-start.1 = ((bf16[8,40,80]{2,1,0:T(8,128)(2,1)}), bf16[8,40,80]{2,1,0:T(8,128)(2,1)S(1)}, u32[]{:S(2)}, u32[]{:S(2)}) async-start(bf16[8,40,80]{2,1,0:T(8,128)(2,1)} %broadcast_in_dim.7), calls=%async_computation.1 | async-start | bytes 163840 | tf_op jit(solution)/shard_map/all_to_all | solution.py:14
  54.7 0.6 copy-start.5
  57.1 25.6 %all-to-all-start.2 = ((bf16[16,2,16,320]{3,2,1,0:T(8,128)(2,1)}), bf16[16,2,16,320]{3,2,1,0:T(8,128)(2,1)S(1)}, u32[]{:S(2)}, u32[]{:S(2)}) async-start(bf16[16,2,16,320]{3,2,1,0:T(8,128)(2,1)} %bitcast.176), calls=%async_computation.2 | async-start | bytes 786432 | tf_op jit(solution)/shard_map/all_to_all | solution.py:124
  63.0 11.3 %collective-permute-start.3 = (bf16[4,1,320,128]{3,2,1,0:T(8,128)(2,1)S(1)}, bf16[4,1,320,128]{3,2,1,0:T(8,128)(2,1)S(1)}, u32[]{:S(2)}, u32[]{:S(2)}) collective-permute-start(bf16[4,1,320,128]{3,2,1,0:T(8,128)(2,1)S(1)} %broadcast_select_fusion.2), channel_id=1, source_target_pairs={{0,1},{1,0},{2,3},{3,2},{4,5},{5,4},{6,7},{7,6},{8,9},{9,8},{10,11... | collective-permute-start | bytes 983048 | tf_op jit(solution)/shard_map/ppermute | solution.py:141
  64.9 16.9 %collective-permute-start.2 = (bf16[4,1,320,128]{3,2,1,0:T(8,128)(2,1)S(1)}, bf16[4,1,320,128]{3,2,1,0:T(8,128)(2,1)S(1)}, u32[]{:S(2)}, u32[]{:S(2)}) collective-permute-start(bf16[4,1,320,128]{3,2,1,0:T(8,128)(2,1)S(1)} %get-tuple-element.7), channel_id=1, source_target_pairs={{1,2},{3,4},{5,6},{7,8},{9,10},{11,12},{13,14},{15,16},{17,18},{19... | collective-permute-start | bytes 983048 | tf_op jit(solution)/shard_map/ppermute | solution.py:142
  82.8 7.3 %collective-permute-start.5 = (bf16[2,16,320]{2,1,0:T(8,128)(2,1)S(1)}, bf16[2,16,320]{2,1,0:T(8,128)(2,1)S(1)}, u32[]{:S(2)}, u32[]{:S(2)}) collective-permute-start(bf16[2,16,320]{2,1,0:T(8,128)(2,1)S(1)} %reduce_sum.40), channel_id=1, source_target_pairs={{1,2},{3,4},{5,6},{7,8},{9,10},{11,12},{13,14},{15,16},{17,18},{19... | collective-permute-start | bytes 61448 | tf_op jit(solution)/shard_map/ppermute | solution.py:126
  98.7 2.7 %copy-start.8 = (f32[320]{0:T(512)S(1)}, f32[320]{0:T(512)}, u32[]{:S(2)}) copy-start(f32[320]{0:T(512)} %param.14) | copy-start | bytes 3844
  101.3 1.6 %copy-start.1 = (bf16[3,3,320,320]{3,2,1,0:T(8,128)(2,1)S(1)}, bf16[3,3,320,320]{3,2,1,0:T(8,128)(2,1)}, u32[]{:S(2)}) copy-start(bf16[3,3,320,320]{3,2,1,0:T(8,128)(2,1)} %param.15) | copy-start | bytes 5529604
  110.7 2.9 %copy-start.9 = (f32[320]{0:T(512)S(1)}, f32[320]{0:T(512)}, u32[]{:S(2)}) copy-start(f32[320]{0:T(512)} %param.16) | copy-start | bytes 3844
  113.6 1.1 copy-start.4

commit v2 on v1

v2 whole, which is shorter than its diff:
```python
import math

import jax
import jax.numpy as jnp
from jax import lax
from jax.experimental import pallas as pl
from jax.experimental.pallas import tpu as pltpu
from jax.sharding import PartitionSpec as P

HD = 80


def send_all(message, axis, count, groups=None):
    copies = jnp.broadcast_to(message[None], (count, *message.shape))
    return lax.all_to_all(copies, axis, 0, 0, tiled=True, axis_index_groups=groups)


def project(both, folded, w_up, wanted):
    cf, cells, width = both.shape[1:]

    def body(both_ref, folded_ref, up_ref, out_ref):
        attn = both_ref[0].reshape(cf * cells, width)
        inputs = both_ref[1].reshape(cf * cells, width)
        partial = lax.dot_general(
            attn, folded_ref[...], (((1,), (1,)), ((), ())), preferred_element_type=jnp.float32
        )
        partial += jnp.dot(inputs, up_ref[...], preferred_element_type=jnp.float32)
        partial = partial.astype(jnp.bfloat16)
        for place, source in enumerate(wanted):
            out_ref[place] = partial[source * cells : (source + 1) * cells]

    return pl.pallas_call(
        body,
        out_shape=jax.ShapeDtypeStruct((len(wanted), cells, w_up.shape[1]), jnp.bfloat16),
        in_specs=[pl.BlockSpec(memory_space=pltpu.VMEM)] * 3,
        out_specs=pl.BlockSpec(memory_space=pltpu.VMEM),
        compiler_params=pltpu.CompilerParams(vmem_limit_bytes=2 * 2**20),
        name="project",
    )(both, folded, w_up)


def fine_kernel(flags, own, left, right, above, below, up_own, up_next, gains, space, time, out, stack, second, merged):
    channels, width = own.shape[2:]
    cells = up_own.shape[1]
    even, first_slot = flags[0] == 1, flags[1] == 1
    valid_above, valid_below = flags[2].astype(jnp.float32), flags[3].astype(jnp.float32)
    valid_before, valid_after = flags[4].astype(jnp.float32), flags[5].astype(jnp.float32)
    across = width // cells
    column = lax.broadcasted_iota(jnp.int32, (cells, width), 1)
    cell = lax.broadcasted_iota(jnp.int32, (cells, width), 0) * across
    expand = ((column >= cell) & (column < cell + across)).astype(jnp.float32).astype(jnp.bfloat16)
    lane = lax.broadcasted_iota(jnp.int32, (channels, width), 1)

    def spread(cells_of):
        return lax.dot_general(cells_of, expand, (((0,), (0,)), ((), ())), preferred_element_type=jnp.float32)

    here = [spread(up_own[i]) for i in range(2)]
    beyond = [spread(up_next[i]) for i in range(2)]

    def by_frame(pair):
        middle = jnp.where(first_slot, pair[1], pair[0])
        return [pair[0], middle, middle, pair[1]]

    here, beyond = by_frame(here), by_frame(beyond)

    def norm(values, gain, scale):
        square = jnp.sum(values * values, axis=0, keepdims=True) * (1.0 / channels)
        inverse = lax.rsqrt(square + 1e-06)
        if scale is not None:
            inverse = inverse * scale
        half = values * inverse * gain
        return half + half * jnp.tanh(half)

    def keep(frame, position, pixels, added, scale):
        total = (pixels.astype(jnp.float32) + added).astype(jnp.bfloat16)
        if frame in (1, 2) and 1 <= position <= 4:
            merged[frame - 1, position - 1] = total
        normed = norm(total.astype(jnp.float32), gains[0], scale)
        before = jnp.where(lane == 0, 0.0, pltpu.roll(normed, 1, 1))
        after = jnp.where(lane == width - 1, 0.0, pltpu.roll(normed, width - 1, 1))
        lanes = pl.ds(width * (frame % 2), width)
        for place, part in enumerate((before, normed, after)):
            stack[frame // 2, position, pl.ds(place * channels, channels), lanes] = part.astype(jnp.bfloat16)

    for pair in range(2):
        for position in range(6):
            for frame in (2 * pair, 2 * pair + 1):
                if position == 0:
                    keep(frame, 0, above[frame, 0], jnp.where(even, beyond[frame], here[frame]), valid_above)
                elif position == 5:
                    keep(frame, 5, below[frame, 0], jnp.where(even, here[frame], beyond[frame]), valid_below)
                else:
                    held = (left.at[0], own.at[0], own.at[1], right.at[0])[frame]
                    keep(frame, position, held[position - 1], here[frame], None)
        for row in range(4):
            window = stack[pair, pl.ds(row, 3)].reshape(9 * channels, 2 * width)
            spatial = jnp.dot(space[...], window, preferred_element_type=jnp.float32)
            for side in range(2):
                frame = 2 * pair + side
                scale = (valid_before, None, None, valid_after)[frame]
                normed = norm(spatial[:, side * width : (side + 1) * width], gains[1], scale)
                second[row // 2, frame, :, pl.ds(width * (row % 2), width)] = normed.astype(jnp.bfloat16)

    for frame in range(2):
        for half in range(2):
            window = second[half, pl.ds(frame, 3)].reshape(3 * channels, 2 * width)
            temporal = jnp.dot(time[...], window, preferred_element_type=jnp.float32)
            for side in range(2):
                row = 2 * half + side
                total = merged[frame, row].astype(jnp.float32) + temporal[:, side * width : (side + 1) * width]
                out[frame, row] = total.astype(jnp.bfloat16)

def fine_stage(flags, own, left, right, above, below, up_own, up_next, gains, space, time):
    channels, width = own.shape[2:]
    vm = pl.BlockSpec(memory_space=pltpu.VMEM)
    return pl.pallas_call(
        fine_kernel,
        out_shape=jax.ShapeDtypeStruct(own.shape, jnp.bfloat16),
        in_specs=[pl.BlockSpec(memory_space=pltpu.SMEM)] + [vm] * 10,
        out_specs=vm,
        scratch_shapes=[
            pltpu.VMEM((2, 6, 3 * channels, 2 * width), jnp.bfloat16),
            pltpu.VMEM((2, 4, channels, 2 * width), jnp.bfloat16),
            pltpu.VMEM((2, 4, channels, width), jnp.bfloat16),
        ],
        compiler_params=pltpu.CompilerParams(vmem_limit_bytes=24 * 2**20),
        name="fine_stage",
    )(flags, own, left, right, above, below, up_own, up_next, gains, space, time)


def local(fine, coarse, w_qkv, w_out, w_up, gain_one, conv_space, gain_two, conv_time):
    frames = lax.axis_size("frame")
    rows = lax.axis_size("row")
    frame = lax.axis_index("frame")
    row = lax.axis_index("row")
    even = row % 2 == 0
    cf, cells, c_dev = coarse.shape
    fine_c = w_up.shape[1]
    tokens = cf * cells
    share = 8
    columns = fine_c // share
    groups = [list(range(k, k + share)) for k in range(0, rows, share)]
    partner = [(i, i ^ 1) for i in range(rows)]
    across = [(i, i + 1) for i in range(1, rows - 1, 2)]
    across += [(b, a) for a, b in across]

    up_slice = lax.dynamic_slice_in_dim(w_up, (row % share) * columns, columns, 1)
    message = jnp.concatenate([coarse.reshape(tokens, c_dev), up_slice.T], axis=0)
    message, fine, conv_space, conv_time, gain_one, gain_two = lax.optimization_barrier(
        (message, fine, conv_space, conv_time, gain_one, gain_two)
    )
    arrived = send_all(message, "frame", frames)

    width = fine.shape[3]
    rows_first = jnp.swapaxes(fine, 1, 2)
    space = jnp.transpose(conv_space, (3, 0, 1, 2)).reshape(fine_c, 9 * fine_c)
    time = jnp.transpose(conv_time, (2, 0, 1)).reshape(fine_c, 3 * fine_c)
    gains = 0.5 * jnp.stack([gain_one, gain_two])
    gains = jnp.broadcast_to(gains[:, :, None], (2, fine_c, width))

    whole = jnp.swapaxes(arrived, 0, 1).reshape(tokens + columns, frames * c_dev)
    folded_slice = jnp.einsum(
        "jk,dk->jd", whole[tokens:], w_out, preferred_element_type=jnp.float32
    ).astype(jnp.bfloat16)
    copies = jnp.broadcast_to(folded_slice[None], (share, columns, c_dev))
    copies, whole, rows_first, gains = lax.optimization_barrier((copies, whole, rows_first, gains))
    folded = lax.all_to_all(copies, "row", 0, 0, tiled=True, axis_index_groups=groups)
    folded = folded.reshape(fine_c, c_dev)

    heads = w_qkv.shape[2] // HD
    qkv = jnp.einsum("tc,icd->itd", whole[:tokens], w_qkv, preferred_element_type=jnp.float32)
    qkv = qkv.astype(jnp.bfloat16).reshape(3, cf, cells, heads, HD)
    query, keys, values = qkv[0], qkv[1], qkv[2]
    scores = jnp.einsum(
        "fphd,gphd->phfg", query, keys, preferred_element_type=jnp.float32
    ) / math.sqrt(HD)
    probs = jax.nn.softmax(scores, axis=-1).astype(jnp.bfloat16)
    attn = jnp.einsum("phfg,gphd->fphd", probs, values, preferred_element_type=jnp.float32)
    attn = attn.astype(jnp.bfloat16).reshape(cf, cells, heads * HD)

    mine = jnp.stack([attn, coarse])
    other = lax.ppermute(mine, "row", partner)
    both = jnp.concatenate([jnp.where(even, mine, other), jnp.where(even, other, mine)], axis=2)

    left = lax.ppermute(rows_first[1:], "frame", [(i, i + 1) for i in range(frames - 1)])
    right = lax.ppermute(rows_first[:1], "frame", [(i + 1, i) for i in range(frames - 1)])

    per = frames // cf
    wanted = []
    for f in range(frames):
        wanted.append(max(f - 1, 0) // per)
        wanted.append(min(f + 1, frames - 1) // per)
    outgoing = project(both, folded, w_up, wanted).reshape(frames, 2, 2 * cells, fine_c)
    summed = lax.all_to_all(outgoing, "frame", 0, 0, tiled=True)
    near = (left, rows_first, right)
    to_pair = jnp.concatenate([jnp.where(even, part[:, 3:], part[:, :1]) for part in near])
    to_next = jnp.concatenate([jnp.where(even, part[:, :1], part[:, 3:]) for part in near])
    to_pair, to_next, _ = lax.optimization_barrier((to_pair, to_next, outgoing))

    from_pair = lax.ppermute(to_pair, "row", partner)
    from_next = lax.ppermute(to_next, "row", across)
    above = jnp.where(even, from_next, from_pair)
    below = jnp.where(even, from_pair, from_next)

    up_own = jnp.sum(summed.astype(jnp.float32), axis=0).astype(jnp.bfloat16)
    up_next = lax.ppermute(up_own, "row", across)
    flags = jnp.stack([even, frame % per == 0, row > 0, row < rows - 1, frame > 0, frame < frames - 1])
    result = fine_stage(
        flags.astype(jnp.int32), rows_first, left, right, above, below, up_own, up_next, gains, space, time
    )
    return jnp.swapaxes(result, 1, 2)


def solution(mesh):
    return jax.shard_map(
        local,
        mesh=mesh,
        in_specs=(
            P("frame", None, "row", None),
            P(None, "row", "frame"),
            P(None, None, "frame"),
            P("frame", None),
            P("frame", None),
            P(),
            P(),
            P(),
            P(),
        ),
        out_specs=P("frame", None, "row", None),
        check_vma=False,
    )
```

time: 119 us -> 114 us (0.958)
  the two profiles are of different devices: /device:TPU:8 before, /device:TPU:56 now
where the time goes in v2:
time: 114 us; the launch traced here: 113 us
  starting transfers between devices  63.6 us (56%)
  waiting for transfers between devices  17.6 us (15%)
  local copies, waits for them, and re-layouts  16 us (14%)
  Pallas kernels  9.08 us (8%)
  other arithmetic  5 us (4%)
    ppermute x1, starting transfers between devices, local(): from_next = lax.ppermute(to_next, 'row', across)  17.9 us
    all_to_all x1, starting transfers between devices, send_all(): lax.all_to_all(copies, axis, 0, 0, tiled=True, axis_index_groups=groups)  15.7 us
    all_to_all x1, starting transfers between devices, local(): summed = lax.all_to_all(outgoing, 'frame', 0, 0, tiled=True)  9.89 us
    pallas_call x1, Pallas kernels, fine_stage(): pl.pallas_call(fine_kernel, out_shape=jax.ShapeDtypeStruct(own.shape, jnp...  8.15 us
    all_to_all x1, waiting for transfers between devices, send_all(): lax.all_to_all(copies, axis, 0, 0, tiled=True, axis_index_groups=groups)  7.32 us
    ppermute x1, waiting for transfers between devices, local(): lax.ppermute(rows_first[1:], 'frame', [(i, i + 1) for i in range(frames -...  7.05 us
    ppermute x1, starting transfers between devices, local(): lax.ppermute(rows_first[:1], 'frame', [(i + 1, i) for i in range(frames -...  6.65 us
    all_to_all x1, starting transfers between devices, local(): lax.all_to_all(copies, 'row', 0, 0, tiled=True, axis_index_groups=groups)  4.31 us
  transfers between devices with their start and end apart: 9, of which 3 were waited for; matrix products, arithmetic and copies ran while one was open for 11% of the time, Pallas kernels for 1%

profile of v2, /device:TPU:56, one launch (start us, length us, event | category | flops | bytes accessed | tf_op | source)
XLA Modules:
  0.0 112.6 jit_solution(10618035263197993574)
XLA Ops:
  0.0 0.9 copy.44
  0.9 0.9 dynamic-slice_bitcast_fusion
  1.7 0.1 pad_maximum_fusion.3
  1.8 0.1 copy.45
  1.9 0.8 broadcast_in_dim.6
  2.7 15.7 %all-to-all-start = ((bf16[16,72,80]{2,1,0:T(8,128)(2,1)}), bf16[16,72,80]{2,1,0:T(8,128)(2,1)S(1)}, u32[]{:S(2)}, u32[]{:S(2)}) async-start(bf16[16,72,80]{2,1,0:T(8,128)(2,1)} %broadcast_in_dim.6), calls=%async_computation | async-start | bytes 589824 | tf_op jit(solution)/shard_map/all_to_all | solution.py:15
  18.4 0.7 stack.43
  19.1 0.7 stack.44
  19.8 1.2 %copy.88 = bf16[2,320,4,128]{3,1,2,0:T(8,128)(2,1)S(1)} copy(bf16[2,320,4,128]{3,2,1,0:T(4,128)(2,1)} %param.9) | data formatting | bytes 1310720 | tf_op jit(solution)/shard_map/optimization_barrier | solution.py:149
  20.9 0.0 copy-start.9
  21.0 7.3 %all-to-all-done = bf16[16,72,80]{2,1,0:T(8,128)(2,1)S(1)} async-done(((bf16[16,72,80]{2,1,0:T(8,128)(2,1)}), bf16[16,72,80]{2,1,0:T(8,128)(2,1)S(1)}, u32[]{:S(2)}, u32[]{:S(2)}) %all-to-all-start) | async-done | bytes 184352 | tf_op jit(solution)/shard_map/all_to_all | solution.py:15
  28.3 0.3 reshape.78
  28.7 0.0 copy-start.6
  28.7 0.2 slice.52
  28.9 0.2 convolution_convert_fusion.1
  29.1 0.7 broadcast_in_dim.7
  29.7 0.1 broadcast_in_dim.8.gains
  29.9 0.3 fusion.1
  30.2 0.2 fusion.32
  30.4 0.3 fusion.7
  30.7 4.3 %all-to-all-start.1 = ((bf16[8,40,80]{2,1,0:T(8,128)(2,1)}), bf16[8,40,80]{2,1,0:T(8,128)(2,1)S(1)}, u32[]{:S(2)}, u32[]{:S(2)}) async-start(bf16[8,40,80]{2,1,0:T(8,128)(2,1)} %broadcast_in_dim.7), calls=%async_computation.1 | async-start | bytes 163840 | tf_op jit(solution)/shard_map/all_to_all | solution.py:167
  35.0 2.4 %collective-permute-start.2 = (bf16[2,4,8,80]{3,2,1,0:T(8,128)(2,1)S(1)}, bf16[2,4,8,80]{3,2,1,0:T(8,128)(2,1)S(1)}, u32[]{:S(2)}, u32[]{:S(2)}) collective-permute-start(bf16[2,4,8,80]{3,2,1,0:T(8,128)(2,1)S(1)} %pad_maximum_fusion.4), channel_id=1, source_target_pairs={{0,1},{1,0},{2,3},{3,2},{4,5},{5,4},{6,7},{7,6},{8,9},{9,8},{10,11... | collective-permute-start | bytes 30728 | tf_op jit(solution)/shard_map/ppermute | solution.py:182
  37.5 0.9 fusion.31
  38.3 0.7 broadcast_select_fusion.2
  39.0 6.7 %collective-permute-start.1 = (bf16[1,4,320,128]{3,2,1,0:T(8,128)(2,1)}, bf16[1,4,320,128]{3,2,1,0:T(8,128)(2,1)S(1)}, u32[]{:S(2)}, u32[]{:S(2)}) collective-permute-start(bf16[1,4,320,128]{3,2,1,0:T(8,128)(2,1)} %get-tuple-element.33), channel_id=1, source_target_pairs={{32,0},{64,32},{96,64},{128,96},{160,128},{192,160},{224,192},{256... | collective-permute-start | bytes 983048 | tf_op jit(solution)/shard_map/ppermute | solution.py:186
  45.7 1.9 %collective-permute-start = (bf16[1,4,320,128]{3,2,1,0:T(8,128)(2,1)}, bf16[1,4,320,128]{3,2,1,0:T(8,128)(2,1)S(1)}, u32[]{:S(2)}, u32[]{:S(2)}) collective-permute-start(bf16[1,4,320,128]{3,2,1,0:T(8,128)(2,1)} %get-tuple-element.34), channel_id=1, source_target_pairs={{0,32},{32,64},{64,96},{96,128},{128,160},{160,192},{192,224},{224... | collective-permute-start | bytes 983048 | tf_op jit(solution)/shard_map/ppermute | solution.py:185
  47.6 0.0 collective-permute-done.2
  47.7 0.0 all-to-all-done.1
  47.7 0.9 project.1
  48.6 9.9 %all-to-all-start.2 = ((bf16[16,2,16,320]{3,2,1,0:T(8,128)(2,1)}), bf16[16,2,16,320]{3,2,1,0:T(8,128)(2,1)}, u32[]{:S(2)}, u32[]{:S(2)}) async-start(bf16[16,2,16,320]{3,2,1,0:T(8,128)(2,1)} %bitcast.20), calls=%async_computation.2 | async-start | bytes 786432 | tf_op jit(solution)/shard_map/all_to_all | solution.py:194
  58.5 7.1 %collective-permute-done.left = bf16[1,4,320,128]{3,2,1,0:T(8,128)(2,1)S(1)} collective-permute-done((bf16[1,4,320,128]{3,2,1,0:T(8,128)(2,1)}, bf16[1,4,320,128]{3,2,1,0:T(8,128)(2,1)S(1)}, u32[]{:S(2)}, u32[]{:S(2)}) %collective-permute-start) | collective-permute-done | bytes 327712 | tf_op jit(solution)/shard_map/ppermute | solution.py:185
  65.6 2.0 %pad_maximum_fusion = (bf16[4,1,320,128]{3,2,1,0:T(8,128)(2,1)}, bf16[4,1,320,128]{3,2,1,0:T(8,128)(2,1)}) fusion(bf16[1,1,320,128]{3,2,1,0:T(8,128)(2,1)S(1)} %get-tuple-element.38, bf16[2,1,320,128]{3,2,1,0:T(8,128)(2,1)} %get-tuple-element.32, bf16[1,1,320,128]{3,2,1,0:T(8,128)(2,1)S(1)} %get-tuple-element.36, ...), kind=kLoop, calls=%fused_computation.8 | loop fusion | flops 655360 | bytes 1310720 | tf_op jit(solution)/shard_map/concatenate | solution.py:196
  67.6 17.9 %collective-permute-start.3 = (bf16[4,1,320,128]{3,2,1,0:T(8,128)(2,1)}, bf16[4,1,320,128]{3,2,1,0:T(8,128)(2,1)}, u32[]{:S(2)}, u32[]{:S(2)}) collective-permute-start(bf16[4,1,320,128]{3,2,1,0:T(8,128)(2,1)} %get-tuple-element.24), channel_id=1, source_target_pairs={{1,2},{3,4},{5,6},{7,8},{9,10},{11,12},{13,14},{15,16},{17,18},{19... | collective-permute-start | bytes 983048 | tf_op jit(solution)/shard_map/ppermute | solution.py:201
  85.5 1.9 %collective-permute-start.4 = (bf16[4,1,320,128]{3,2,1,0:T(8,128)(2,1)}, bf16[4,1,320,128]{3,2,1,0:T(8,128)(2,1)}, u32[]{:S(2)}, u32[]{:S(2)}) collective-permute-start(bf16[4,1,320,128]{3,2,1,0:T(8,128)(2,1)} %get-tuple-element.25), channel_id=1, source_target_pairs={{0,1},{1,0},{2,3},{3,2},{4,5},{5,4},{6,7},{7,6},{8,9},{9,8},{10,11... | collective-permute-start | bytes 983048 | tf_op jit(solution)/shard_map/ppermute | solution.py:200
  87.5 0.1 stack.42
  87.6 1.1 copy.55.time
  88.7 3.0 %copy.54.space = bf16[320,2880]{1,0:T(8,128)(2,1)S(1)} copy(bf16[320,2880]{0,1:T(8,128)(2,1)} %bitcast.49) | data formatting | bytes 3686400 | tf_op jit(solution)/shard_map/reshape | solution.py:156
  91.7 1.1 reduce_sum.22.up_own
  92.8 2.9 %collective-permute-start.5 = (bf16[2,16,320]{2,1,0:T(8,128)(2,1)S(1)}, bf16[2,16,320]{2,1,0:T(8,128)(2,1)S(1)}, u32[]{:S(2)}, u32[]{:S(2)}) collective-permute-start(bf16[2,16,320]{2,1,0:T(8,128)(2,1)S(1)} %reduce_sum.22.up_own), channel_id=1, source_target_pairs={{1,2},{3,4},{5,6},{7,8},{9,10},{11,12},{13,14},{15,16},{17,18},{19... | collective-permute-start | bytes 61448 | tf_op jit(solution)/shard_map/ppermute | solution.py:206
  95.7 0.0 collective-permute-done.3
  95.7 0.0 collective-permute-done.4
  95.7 1.1 broadcast_select_fusion
  96.8 3.2 %collective-permute-done.5.up_next = bf16[2,16,320]{2,1,0:T(8,128)(2,1)S(1)} collective-permute-done((bf16[2,16,320]{2,1,0:T(8,128)(2,1)S(1)}, bf16[2,16,320]{2,1,0:T(8,128)(2,1)S(1)}, u32[]{:S(2)}, u32[]{:S(2)}) %collective-permute-start.5) | collective-permute-done | bytes 20512 | tf_op jit(solution)/shard_map/ppermute | solution.py:206
  100.0 1.1 copy-done.1
  101.1 1.0 copy-done.3
  102.1 1.0 copy-done.5
  103.1 8.2 %fine_stage.1 = bf16[2,4,320,128]{3,2,1,0:T(8,128)(2,1)S(1)} custom-call(s32[6]{0:T(128)S(1)} %convert_element_type.27.flags, bf16[2,4,320,128]{3,2,1,0:T(8,128)(2,1)S(1)} %bitcast.46, bf16[1,4,320,128]{3,2,1,0:T(8,128)(2,1)S(1)} %copy-done.5, bf16[1,4,320,128]{3,2,1,0:T(8,128)(2,1)S(1)} %copy-done.3, bf16[4,1,320,128]{3,2,1,0:T(8,128)(2,1)S(1)} %get-tuple-element.30.above, ...), custom_call_target="tpu_custom_call" | custom-call | tf_op jit(solution)/shard_map/fine_stage/pallas_call | solution.py:116
  111.2 1.3 %copy.56 = bf16[2,320,4,128]{3,2,1,0:T(4,128)(2,1)} copy(bf16[2,320,4,128]{3,1,2,0:T(8,128)(2,1)S(1)} %bitcast.47) | data formatting | bytes 1310720 | tf_op jit(solution)/shard_map/transpose | solution.py:211
  (29 shorter events, 0.2 us)
Async XLA Ops:
  0.0 29.9 %copy-start = (bf16[3,1280,80]{1,2,0:T(8,128)(2,1)S(1)}, bf16[3,1280,80]{1,2,0:T(8,128)(2,1)}, u32[]{:S(2)}) copy-start(bf16[3,1280,80]{1,2,0:T(8,128)(2,1)} %param.11) | copy-start | bytes 1843204
  0.0 28.9 %copy-start.8 = (bf16[80,1280]{1,0:T(8,128)(2,1)S(1)}, bf16[80,1280]{1,0:T(8,128)(2,1)}, u32[]{:S(2)}) copy-start(bf16[80,1280]{1,0:T(8,128)(2,1)} %param.12) | copy-start | bytes 614404
  2.7 25.6 %all-to-all-start = ((bf16[16,72,80]{2,1,0:T(8,128)(2,1)}), bf16[16,72,80]{2,1,0:T(8,128)(2,1)S(1)}, u32[]{:S(2)}, u32[]{:S(2)}) async-start(bf16[16,72,80]{2,1,0:T(8,128)(2,1)} %broadcast_in_dim.6), calls=%async_computation | async-start | bytes 589824 | tf_op jit(solution)/shard_map/all_to_all | solution.py:15
  20.9 14.1 %copy-start.9 = (bf16[4,8,80]{2,1,0:T(8,128)(2,1)S(1)}, bf16[4,8,80]{2,1,0:T(8,128)(2,1)}, u32[]{:S(2)}) copy-start(bf16[4,8,80]{2,1,0:T(8,128)(2,1)} %param.10) | copy-start | bytes 15364
  28.7 19.0 %copy-start.6 = (bf16[80,320]{1,0:T(8,128)(2,1)S(1)}, bf16[80,320]{1,0:T(8,128)(2,1)}, u32[]{:S(2)}) copy-start(bf16[80,320]{1,0:T(8,128)(2,1)} %up_ref.1) | copy-start | bytes 153604
  30.7 17.0 %all-to-all-start.1 = ((bf16[8,40,80]{2,1,0:T(8,128)(2,1)}), bf16[8,40,80]{2,1,0:T(8,128)(2,1)S(1)}, u32[]{:S(2)}, u32[]{:S(2)}) async-start(bf16[8,40,80]{2,1,0:T(8,128)(2,1)} %broadcast_in_dim.7), calls=%async_computation.1 | async-start | bytes 163840 | tf_op jit(solution)/shard_map/all_to_all | solution.py:167
  35.0 12.6 %collective-permute-start.2 = (bf16[2,4,8,80]{3,2,1,0:T(8,128)(2,1)S(1)}, bf16[2,4,8,80]{3,2,1,0:T(8,128)(2,1)S(1)}, u32[]{:S(2)}, u32[]{:S(2)}) collective-permute-start(bf16[2,4,8,80]{3,2,1,0:T(8,128)(2,1)S(1)} %pad_maximum_fusion.4), channel_id=1, source_target_pairs={{0,1},{1,0},{2,3},{3,2},{4,5},{5,4},{6,7},{7,6},{8,9},{9,8},{10,11... | collective-permute-start | bytes 30728 | tf_op jit(solution)/shard_map/ppermute | solution.py:182
  38.3 49.2 %copy-start.7 = (bf16[3,320,320]{2,1,0:T(8,128)(2,1)S(1)}, bf16[3,320,320]{2,1,0:T(8,128)(2,1)}, u32[]{:S(2)}) copy-start(bf16[3,320,320]{2,1,0:T(8,128)(2,1)} %param.17) | copy-start | bytes 1843204
  39.0 19.5 %collective-permute-start.1 = (bf16[1,4,320,128]{3,2,1,0:T(8,128)(2,1)}, bf16[1,4,320,128]{3,2,1,0:T(8,128)(2,1)S(1)}, u32[]{:S(2)}, u32[]{:S(2)}) collective-permute-start(bf16[1,4,320,128]{3,2,1,0:T(8,128)(2,1)} %get-tuple-element.33), channel_id=1, source_target_pairs={{32,0},{64,32},{96,64},{128,96},{160,128},{192,160},{224,192},{256... | collective-permute-start | bytes 983048 | tf_op jit(solution)/shard_map/ppermute | solution.py:186
  45.7 19.9 %collective-permute-start = (bf16[1,4,320,128]{3,2,1,0:T(8,128)(2,1)}, bf16[1,4,320,128]{3,2,1,0:T(8,128)(2,1)S(1)}, u32[]{:S(2)}, u32[]{:S(2)}) collective-permute-start(bf16[1,4,320,128]{3,2,1,0:T(8,128)(2,1)} %get-tuple-element.34), channel_id=1, source_target_pairs={{0,32},{32,64},{64,96},{96,128},{128,160},{160,192},{192,224},{224... | collective-permute-start | bytes 983048 | tf_op jit(solution)/shard_map/ppermute | solution.py:185
  48.6 43.1 %all-to-all-start.2 = ((bf16[16,2,16,320]{3,2,1,0:T(8,128)(2,1)}), bf16[16,2,16,320]{3,2,1,0:T(8,128)(2,1)}, u32[]{:S(2)}, u32[]{:S(2)}) async-start(bf16[16,2,16,320]{3,2,1,0:T(8,128)(2,1)} %bitcast.20), calls=%async_computation.2 | async-start | bytes 786432 | tf_op jit(solution)/shard_map/all_to_all | solution.py:194
  58.5 30.2 %copy-start.2 = (bf16[1,4,320,128]{3,2,1,0:T(8,128)(2,1)}, bf16[1,4,320,128]{3,2,1,0:T(8,128)(2,1)S(1)}, u32[]{:S(2)}) copy-start(bf16[1,4,320,128]{3,2,1,0:T(8,128)(2,1)S(1)} %collective-permute-done.1.right) | copy-start | bytes 983044
  65.6 23.1 %copy-start.4 = (bf16[1,4,320,128]{3,2,1,0:T(8,128)(2,1)}, bf16[1,4,320,128]{3,2,1,0:T(8,128)(2,1)S(1)}, u32[]{:S(2)}) copy-start(bf16[1,4,320,128]{3,2,1,0:T(8,128)(2,1)S(1)} %collective-permute-done.left) | copy-start | bytes 983044
  67.6 28.1 %collective-permute-start.3 = (bf16[4,1,320,128]{3,2,1,0:T(8,128)(2,1)}, bf16[4,1,320,128]{3,2,1,0:T(8,128)(2,1)}, u32[]{:S(2)}, u32[]{:S(2)}) collective-permute-start(bf16[4,1,320,128]{3,2,1,0:T(8,128)(2,1)} %get-tuple-element.24), channel_id=1, source_target_pairs={{1,2},{3,4},{5,6},{7,8},{9,10},{11,12},{13,14},{15,16},{17,18},{19... | collective-permute-start | bytes 983048 | tf_op jit(solution)/shard_map/ppermute | solution.py:201
  85.5 10.1 %collective-permute-start.4 = (bf16[4,1,320,128]{3,2,1,0:T(8,128)(2,1)}, bf16[4,1,320,128]{3,2,1,0:T(8,128)(2,1)}, u32[]{:S(2)}, u32[]{:S(2)}) collective-permute-start(bf16[4,1,320,128]{3,2,1,0:T(8,128)(2,1)} %get-tuple-element.25), channel_id=1, source_target_pairs={{0,1},{1,0},{2,3},{3,2},{4,5},{5,4},{6,7},{7,6},{8,9},{9,8},{10,11... | collective-permute-start | bytes 983048 | tf_op jit(solution)/shard_map/ppermute | solution.py:200
  92.8 7.3 %collective-permute-start.5 = (bf16[2,16,320]{2,1,0:T(8,128)(2,1)S(1)}, bf16[2,16,320]{2,1,0:T(8,128)(2,1)S(1)}, u32[]{:S(2)}, u32[]{:S(2)}) collective-permute-start(bf16[2,16,320]{2,1,0:T(8,128)(2,1)S(1)} %reduce_sum.22.up_own), channel_id=1, source_target_pairs={{1,2},{3,4},{5,6},{7,8},{9,10},{11,12},{13,14},{15,16},{17,18},{19... | collective-permute-start | bytes 61448 | tf_op jit(solution)/shard_map/ppermute | solution.py:206
  100.0 1.1 copy-start.1
  101.1 1.0 copy-start.3
  102.1 1.0 copy-start.5

commit v3 on v2

v3 whole, which is shorter than its diff:
```python
import math

import jax
import jax.numpy as jnp
from jax import lax
from jax.experimental import pallas as pl
from jax.experimental.pallas import tpu as pltpu
from jax.sharding import PartitionSpec as P

HD = 80
VMEM = pl.BlockSpec(memory_space=pltpu.VMEM)
ANY = pl.BlockSpec(memory_space=pl.ANY)
HBM = pl.BlockSpec(memory_space=pltpu.HBM)
FREE = pl.CostEstimate(flops=0, bytes_accessed=0, transcendentals=0)


def limit(mib):
    return pltpu.CompilerParams(vmem_limit_bytes=mib * 2**20)


def pack(coarse, w_up, share, count):
    cf, cells, depth = coarse.shape
    columns = w_up.shape[1] // share

    def body(coarse_in, up_in, out_ref, coarse_ref, up_ref, sems):
        moves = [
            pltpu.make_async_copy(coarse_in, coarse_ref, sems.at[0]),
            pltpu.make_async_copy(up_in, up_ref, sems.at[1]),
        ]
        for move in moves:
            move.start()
        for move in moves:
            move.wait()
        first = lax.rem(lax.axis_index("row"), share) * columns
        shape = (columns, w_up.shape[1])
        wanted = lax.broadcasted_iota(jnp.int32, shape, 0) + first
        pick = (lax.broadcasted_iota(jnp.int32, shape, 1) == wanted).astype(jnp.float32)
        rows = lax.dot_general(
            pick.astype(jnp.bfloat16),
            up_ref[...],
            (((1,), (1,)), ((), ())),
            preferred_element_type=jnp.float32,
        ).astype(jnp.bfloat16)
        for place in range(count):
            for frame in range(cf):
                out_ref[place, pl.ds(frame * cells, cells)] = coarse_ref[frame]
            out_ref[place, pl.ds(cf * cells, columns)] = rows

    return pl.pallas_call(
        body,
        out_shape=jax.ShapeDtypeStruct((count, cf * cells + columns, depth), jnp.bfloat16),
        in_specs=[HBM] * 2,
        out_specs=VMEM,
        scratch_shapes=[
            pltpu.VMEM(coarse.shape, coarse.dtype),
            pltpu.VMEM(w_up.shape, w_up.dtype),
            pltpu.SemaphoreType.DMA((2,)),
        ],
        compiler_params=limit(56),
        cost_estimate=FREE,
        name="pack",
    )(coarse, w_up)


def fold(arrived, w_out, tokens, count):
    blocks, rows, depth = arrived.shape
    heads = w_out.shape[0]

    def body(arrived_ref, out_w_ref, out_ref, cells_ref, whole_ref):
        for block in range(blocks):
            whole_ref[:, pl.ds(block * depth, depth)] = arrived_ref[block]
        cells_ref[...] = whole_ref[pl.ds(0, tokens)]
        total = lax.dot_general(
            whole_ref[pl.ds(tokens, rows - tokens)],
            out_w_ref[...],
            (((1,), (1,)), ((), ())),
            preferred_element_type=jnp.float32,
        ).astype(jnp.bfloat16)
        for place in range(count):
            out_ref[place] = total

    return pl.pallas_call(
        body,
        out_shape=(
            jax.ShapeDtypeStruct((count, rows - tokens, heads), jnp.bfloat16),
            jax.ShapeDtypeStruct((tokens, blocks * depth), jnp.bfloat16),
        ),
        in_specs=[VMEM] * 2,
        out_specs=(VMEM, VMEM),
        scratch_shapes=[pltpu.VMEM((rows, blocks * depth), jnp.bfloat16)],
        compiler_params=limit(2),
        cost_estimate=FREE,
        name="fold",
    )(arrived, w_out)


def attend(whole, w_qkv_t, coarse):
    cf, cells, depth = coarse.shape

    def body(whole_ref, w_ref, coarse_ref, out_ref):
        projected = []
        for part in range(3):
            value = lax.dot_general(
                whole_ref[...],
                w_ref[part],
                (((1,), (1,)), ((), ())),
                preferred_element_type=jnp.float32,
            )
            value = value.astype(jnp.bfloat16).astype(jnp.float32)
            projected.append([value[cells * f : cells * (f + 1)] for f in range(cf)])
        query, keys, values = projected
        for f in range(cf):
            scores = [
                jnp.sum(query[f] * keys[g], axis=1, keepdims=True) * (1.0 / math.sqrt(HD))
                for g in range(cf)
            ]
            most = scores[0]
            for score in scores[1:]:
                most = jnp.maximum(most, score)
            weights = [jnp.exp(score - most) for score in scores]
            total = sum(weights[1:], weights[0])
            mixed = None
            for g in range(cf):
                share = (weights[g] / total).astype(jnp.bfloat16).astype(jnp.float32)
                term = share * values[g]
                mixed = term if mixed is None else mixed + term
            out_ref[0, f] = mixed.astype(jnp.bfloat16)
            out_ref[1, f] = coarse_ref[f]

    return pl.pallas_call(
        body,
        out_shape=jax.ShapeDtypeStruct((2, *coarse.shape), jnp.bfloat16),
        in_specs=[VMEM] * 3,
        out_specs=VMEM,
        compiler_params=limit(2),
        cost_estimate=FREE,
        name="attend",
    )(whole, w_qkv_t, coarse)


def project(mine, other, folded, w_up, earlier, wanted):
    cf, cells, width = mine.shape[1:]

    def body(mine_ref, other_ref, folded_ref, up_ref, _, out_ref):
        even = lax.rem(lax.axis_index("row"), 2) == 0

        def through(ref):
            attn = ref[0].reshape(cf * cells, width)
            inputs = ref[1].reshape(cf * cells, width)
            partial = lax.dot_general(
                attn, folded_ref[...], (((1,), (1,)), ((), ())), preferred_element_type=jnp.float32
            )
            return partial + jnp.dot(inputs, up_ref[...], preferred_element_type=jnp.float32)

        own, far = through(mine_ref), through(other_ref)
        first, second = jnp.where(even, own, far), jnp.where(even, far, own)
        for f in range(cf):
            part = slice(cells * f, cells * (f + 1))
            block = jnp.concatenate([first[part], second[part]], axis=0).astype(jnp.bfloat16)
            for place, source in enumerate(wanted):
                if source == f:
                    out_ref[place] = block

    return pl.pallas_call(
        body,
        out_shape=jax.ShapeDtypeStruct((len(wanted), 2 * cells, w_up.shape[1]), jnp.bfloat16),
        in_specs=[VMEM] * 4 + [HBM],
        out_specs=VMEM,
        compiler_params=limit(2),
        cost_estimate=FREE,
        name="project",
    )(mine, other, folded, w_up, earlier)


def edge_rows(left, own, right):
    rows, channels, width = own.shape[1:]

    def body(left_ref, own_ref, right_ref, pair_ref, next_ref, sems):
        odd = lax.rem(lax.axis_index("row"), 2)
        frames = (left_ref.at[0], own_ref.at[0], own_ref.at[1], right_ref.at[0])
        moves = []
        for place, frame in enumerate(frames):
            for side, (out, row) in enumerate(((pair_ref, 1 - odd), (next_ref, odd))):
                moves.append(
                    pltpu.make_async_copy(
                        frame.at[row * (rows - 1)], out.at[place], sems.at[2 * place + side]
                    )
                )
        for move in moves:
            move.start()
        for move in moves:
            move.wait()

    shape = jax.ShapeDtypeStruct((4, channels, width), jnp.bfloat16)
    return pl.pallas_call(
        body,
        out_shape=(shape, shape),
        in_specs=[ANY] * 3,
        out_specs=(ANY, ANY),
        scratch_shapes=[pltpu.SemaphoreType.DMA((8,))],
        compiler_params=limit(1),
        cost_estimate=FREE,
        name="edge_rows",
    )(left, own, right)


def total(summed, earlier):
    def body(summed_ref, *refs):
        result = summed_ref[0].astype(jnp.float32)
        for source in range(1, summed.shape[0]):
            result += summed_ref[source].astype(jnp.float32)
        refs[-1][...] = result.astype(jnp.bfloat16)

    return pl.pallas_call(
        body,
        out_shape=jax.ShapeDtypeStruct(summed.shape[1:], jnp.bfloat16),
        in_specs=[VMEM] + [ANY] * len(earlier),
        out_specs=VMEM,
        compiler_params=limit(2),
        cost_estimate=FREE,
        name="total",
    )(summed, *earlier)


def fine_kernel(
    own, left_in, right_in, pair_in, next_in, up_own, up_next, one_in, two_in, space_in, time_in,
    out, left, right, pair, beyond, space, time, gains, stack, second, merged, sems,
):
    channels, width = own.shape[2:]
    cells = up_own.shape[1]
    row, frame_index = lax.axis_index("row"), lax.axis_index("frame")
    last_row, last_frame = lax.axis_size("row") - 1, lax.axis_size("frame") - 1
    even = lax.rem(row, 2) == 0
    first_slot = lax.rem(frame_index, 4) == 0
    valid_above = (row > 0).astype(jnp.float32)
    valid_below = (row < last_row).astype(jnp.float32)
    valid_before = (frame_index > 0).astype(jnp.float32)
    valid_after = (frame_index < last_frame).astype(jnp.float32)

    moves = []
    halo = ((left_in, left), (right_in, right), (pair_in, pair), (next_in, beyond))
    kernels = ((space_in, space), (time_in, time))
    for place, (source, target) in enumerate((*halo, *kernels)):
        moves.append(pltpu.make_async_copy(source, target, sems.at[place]))
    for move in moves:
        move.start()

    for place, gain in enumerate((one_in, two_in)):
        gains[place] = jnp.broadcast_to(0.5 * gain[...].reshape(1, channels), (width, channels)).T
    gain_one, gain_two = gains.at[0], gains.at[1]

    across = width // cells
    column = lax.broadcasted_iota(jnp.int32, (cells, width), 1)
    cell = lax.broadcasted_iota(jnp.int32, (cells, width), 0) * across
    expand = ((column >= cell) & (column < cell + across)).astype(jnp.float32).astype(jnp.bfloat16)
    lane = lax.broadcasted_iota(jnp.int32, (channels, width), 1)

    def spread(source):
        by_slot = [
            lax.dot_general(
                source[slot], expand, (((0,), (0,)), ((), ())), preferred_element_type=jnp.float32
            )
            for slot in range(2)
        ]
        middle = jnp.where(first_slot, by_slot[1], by_slot[0])
        return [by_slot[0], middle, middle, by_slot[1]]

    def norm(values, gain, scale):
        square = jnp.sum(values * values, axis=0, keepdims=True) * (1.0 / channels)
        inverse = lax.rsqrt(square + 1e-06)
        if scale is not None:
            inverse = inverse * scale
        half = values * inverse * gain[...]
        return half + half * jnp.tanh(half)

    def keep(frame, position, pixels, added, scale):
        total = (pixels.astype(jnp.float32) + added).astype(jnp.bfloat16)
        if frame in (1, 2) and 1 <= position <= 4:
            merged[frame - 1, position - 1] = total
        normed = norm(total.astype(jnp.float32), gain_one, scale)
        before = jnp.where(lane == 0, 0.0, pltpu.roll(normed, 1, 1))
        after = jnp.where(lane == width - 1, 0.0, pltpu.roll(normed, width - 1, 1))
        lanes = pl.ds(width * (frame % 2), width)
        for place, part in enumerate((before, normed, after)):
            stack[frame // 2, position, pl.ds(place * channels, channels), lanes] = part.astype(
                jnp.bfloat16
            )

    here, further = spread(up_own), spread(up_next)
    for position in range(1, 5):
        keep(1, position, own[0, position - 1], here[1], None)
    for move in moves[:4]:
        move.wait()

    def edges(frame):
        near, far = pair[frame], beyond[frame]
        keep(
            frame, 0, jnp.where(even, far, near), jnp.where(even, further[frame], here[frame]), valid_above
        )
        keep(
            frame, 5, jnp.where(even, near, far), jnp.where(even, here[frame], further[frame]), valid_below
        )

    for position in range(1, 5):
        keep(0, position, left[0, position - 1], here[0], None)
    edges(0)
    edges(1)
    moves[4].wait()
    for half in range(2):
        if half == 1:
            for position in range(1, 5):
                keep(2, position, own[1, position - 1], here[2], None)
                keep(3, position, right[0, position - 1], here[3], None)
            edges(2)
            edges(3)
        for row_out in range(4):
            window = stack[half, pl.ds(row_out, 3)].reshape(9 * channels, 2 * width)
            spatial = jnp.dot(space[...], window, preferred_element_type=jnp.float32)
            for side in range(2):
                frame = 2 * half + side
                scale = (valid_before, None, None, valid_after)[frame]
                normed = norm(spatial[:, side * width : (side + 1) * width], gain_two, scale)
                second[row_out // 2, frame, :, pl.ds(width * (row_out % 2), width)] = normed.astype(
                    jnp.bfloat16
                )

    moves[5].wait()
    for frame in range(2):
        for half in range(2):
            window = second[half, pl.ds(frame, 3)].reshape(3 * channels, 2 * width)
            temporal = jnp.dot(time[...], window, preferred_element_type=jnp.float32)
            for side in range(2):
                row_out = 2 * half + side
                total = merged[frame, row_out].astype(jnp.float32)
                total += temporal[:, side * width : (side + 1) * width]
                out[frame, row_out] = total.astype(jnp.bfloat16)


def fine_stage(own, left, right, pair, beyond, up_own, up_next, gain_one, gain_two, space, time):
    channels, width = own.shape[2:]
    bf16 = jnp.bfloat16
    copied = (left, right, pair, beyond, space, time)
    return pl.pallas_call(
        fine_kernel,
        out_shape=jax.ShapeDtypeStruct(own.shape, bf16),
        in_specs=[VMEM] + [HBM] * 4 + [VMEM] * 4 + [HBM] * 2,
        out_specs=VMEM,
        scratch_shapes=[pltpu.VMEM(array.shape, array.dtype) for array in copied]
        + [
            pltpu.VMEM((2, channels, width), jnp.float32),
            pltpu.VMEM((2, 6, 3 * channels, 2 * width), bf16),
            pltpu.VMEM((2, 4, channels, 2 * width), bf16),
            pltpu.VMEM((2, 4, channels, width), bf16),
            pltpu.SemaphoreType.DMA((len(copied),)),
        ],
        compiler_params=limit(28),
        name="fine_stage",
    )(own, left, right, pair, beyond, up_own, up_next, gain_one, gain_two, space, time)


def local(fine, coarse, w_qkv, w_out, w_up, gain_one, conv_space, gain_two, conv_time):
    frames = lax.axis_size("frame")
    rows = lax.axis_size("row")
    cf, cells, c_dev = coarse.shape
    fine_c, width = fine.shape[1], fine.shape[3]
    tokens = cf * cells
    share = 8
    groups = [list(range(k, k + share)) for k in range(0, rows, share)]
    partner = [(i, i ^ 1) for i in range(rows)]
    across = [(i, i + 1) for i in range(1, rows - 1, 2)]
    across += [(b, a) for a, b in across]

    message = pack(coarse, w_up, share, frames)
    arrived = lax.all_to_all(message, "frame", 0, 0, tiled=True)

    rows_first = jnp.swapaxes(fine, 1, 2)
    left = lax.ppermute(rows_first[1:], "frame", [(i, i + 1) for i in range(frames - 1)])
    right = lax.ppermute(rows_first[:1], "frame", [(i + 1, i) for i in range(frames - 1)])
    space = jnp.transpose(conv_space, (3, 0, 1, 2)).reshape(fine_c, 9 * fine_c)
    time = jnp.transpose(conv_time, (2, 0, 1)).reshape(fine_c, 3 * fine_c)

    copies, whole = fold(arrived, w_out, tokens, share)
    folded = lax.all_to_all(copies, "row", 0, 0, tiled=True, axis_index_groups=groups)
    folded = folded.reshape(fine_c, w_out.shape[0])
    mine = attend(whole, jnp.swapaxes(w_qkv, 1, 2), coarse)
    other = lax.ppermute(mine, "row", partner)

    to_pair, to_next = edge_rows(left, rows_first, right)

    per = frames // cf
    wanted = []
    for f in range(frames):
        wanted.append(max(f - 1, 0) // per)
        wanted.append(min(f + 1, frames - 1) // per)
    outgoing = project(mine, other, folded, w_up, to_pair, wanted).reshape(frames, 2, 2 * cells, fine_c)
    summed = lax.all_to_all(outgoing, "frame", 0, 0, tiled=True)

    from_pair = lax.ppermute(to_pair, "row", partner)
    from_next = lax.ppermute(to_next, "row", across)

    up_own = total(summed, (space, time))
    up_next = lax.ppermute(up_own, "row", across)
    result = fine_stage(
        rows_first, left, right, from_pair, from_next, up_own, up_next, gain_one, gain_two, space, time
    )
    return jnp.swapaxes(result, 1, 2)


def solution(mesh):
    return jax.shard_map(
        local,
        mesh=mesh,
        in_specs=(
            P("frame", None, "row", None),
            P(None, "row", "frame"),
            P(None, None, "frame"),
            P("frame", None),
            P("frame", None),
            P(),
            P(),
            P(),
            P(),
        ),
        out_specs=P("frame", None, "row", None),
        check_vma=False,
    )
```

time: 114 us -> 89.7 us (0.79)
  the two profiles are of different devices: /device:TPU:56 before, /device:TPU:8 now
where the time goes in v3:
time: 89.7 us; the launch traced here: 89 us
  starting transfers between devices  46.6 us (52%)
  waiting for transfers between devices  20.8 us (23%)
  Pallas kernels  14.7 us (16%)
  local copies, waits for them, and re-layouts  6.7 us (7%)
    all_to_all x1, starting transfers between devices, local(): arrived = lax.all_to_all(message, 'frame', 0, 0, tiled=True)  14.8 us
    all_to_all x1, starting transfers between devices, local(): summed = lax.all_to_all(outgoing, 'frame', 0, 0, tiled=True)  11.8 us
    pallas_call x1, Pallas kernels, fine_stage(): pl.pallas_call(fine_kernel, out_shape=jax.ShapeDtypeStruct(own.shape, bf1...  8.51 us
    all_to_all x1, waiting for transfers between devices, local(): arrived = lax.all_to_all(message, 'frame', 0, 0, tiled=True)  8.02 us
    all_to_all x1, waiting for transfers between devices, local(): summed = lax.all_to_all(outgoing, 'frame', 0, 0, tiled=True)  5.61 us
    ppermute x1, waiting for transfers between devices, local(): up_next = lax.ppermute(up_own, 'row', across)  5.31 us
    ppermute x1, starting transfers between devices, local(): lax.ppermute(rows_first[1:], 'frame', [(i, i + 1) for i in range(frames -...  4.57 us
    all_to_all x1, starting transfers between devices, local(): lax.all_to_all(copies, 'row', 0, 0, tiled=True, axis_index_groups=groups)  4.3 us
  transfers between devices with their start and end apart: 9, of which 4 were waited for; matrix products, arithmetic and copies ran while one was open for 6% of the time, Pallas kernels for 4%

profile of v3, /device:TPU:8, one launch (start us, length us, event | category | flops | bytes accessed | tf_op | source)
XLA Modules:
  0.0 89.0 jit_solution(17946751615990388006)
XLA Ops:
  0.0 0.0 copy-start.5
  0.0 0.0 copy-start.4
  0.0 0.0 copy-start.2
  0.0 1.8 %pack.1 = bf16[16,72,80]{2,1,0:T(8,128)(2,1)} custom-call(bf16[4,8,80]{2,1,0:T(8,128)(2,1)} %coarse_ref.1, bf16[80,320]{1,0:T(8,128)(2,1)} %up_ref.1), custom_call_target="tpu_custom_call" | custom-call | tf_op jit(solution)/shard_map/pack/pallas_call | solution.py:49
  1.8 14.8 %all-to-all-start = ((bf16[16,72,80]{2,1,0:T(8,128)(2,1)}), bf16[16,72,80]{2,1,0:T(8,128)(2,1)S(1)}, u32[]{:S(2)}, u32[]{:S(2)}) async-start(bf16[16,72,80]{2,1,0:T(8,128)(2,1)} %pack.1), calls=%async_computation | async-start | bytes 589824 | tf_op jit(solution)/shard_map/all_to_all | solution.py:374
  16.6 1.2 %copy.21 = bf16[2,320,4,128]{3,1,2,0:T(8,128)(2,1)S(1)} copy(bf16[2,320,4,128]{3,2,1,0:T(4,128)(2,1)} %param.9) | data formatting | bytes 1310720 | tf_op args[0]
  17.8 0.0 copy-start.3
  17.8 0.9 fusion
  18.7 0.0 copy-start.8
  18.7 1.4 %collective-permute-start.1 = (bf16[1,4,320,128]{3,2,1,0:T(8,128)(2,1)}, bf16[1,4,320,128]{3,2,1,0:T(8,128)(2,1)S(1)}, u32[]{:S(2)}, u32[]{:S(2)}) collective-permute-start(bf16[1,4,320,128]{3,2,1,0:T(8,128)(2,1)} %get-tuple-element.13), channel_id=1, source_target_pairs={{32,0},{64,32},{96,64},{128,96},{160,128},{192,160},{224,192},{256... | collective-permute-start | bytes 983048 | tf_op jit(solution)/shard_map/ppermute | solution.py:378
  20.1 4.6 %collective-permute-start = (bf16[1,4,320,128]{3,2,1,0:T(8,128)(2,1)}, bf16[1,4,320,128]{3,2,1,0:T(8,128)(2,1)S(1)}, u32[]{:S(2)}, u32[]{:S(2)}) collective-permute-start(bf16[1,4,320,128]{3,2,1,0:T(8,128)(2,1)} %get-tuple-element.14), channel_id=1, source_target_pairs={{0,32},{32,64},{64,96},{96,128},{128,160},{160,192},{192,224},{224... | collective-permute-start | bytes 983048 | tf_op jit(solution)/shard_map/ppermute | solution.py:377
  24.7 8.0 %all-to-all-done.arrived_ref = bf16[16,72,80]{2,1,0:T(8,128)(2,1)S(1)} async-done(((bf16[16,72,80]{2,1,0:T(8,128)(2,1)}), bf16[16,72,80]{2,1,0:T(8,128)(2,1)S(1)}, u32[]{:S(2)}, u32[]{:S(2)}) %all-to-all-start) | async-done | bytes 184352 | tf_op jit(solution)/shard_map/all_to_all | solution.py:374
  32.7 0.0 copy-done.4
  32.7 0.9 %fold.1 = (bf16[8,40,80]{2,1,0:T(8,128)(2,1)}, bf16[32,1280]{1,0:T(8,128)(2,1)S(1)}) custom-call(bf16[16,72,80]{2,1,0:T(8,128)(2,1)S(1)} %all-to-all-done.arrived_ref, bf16[80,1280]{1,0:T(8,128)(2,1)S(1)} %copy-done.4), custom_call_target="tpu_custom_call" | custom-call | tf_op jit(solution)/shard_map/fold/pallas_call | solution.py:82
  33.6 4.3 %all-to-all-start.1 = ((bf16[8,40,80]{2,1,0:T(8,128)(2,1)}), bf16[8,40,80]{2,1,0:T(8,128)(2,1)S(1)}, u32[]{:S(2)}, u32[]{:S(2)}) async-start(bf16[8,40,80]{2,1,0:T(8,128)(2,1)} %get-tuple-element.12), calls=%async_computation.1 | async-start | bytes 163840 | tf_op jit(solution)/shard_map/all_to_all | solution.py:383
  37.9 0.0 copy-done.5
  37.9 0.0 copy-done.2
  38.0 0.4 attend.1.mine_ref
  38.4 2.4 %collective-permute-start.4 = (bf16[2,4,8,80]{3,2,1,0:T(8,128)(2,1)S(1)}, bf16[2,4,8,80]{3,2,1,0:T(8,128)(2,1)S(1)}, u32[]{:S(2)}, u32[]{:S(2)}) collective-permute-start(bf16[2,4,8,80]{3,2,1,0:T(8,128)(2,1)S(1)} %attend.1.mine_ref), channel_id=1, source_target_pairs={{0,1},{1,0},{2,3},{3,2},{4,5},{5,4},{6,7},{7,6},{8,9},{9,8},{10,11... | collective-permute-start | bytes 30728 | tf_op jit(solution)/shard_map/ppermute | solution.py:386
  40.8 0.0 collective-permute-done.1.right_ref.right_in
  40.8 0.0 collective-permute-done.left_ref.left_in
  40.8 0.0 copy-start
  40.8 1.0 %edge_rows.1 = (bf16[4,320,128]{2,1,0:T(8,128)(2,1)}, bf16[4,320,128]{2,1,0:T(8,128)(2,1)}) custom-call(bf16[1,4,320,128]{3,2,1,0:T(8,128)(2,1)S(1)} %collective-permute-done.left_ref.left_in, bf16[2,4,320,128]{3,2,1,0:T(8,128)(2,1)S(1)} %bitcast.14, bf16[1,4,320,128]{3,2,1,0:T(8,128)(2,1)S(1)} %collective-permute-done.1.right_ref.right_in), custom_call_target="tpu_custom_call" | custom-call | tf_op jit(solution)/shard_map/edge_rows/pallas_call | solution.py:195
  41.8 0.0 collective-permute-done.4.other_ref
  41.8 1.8 %all-to-all-done.1 = bf16[8,40,80]{2,1,0:T(8,128)(2,1)S(1)} async-done(((bf16[8,40,80]{2,1,0:T(8,128)(2,1)}), bf16[8,40,80]{2,1,0:T(8,128)(2,1)S(1)}, u32[]{:S(2)}, u32[]{:S(2)}) %all-to-all-start.1) | async-done | bytes 51232 | tf_op jit(solution)/shard_map/all_to_all | solution.py:383
  43.7 0.0 copy-done.3
  43.7 1.0 %project.1 = bf16[32,16,320]{2,1,0:T(8,128)(2,1)} custom-call(bf16[2,4,8,80]{3,2,1,0:T(8,128)(2,1)S(1)} %attend.1.mine_ref, bf16[2,4,8,80]{3,2,1,0:T(8,128)(2,1)S(1)} %collective-permute-done.4.other_ref, bf16[320,80]{1,0:T(8,128)(2,1)S(1)} %bitcast.18, bf16[80,320]{1,0:T(8,128)(2,1)S(1)} %copy-done.3, bf16[4,320,128]{2,1,0:T(8,128)(2,1)} %get-tuple-element.9._), custom_call_target="tpu_custom_call" | custom-call | tf_op jit(solution)/shard_map/project/pallas_call | solution.py:164
  44.6 11.8 %all-to-all-start.2 = ((bf16[16,2,16,320]{3,2,1,0:T(8,128)(2,1)}), bf16[16,2,16,320]{3,2,1,0:T(8,128)(2,1)}, u32[]{:S(2)}, u32[]{:S(2)}) async-start(bf16[16,2,16,320]{3,2,1,0:T(8,128)(2,1)} %bitcast.3), calls=%async_computation.2 | async-start | bytes 786432 | tf_op jit(solution)/shard_map/all_to_all | solution.py:396
  56.4 1.9 %collective-permute-start.3 = (bf16[4,320,128]{2,1,0:T(8,128)(2,1)}, bf16[4,320,128]{2,1,0:T(8,128)(2,1)}, u32[]{:S(2)}, u32[]{:S(2)}) collective-permute-start(bf16[4,320,128]{2,1,0:T(8,128)(2,1)} %get-tuple-element.10), channel_id=1, source_target_pairs={{1,2},{3,4},{5,6},{7,8},{9,10},{11,12},{13,14},{15,16},{17,18},{19... | collective-permute-start | bytes 983048 | tf_op jit(solution)/shard_map/ppermute | solution.py:399
  58.3 3.5 %collective-permute-start.2 = (bf16[4,320,128]{2,1,0:T(8,128)(2,1)}, bf16[4,320,128]{2,1,0:T(8,128)(2,1)}, u32[]{:S(2)}, u32[]{:S(2)}) collective-permute-start(bf16[4,320,128]{2,1,0:T(8,128)(2,1)} %get-tuple-element.9._), channel_id=1, source_target_pairs={{0,1},{1,0},{2,3},{3,2},{4,5},{5,4},{6,7},{7,6},{8,9},{9,8},{10,11... | collective-permute-start | bytes 983048 | tf_op jit(solution)/shard_map/ppermute | solution.py:398
  61.8 0.0 copy-done
  61.8 0.0 copy-done.8
  61.9 0.3 copy.16.refs_1_.time_in
  62.1 3.0 %copy.15.refs_0_.space_in = bf16[320,2880]{1,0:T(8,128)(2,1)S(1)} copy(bf16[320,2880]{0,1:T(8,128)(2,1)} %bitcast.19) | data formatting | bytes 3686400 | tf_op jit(solution)/shard_map/reshape | solution.py:379
  65.1 0.0 copy-start.6
  65.1 0.0 copy-start.7
  65.2 5.6 %all-to-all-done.2.summed_ref = bf16[16,2,16,320]{3,2,1,0:T(8,128)(2,1)} async-done(((bf16[16,2,16,320]{3,2,1,0:T(8,128)(2,1)}), bf16[16,2,16,320]{3,2,1,0:T(8,128)(2,1)}, u32[]{:S(2)}, u32[]{:S(2)}) %all-to-all-start.2) | async-done | bytes 327712 | tf_op jit(solution)/shard_map/all_to_all | solution.py:396
  70.8 0.0 copy-start.1
  70.8 1.1 %total.1.up_own = bf16[2,16,320]{2,1,0:T(8,128)(2,1)S(1)} custom-call(bf16[16,2,16,320]{3,2,1,0:T(8,128)(2,1)} %all-to-all-done.2.summed_ref, bf16[320,2880]{1,0:T(8,128)(2,1)S(1)} %copy.15.refs_0_.space_in, bf16[320,960]{1,0:T(8,128)(2,1)S(1)} %copy.16.refs_1_.time_in), custom_call_target="tpu_custom_call" | custom-call | tf_op jit(solution)/shard_map/total/pallas_call | solution.py:214
  71.9 1.9 %collective-permute-start.5 = (bf16[2,16,320]{2,1,0:T(8,128)(2,1)S(1)}, bf16[2,16,320]{2,1,0:T(8,128)(2,1)S(1)}, u32[]{:S(2)}, u32[]{:S(2)}) collective-permute-start(bf16[2,16,320]{2,1,0:T(8,128)(2,1)S(1)} %total.1.up_own), channel_id=1, source_target_pairs={{1,2},{3,4},{5,6},{7,8},{9,10},{11,12},{13,14},{15,16},{17,18},{19... | collective-permute-start | bytes 61448 | tf_op jit(solution)/shard_map/ppermute | solution.py:402
  73.8 0.0 collective-permute-done.3.next_in
  73.8 0.0 collective-permute-done.2.pair_in
  73.8 5.3 %collective-permute-done.5.up_next = bf16[2,16,320]{2,1,0:T(8,128)(2,1)S(1)} collective-permute-done((bf16[2,16,320]{2,1,0:T(8,128)(2,1)S(1)}, bf16[2,16,320]{2,1,0:T(8,128)(2,1)S(1)}, u32[]{:S(2)}, u32[]{:S(2)}) %collective-permute-start.5) | collective-permute-done | bytes 20512 | tf_op jit(solution)/shard_map/ppermute | solution.py:402
  79.1 0.0 copy-done.6
  79.1 0.0 copy-done.7
  79.1 0.0 copy-done.1
  79.1 8.5 %fine_stage.1 = bf16[2,4,320,128]{3,2,1,0:T(8,128)(2,1)S(1)} custom-call(bf16[2,4,320,128]{3,2,1,0:T(8,128)(2,1)S(1)} %bitcast.15, bf16[1,4,320,128]{3,2,1,0:T(8,128)(2,1)S(1)} %copy-done.1, bf16[1,4,320,128]{3,2,1,0:T(8,128)(2,1)S(1)} %collective-permute-done.1.right_ref.right_in, bf16[4,320,128]{2,1,0:T(8,128)(2,1)} %collective-permute-done.2.pair_in, ...), custom_call_target="tpu_custom_call" | custom-call | tf_op jit(solution)/shard_map/fine_stage/pallas_call | solution.py:343
  87.7 1.3 %copy.19 = bf16[2,320,4,128]{3,2,1,0:T(4,128)(2,1)} copy(bf16[2,320,4,128]{3,1,2,0:T(8,128)(2,1)S(1)} %bitcast.16) | data formatting | bytes 1310720 | tf_op jit(solution)/shard_map/transpose | solution.py:406
Async XLA Ops:
  0.0 37.9 %copy-start.5 = (bf16[4,8,80]{2,1,0:T(8,128)(2,1)S(1)}, bf16[4,8,80]{2,1,0:T(8,128)(2,1)}, u32[]{:S(2)}) copy-start(bf16[4,8,80]{2,1,0:T(8,128)(2,1)} %coarse_ref.1) | copy-start | bytes 15364
  0.0 32.7 %copy-start.4 = (bf16[80,1280]{1,0:T(8,128)(2,1)S(1)}, bf16[80,1280]{1,0:T(8,128)(2,1)}, u32[]{:S(2)}) copy-start(bf16[80,1280]{1,0:T(8,128)(2,1)} %out_w_ref.1) | copy-start | bytes 614404
  0.0 37.9 %copy-start.2 = (bf16[3,1280,80]{1,2,0:T(8,128)(2,1)S(1)}, bf16[3,1280,80]{1,2,0:T(8,128)(2,1)}, u32[]{:S(2)}) copy-start(bf16[3,1280,80]{1,2,0:T(8,128)(2,1)} %param.11) | copy-start | bytes 1843204
  1.8 30.9 %all-to-all-start = ((bf16[16,72,80]{2,1,0:T(8,128)(2,1)}), bf16[16,72,80]{2,1,0:T(8,128)(2,1)S(1)}, u32[]{:S(2)}, u32[]{:S(2)}) async-start(bf16[16,72,80]{2,1,0:T(8,128)(2,1)} %pack.1), calls=%async_computation | async-start | bytes 589824 | tf_op jit(solution)/shard_map/all_to_all | solution.py:374
  17.8 25.8 %copy-start.3 = (bf16[80,320]{1,0:T(8,128)(2,1)S(1)}, bf16[80,320]{1,0:T(8,128)(2,1)}, u32[]{:S(2)}) copy-start(bf16[80,320]{1,0:T(8,128)(2,1)} %up_ref.1) | copy-start | bytes 153604
  18.7 43.1 %copy-start.8 = (bf16[3,320,320]{2,1,0:T(8,128)(2,1)S(1)}, bf16[3,320,320]{2,1,0:T(8,128)(2,1)}, u32[]{:S(2)}) copy-start(bf16[3,320,320]{2,1,0:T(8,128)(2,1)} %param.17) | copy-start | bytes 1843204
  18.7 22.1 %collective-permute-start.1 = (bf16[1,4,320,128]{3,2,1,0:T(8,128)(2,1)}, bf16[1,4,320,128]{3,2,1,0:T(8,128)(2,1)S(1)}, u32[]{:S(2)}, u32[]{:S(2)}) collective-permute-start(bf16[1,4,320,128]{3,2,1,0:T(8,128)(2,1)} %get-tuple-element.13), channel_id=1, source_target_pairs={{32,0},{64,32},{96,64},{128,96},{160,128},{192,160},{224,192},{256... | collective-permute-start | bytes 983048 | tf_op jit(solution)/shard_map/ppermute | solution.py:378
  20.1 20.7 %collective-permute-start = (bf16[1,4,320,128]{3,2,1,0:T(8,128)(2,1)}, bf16[1,4,320,128]{3,2,1,0:T(8,128)(2,1)S(1)}, u32[]{:S(2)}, u32[]{:S(2)}) collective-permute-start(bf16[1,4,320,128]{3,2,1,0:T(8,128)(2,1)} %get-tuple-element.14), channel_id=1, source_target_pairs={{0,32},{32,64},{64,96},{96,128},{128,160},{160,192},{192,224},{224... | collective-permute-start | bytes 983048 | tf_op jit(solution)/shard_map/ppermute | solution.py:377
  33.6 10.0 %all-to-all-start.1 = ((bf16[8,40,80]{2,1,0:T(8,128)(2,1)}), bf16[8,40,80]{2,1,0:T(8,128)(2,1)S(1)}, u32[]{:S(2)}, u32[]{:S(2)}) async-start(bf16[8,40,80]{2,1,0:T(8,128)(2,1)} %get-tuple-element.12), calls=%async_computation.1 | async-start | bytes 163840 | tf_op jit(solution)/shard_map/all_to_all | solution.py:383
  38.4 3.4 %collective-permute-start.4 = (bf16[2,4,8,80]{3,2,1,0:T(8,128)(2,1)S(1)}, bf16[2,4,8,80]{3,2,1,0:T(8,128)(2,1)S(1)}, u32[]{:S(2)}, u32[]{:S(2)}) collective-permute-start(bf16[2,4,8,80]{3,2,1,0:T(8,128)(2,1)S(1)} %attend.1.mine_ref), channel_id=1, source_target_pairs={{0,1},{1,0},{2,3},{3,2},{4,5},{5,4},{6,7},{7,6},{8,9},{9,8},{10,11... | collective-permute-start | bytes 30728 | tf_op jit(solution)/shard_map/ppermute | solution.py:386
  40.8 21.0 %copy-start = (bf16[1,4,320,128]{3,2,1,0:T(8,128)(2,1)}, bf16[1,4,320,128]{3,2,1,0:T(8,128)(2,1)S(1)}, u32[]{:S(2)}) copy-start(bf16[1,4,320,128]{3,2,1,0:T(8,128)(2,1)S(1)} %collective-permute-done.left_ref.left_in) | copy-start | bytes 983044
  44.6 26.1 %all-to-all-start.2 = ((bf16[16,2,16,320]{3,2,1,0:T(8,128)(2,1)}), bf16[16,2,16,320]{3,2,1,0:T(8,128)(2,1)}, u32[]{:S(2)}, u32[]{:S(2)}) async-start(bf16[16,2,16,320]{3,2,1,0:T(8,128)(2,1)} %bitcast.3), calls=%async_computation.2 | async-start | bytes 786432 | tf_op jit(solution)/shard_map/all_to_all | solution.py:396
  56.4 17.4 %collective-permute-start.3 = (bf16[4,320,128]{2,1,0:T(8,128)(2,1)}, bf16[4,320,128]{2,1,0:T(8,128)(2,1)}, u32[]{:S(2)}, u32[]{:S(2)}) collective-permute-start(bf16[4,320,128]{2,1,0:T(8,128)(2,1)} %get-tuple-element.10), channel_id=1, source_target_pairs={{1,2},{3,4},{5,6},{7,8},{9,10},{11,12},{13,14},{15,16},{17,18},{19... | collective-permute-start | bytes 983048 | tf_op jit(solution)/shard_map/ppermute | solution.py:399
  58.3 15.5 %collective-permute-start.2 = (bf16[4,320,128]{2,1,0:T(8,128)(2,1)}, bf16[4,320,128]{2,1,0:T(8,128)(2,1)}, u32[]{:S(2)}, u32[]{:S(2)}) collective-permute-start(bf16[4,320,128]{2,1,0:T(8,128)(2,1)} %get-tuple-element.9._), channel_id=1, source_target_pairs={{0,1},{1,0},{2,3},{3,2},{4,5},{5,4},{6,7},{7,6},{8,9},{9,8},{10,11... | collective-permute-start | bytes 983048 | tf_op jit(solution)/shard_map/ppermute | solution.py:398
  65.1 14.0 %copy-start.6 = (f32[320]{0:T(512)S(1)}, f32[320]{0:T(512)}, u32[]{:S(2)}) copy-start(f32[320]{0:T(512)} %one_in.1) | copy-start | bytes 3844
  65.1 14.0 %copy-start.7 = (f32[320]{0:T(512)S(1)}, f32[320]{0:T(512)}, u32[]{:S(2)}) copy-start(f32[320]{0:T(512)} %two_in.1) | copy-start | bytes 3844
  70.8 8.4 %copy-start.1 = (bf16[1,4,320,128]{3,2,1,0:T(8,128)(2,1)S(1)}, bf16[1,4,320,128]{3,2,1,0:T(8,128)(2,1)}, u32[]{:S(2)}) copy-start(bf16[1,4,320,128]{3,2,1,0:T(8,128)(2,1)} %copy-done) | copy-start | bytes 983044
  71.9 7.3 %collective-permute-start.5 = (bf16[2,16,320]{2,1,0:T(8,128)(2,1)S(1)}, bf16[2,16,320]{2,1,0:T(8,128)(2,1)S(1)}, u32[]{:S(2)}, u32[]{:S(2)}) collective-permute-start(bf16[2,16,320]{2,1,0:T(8,128)(2,1)S(1)} %total.1.up_own), channel_id=1, source_target_pairs={{1,2},{3,4},{5,6},{7,8},{9,10},{11,12},{13,14},{15,16},{17,18},{19... | collective-permute-start | bytes 61448 | tf_op jit(solution)/shard_map/ppermute | solution.py:402

commit v4 on v3

--- a/solution.py
+++ b/solution.py
@@ -133,15 +133,15 @@
         in_specs=[VMEM] * 3,
         out_specs=VMEM,
         compiler_params=limit(2),
-        cost_estimate=FREE,
+        cost_estimate=pl.CostEstimate(flops=10000000000, bytes_accessed=0, transcendentals=0),
         name="attend",
     )(whole, w_qkv_t, coarse)
 
 
-def project(mine, other, folded, w_up, earlier, wanted):
+def project(mine, other, folded, w_up, wanted):
     cf, cells, width = mine.shape[1:]
 
-    def body(mine_ref, other_ref, folded_ref, up_ref, _, out_ref):
+    def body(mine_ref, other_ref, folded_ref, up_ref, out_ref):
         even = lax.rem(lax.axis_index("row"), 2) == 0
 
         def through(ref):
@@ -164,18 +164,19 @@
     return pl.pallas_call(
         body,
         out_shape=jax.ShapeDtypeStruct((len(wanted), 2 * cells, w_up.shape[1]), jnp.bfloat16),
-        in_specs=[VMEM] * 4 + [HBM],
+        in_specs=[VMEM] * 4,
         out_specs=VMEM,
         compiler_params=limit(2),
         cost_estimate=FREE,
         name="project",
-    )(mine, other, folded, w_up, earlier)
-
-
-def edge_rows(left, own, right):
+    )(mine, other, folded, w_up)
+
+
+def edge_rows(left, own, right, earlier):
     rows, channels, width = own.shape[1:]
 
-    def body(left_ref, own_ref, right_ref, pair_ref, next_ref, sems):
+    def body(left_ref, own_ref, right_ref, *refs):
+        pair_ref, next_ref, sems = refs[-3:]
         odd = lax.rem(lax.axis_index("row"), 2)
         frames = (left_ref.at[0], own_ref.at[0], own_ref.at[1], right_ref.at[0])
         moves = []
@@ -195,31 +196,31 @@
     return pl.pallas_call(
         body,
         out_shape=(shape, shape),
-        in_specs=[ANY] * 3,
+        in_specs=[ANY] * (3 + len(earlier)),
         out_specs=(ANY, ANY),
         scratch_shapes=[pltpu.SemaphoreType.DMA((8,))],
         compiler_params=limit(1),
         cost_estimate=FREE,
         name="edge_rows",
-    )(left, own, right)
-
-
-def total(summed, earlier):
-    def body(summed_ref, *refs):
+    )(left, own, right, *earlier)
+
+
+def total(summed):
+    def body(summed_ref, out_ref):
         result = summed_ref[0].astype(jnp.float32)
         for source in range(1, summed.shape[0]):
             result += summed_ref[source].astype(jnp.float32)
-        refs[-1][...] = result.astype(jnp.bfloat16)
+        out_ref[...] = result.astype(jnp.bfloat16)
 
     return pl.pallas_call(
         body,
         out_shape=jax.ShapeDtypeStruct(summed.shape[1:], jnp.bfloat16),
-        in_specs=[VMEM] + [ANY] * len(earlier),
+        in_specs=[VMEM],
         out_specs=VMEM,
         compiler_params=limit(2),
         cost_estimate=FREE,
         name="total",
-    )(summed, *earlier)
+    )(summed)
 
 
 def fine_kernel(
@@ -385,20 +386,19 @@
     mine = attend(whole, jnp.swapaxes(w_qkv, 1, 2), coarse)
     other = lax.ppermute(mine, "row", partner)
 
-    to_pair, to_next = edge_rows(left, rows_first, right)
-
     per = frames // cf
     wanted = []
     for f in range(frames):
         wanted.append(max(f - 1, 0) // per)
         wanted.append(min(f + 1, frames - 1) // per)
-    outgoing = project(mine, other, folded, w_up, to_pair, wanted).reshape(frames, 2, 2 * cells, fine_c)
+    outgoing = project(mine, other, folded, w_up, wanted).reshape(frames, 2, 2 * cells, fine_c)
     summed = lax.all_to_all(outgoing, "frame", 0, 0, tiled=True)
 
+    to_pair, to_next = edge_rows(left, rows_first, right, (outgoing, space, time))
     from_pair = lax.ppermute(to_pair, "row", partner)
     from_next = lax.ppermute(to_next, "row", across)
 
-    up_own = total(summed, (space, time))
+    up_own = total(summed)
     up_next = lax.ppermute(up_own, "row", across)
     result = fine_stage(
         rows_first, left, right, from_pair, from_next, up_own, up_next, gain_one, gain_two, space, time

time: 89.7 us -> 85.5 us (0.953)
  starting transfers between devices: 46.6 us -> 39.8 us
  Pallas kernels: 14.7 us -> 19.7 us
  waiting for transfers between devices: 20.8 us -> 18.4 us
    all_to_all x1, starting transfers between devices: 11.8 us -> 4.21 us  [local(): summed = lax.all_to_all(outgoing, 'frame', 0, 0, tiled=True)]
    pallas_call x1, Pallas kernels: 0.98 us -> 6.16 us  [edge_rows(): pl.pallas_call(body, out_shape=(shape, shape), in_specs=[ANY] * (3 + len(...]
    all_to_all x1, waiting for transfers between devices: 5.61 us -> 2.79 us  [local(): summed = lax.all_to_all(outgoing, 'frame', 0, 0, tiled=True)]
    ppermute x1, starting transfers between devices: 1.92 us -> 3.69 us  [local(): from_next = lax.ppermute(to_next, 'row', across)]
    ppermute x1, starting transfers between devices: 3.5 us -> 1.92 us  [local(): from_pair = lax.ppermute(to_pair, 'row', partner)]
    ppermute x1, waiting for transfers between devices: 0.01 us -> 1.33 us  [local(): from_next = lax.ppermute(to_next, 'row', across)]
    ppermute x1, waiting for transfers between devices: 5.31 us -> 3.98 us  [local(): up_next = lax.ppermute(up_own, 'row', across)]
  transfers between devices with their start and end apart: 9 -> 9, of which waited for: 4 -> 6; matrix products, arithmetic and copies ran while one was open for 6% -> 6% of each run, Pallas kernels for 4% -> 11%
where the time goes in v4:
time: 85.5 us; the launch traced here: 84.8 us
  starting transfers between devices  39.8 us (47%)
  Pallas kernels  19.7 us (23%)
  waiting for transfers between devices  18.4 us (22%)
  local copies, waits for them, and re-layouts  6.73 us (8%)
    all_to_all x1, starting transfers between devices, local(): arrived = lax.all_to_all(message, 'frame', 0, 0, tiled=True)  14.8 us
    pallas_call x1, Pallas kernels, fine_stage(): pl.pallas_call(fine_kernel, out_shape=jax.ShapeDtypeStruct(own.shape, bf1...  8.38 us
    all_to_all x1, waiting for transfers between devices, local(): arrived = lax.all_to_all(message, 'frame', 0, 0, tiled=True)  7.42 us
    pallas_call x1, Pallas kernels, edge_rows(): pl.pallas_call(body, out_shape=(shape, shape), in_specs=[ANY] * (3 + len(...  6.16 us
    ppermute x1, starting transfers between devices, local(): lax.ppermute(rows_first[1:], 'frame', [(i, i + 1) for i in range(frames -...  5.28 us
    all_to_all x1, starting transfers between devices, local(): lax.all_to_all(copies, 'row', 0, 0, tiled=True, axis_index_groups=groups)  4.3 us
    all_to_all x1, starting transfers between devices, local(): summed = lax.all_to_all(outgoing, 'frame', 0, 0, tiled=True)  4.21 us
    ppermute x1, waiting for transfers between devices, local(): up_next = lax.ppermute(up_own, 'row', across)  3.98 us
  transfers between devices with their start and end apart: 9, of which 6 were waited for; matrix products, arithmetic and copies ran while one was open for 6% of the time, Pallas kernels for 11%

profile of v4, /device:TPU:8, one launch (start us, length us, event | category | flops | bytes accessed | tf_op | source)
XLA Modules:
  0.0 84.8 jit_solution(1106487608689178301)
XLA Ops:
  0.0 0.0 copy-start.2
  0.0 0.0 copy-start.1
  0.0 0.0 copy-start.5
  0.0 1.8 %pack.1 = bf16[16,72,80]{2,1,0:T(8,128)(2,1)} custom-call(bf16[4,8,80]{2,1,0:T(8,128)(2,1)} %coarse_ref.1, bf16[80,320]{1,0:T(8,128)(2,1)} %up_ref.1), custom_call_target="tpu_custom_call" | custom-call | tf_op jit(solution)/shard_map/pack/pallas_call | solution.py:49
  1.8 14.8 %all-to-all-start = ((bf16[16,72,80]{2,1,0:T(8,128)(2,1)}), bf16[16,72,80]{2,1,0:T(8,128)(2,1)S(1)}, u32[]{:S(2)}, u32[]{:S(2)}) async-start(bf16[16,72,80]{2,1,0:T(8,128)(2,1)} %pack.1), calls=%async_computation | async-start | bytes 589824 | tf_op jit(solution)/shard_map/all_to_all | solution.py:375
  16.6 1.2 %copy.21 = bf16[2,320,4,128]{3,1,2,0:T(8,128)(2,1)S(1)} copy(bf16[2,320,4,128]{3,2,1,0:T(4,128)(2,1)} %param.9) | data formatting | bytes 1310720 | tf_op args[0]
  17.8 0.9 %fusion = (bf16[1,4,320,128]{3,2,1,0:T(8,128)(2,1)}, bf16[1,4,320,128]{3,2,1,0:T(8,128)(2,1)}) fusion(bf16[2,4,320,128]{3,2,1,0:T(8,128)(2,1)S(1)} %bitcast.13), kind=kLoop, calls=%fused_computation.1 | loop fusion | bytes 1310720 | tf_op jit(solution)/shard_map/slice | solution.py:379
  18.7 1.3 %collective-permute-start.1 = (bf16[1,4,320,128]{3,2,1,0:T(8,128)(2,1)}, bf16[1,4,320,128]{3,2,1,0:T(8,128)(2,1)S(1)}, u32[]{:S(2)}, u32[]{:S(2)}) collective-permute-start(bf16[1,4,320,128]{3,2,1,0:T(8,128)(2,1)} %get-tuple-element.13), channel_id=1, source_target_pairs={{32,0},{64,32},{96,64},{128,96},{160,128},{192,160},{224,192},{256... | collective-permute-start | bytes 983048 | tf_op jit(solution)/shard_map/ppermute | solution.py:379
  20.0 5.3 %collective-permute-start = (bf16[1,4,320,128]{3,2,1,0:T(8,128)(2,1)}, bf16[1,4,320,128]{3,2,1,0:T(8,128)(2,1)}, u32[]{:S(2)}, u32[]{:S(2)}) collective-permute-start(bf16[1,4,320,128]{3,2,1,0:T(8,128)(2,1)} %get-tuple-element.14), channel_id=1, source_target_pairs={{0,32},{32,64},{64,96},{96,128},{128,160},{160,192},{192,224},{224... | collective-permute-start | bytes 983048 | tf_op jit(solution)/shard_map/ppermute | solution.py:378
  25.3 7.4 %all-to-all-done.arrived_ref = bf16[16,72,80]{2,1,0:T(8,128)(2,1)S(1)} async-done(((bf16[16,72,80]{2,1,0:T(8,128)(2,1)}), bf16[16,72,80]{2,1,0:T(8,128)(2,1)S(1)}, u32[]{:S(2)}, u32[]{:S(2)}) %all-to-all-start) | async-done | bytes 184352 | tf_op jit(solution)/shard_map/all_to_all | solution.py:375
  32.7 0.0 copy-done.1
  32.7 0.9 %fold.1 = (bf16[8,40,80]{2,1,0:T(8,128)(2,1)}, bf16[32,1280]{1,0:T(8,128)(2,1)S(1)}) custom-call(bf16[16,72,80]{2,1,0:T(8,128)(2,1)S(1)} %all-to-all-done.arrived_ref, bf16[80,1280]{1,0:T(8,128)(2,1)S(1)} %copy-done.1), custom_call_target="tpu_custom_call" | custom-call | tf_op jit(solution)/shard_map/fold/pallas_call | solution.py:82
  33.6 4.3 %all-to-all-start.1 = ((bf16[8,40,80]{2,1,0:T(8,128)(2,1)}), bf16[8,40,80]{2,1,0:T(8,128)(2,1)S(1)}, u32[]{:S(2)}, u32[]{:S(2)}) async-start(bf16[8,40,80]{2,1,0:T(8,128)(2,1)} %get-tuple-element.10), calls=%async_computation.1 | async-start | bytes 163840 | tf_op jit(solution)/shard_map/all_to_all | solution.py:384
  37.9 0.0 copy-done.2
  37.9 0.0 copy-done.5
  38.0 0.0 copy-start
  38.0 0.0 copy-start.6
  38.0 0.4 attend.1.mine_ref
  38.4 2.4 %collective-permute-start.2 = (bf16[2,4,8,80]{3,2,1,0:T(8,128)(2,1)S(1)}, bf16[2,4,8,80]{3,2,1,0:T(8,128)(2,1)S(1)}, u32[]{:S(2)}, u32[]{:S(2)}) collective-permute-start(bf16[2,4,8,80]{3,2,1,0:T(8,128)(2,1)S(1)} %attend.1.mine_ref), channel_id=1, source_target_pairs={{0,1},{1,0},{2,3},{3,2},{4,5},{5,4},{6,7},{7,6},{8,9},{9,8},{10,11... | collective-permute-start | bytes 30728 | tf_op jit(solution)/shard_map/ppermute | solution.py:387
  40.8 0.8 collective-permute-done.2.other_ref
  41.6 2.0 %all-to-all-done.1 = bf16[8,40,80]{2,1,0:T(8,128)(2,1)S(1)} async-done(((bf16[8,40,80]{2,1,0:T(8,128)(2,1)}), bf16[8,40,80]{2,1,0:T(8,128)(2,1)S(1)}, u32[]{:S(2)}, u32[]{:S(2)}) %all-to-all-start.1) | async-done | bytes 51232 | tf_op jit(solution)/shard_map/all_to_all | solution.py:384
  43.7 0.0 copy-done
  43.7 1.0 %project.1 = bf16[32,16,320]{2,1,0:T(8,128)(2,1)} custom-call(bf16[2,4,8,80]{3,2,1,0:T(8,128)(2,1)S(1)} %attend.1.mine_ref, bf16[2,4,8,80]{3,2,1,0:T(8,128)(2,1)S(1)} %collective-permute-done.2.other_ref, bf16[320,80]{1,0:T(8,128)(2,1)S(1)} %bitcast.17, bf16[80,320]{1,0:T(8,128)(2,1)S(1)} %copy-done), custom_call_target="tpu_custom_call" | custom-call | tf_op jit(solution)/shard_map/project/pallas_call | solution.py:164
  44.6 4.2 %all-to-all-start.2 = ((bf16[16,2,16,320]{3,2,1,0:T(8,128)(2,1)}), bf16[16,2,16,320]{3,2,1,0:T(8,128)(2,1)}, u32[]{:S(2)}, u32[]{:S(2)}) async-start(bf16[16,2,16,320]{3,2,1,0:T(8,128)(2,1)} %bitcast.3.refs_0_), calls=%async_computation.2 | async-start | bytes 786432 | tf_op jit(solution)/shard_map/all_to_all | solution.py:395
  48.9 0.0 copy-done.6
  48.9 0.3 copy.16.refs_2_.time_in
  49.2 3.0 %copy.15.refs_1_.space_in = bf16[320,2880]{1,0:T(8,128)(2,1)S(1)} copy(bf16[320,2880]{0,1:T(8,128)(2,1)} %bitcast.19) | data formatting | bytes 3686400 | tf_op jit(solution)/shard_map/reshape | solution.py:380
  52.1 0.0 copy-start.3
  52.2 0.0 copy-start.4
  52.2 0.0 collective-permute-done.1.right_ref.right_in
  52.2 0.0 collective-permute-done.left_ref.left_in
  52.2 6.2 %edge_rows.1 = (bf16[4,320,128]{2,1,0:T(8,128)(2,1)}, bf16[4,320,128]{2,1,0:T(8,128)(2,1)}) custom-call(bf16[1,4,320,128]{3,2,1,0:T(8,128)(2,1)} %collective-permute-done.left_ref.left_in, bf16[2,4,320,128]{3,2,1,0:T(8,128)(2,1)S(1)} %bitcast.14, bf16[1,4,320,128]{3,2,1,0:T(8,128)(2,1)S(1)} %collective-permute-done.1.right_ref.right_in, ...), custom_call_target="tpu_custom_call" | custom-call | tf_op jit(solution)/shard_map/edge_rows/pallas_call | solution.py:196
  58.3 1.9 %collective-permute-start.3 = (bf16[4,320,128]{2,1,0:T(8,128)(2,1)}, bf16[4,320,128]{2,1,0:T(8,128)(2,1)}, u32[]{:S(2)}, u32[]{:S(2)}) collective-permute-start(bf16[4,320,128]{2,1,0:T(8,128)(2,1)} %get-tuple-element.11), channel_id=1, source_target_pairs={{0,1},{1,0},{2,3},{3,2},{4,5},{5,4},{6,7},{7,6},{8,9},{9,8},{10,11... | collective-permute-start | bytes 983048 | tf_op jit(solution)/shard_map/ppermute | solution.py:398
  60.3 3.7 %collective-permute-start.4 = (bf16[4,320,128]{2,1,0:T(8,128)(2,1)}, bf16[4,320,128]{2,1,0:T(8,128)(2,1)}, u32[]{:S(2)}, u32[]{:S(2)}) collective-permute-start(bf16[4,320,128]{2,1,0:T(8,128)(2,1)} %get-tuple-element.12), channel_id=1, source_target_pairs={{1,2},{3,4},{5,6},{7,8},{9,10},{11,12},{13,14},{15,16},{17,18},{19... | collective-permute-start | bytes 983048 | tf_op jit(solution)/shard_map/ppermute | solution.py:399
  64.0 2.8 %all-to-all-done.2.summed_ref = bf16[16,2,16,320]{3,2,1,0:T(8,128)(2,1)} async-done(((bf16[16,2,16,320]{3,2,1,0:T(8,128)(2,1)}), bf16[16,2,16,320]{3,2,1,0:T(8,128)(2,1)}, u32[]{:S(2)}, u32[]{:S(2)}) %all-to-all-start.2) | async-done | bytes 327712 | tf_op jit(solution)/shard_map/all_to_all | solution.py:395
  66.8 1.1 %total.1.up_own = bf16[2,16,320]{2,1,0:T(8,128)(2,1)S(1)} custom-call(bf16[16,2,16,320]{3,2,1,0:T(8,128)(2,1)} %all-to-all-done.2.summed_ref), custom_call_target="tpu_custom_call" | custom-call | tf_op jit(solution)/shard_map/total/pallas_call | solution.py:215
  67.8 1.9 %collective-permute-start.5 = (bf16[2,16,320]{2,1,0:T(8,128)(2,1)S(1)}, bf16[2,16,320]{2,1,0:T(8,128)(2,1)S(1)}, u32[]{:S(2)}, u32[]{:S(2)}) collective-permute-start(bf16[2,16,320]{2,1,0:T(8,128)(2,1)S(1)} %total.1.up_own), channel_id=1, source_target_pairs={{1,2},{3,4},{5,6},{7,8},{9,10},{11,12},{13,14},{15,16},{17,18},{19... | collective-permute-start | bytes 61448 | tf_op jit(solution)/shard_map/ppermute | solution.py:402
  69.8 0.0 collective-permute-done.3.pair_in
  69.8 1.3 %collective-permute-done.4.next_in = bf16[4,320,128]{2,1,0:T(8,128)(2,1)} collective-permute-done((bf16[4,320,128]{2,1,0:T(8,128)(2,1)}, bf16[4,320,128]{2,1,0:T(8,128)(2,1)}, u32[]{:S(2)}, u32[]{:S(2)}) %collective-permute-start.4) | collective-permute-done | bytes 327712 | tf_op jit(solution)/shard_map/ppermute | solution.py:399
  71.1 4.0 %collective-permute-done.5.up_next = bf16[2,16,320]{2,1,0:T(8,128)(2,1)S(1)} collective-permute-done((bf16[2,16,320]{2,1,0:T(8,128)(2,1)S(1)}, bf16[2,16,320]{2,1,0:T(8,128)(2,1)S(1)}, u32[]{:S(2)}, u32[]{:S(2)}) %collective-permute-start.5) | collective-permute-done | bytes 20512 | tf_op jit(solution)/shard_map/ppermute | solution.py:402
  75.1 0.0 copy-done.3
  75.1 0.0 copy-done.4
  75.1 8.4 %fine_stage.1 = bf16[2,4,320,128]{3,2,1,0:T(8,128)(2,1)S(1)} custom-call(bf16[2,4,320,128]{3,2,1,0:T(8,128)(2,1)S(1)} %bitcast.15, bf16[1,4,320,128]{3,2,1,0:T(8,128)(2,1)} %collective-permute-done.left_ref.left_in, bf16[1,4,320,128]{3,2,1,0:T(8,128)(2,1)S(1)} %collective-permute-done.1.right_ref.right_in, ...), custom_call_target="tpu_custom_call" | custom-call | tf_op jit(solution)/shard_map/fine_stage/pallas_call | solution.py:344
  83.5 1.3 %copy.19 = bf16[2,320,4,128]{3,2,1,0:T(4,128)(2,1)} copy(bf16[2,320,4,128]{3,1,2,0:T(8,128)(2,1)S(1)} %bitcast.16) | data formatting | bytes 1310720 | tf_op jit(solution)/shard_map/transpose | solution.py:406
Async XLA Ops:
  0.0 37.9 %copy-start.2 = (bf16[4,8,80]{2,1,0:T(8,128)(2,1)S(1)}, bf16[4,8,80]{2,1,0:T(8,128)(2,1)}, u32[]{:S(2)}) copy-start(bf16[4,8,80]{2,1,0:T(8,128)(2,1)} %coarse_ref.1) | copy-start | bytes 15364
  0.0 32.7 %copy-start.1 = (bf16[80,1280]{1,0:T(8,128)(2,1)S(1)}, bf16[80,1280]{1,0:T(8,128)(2,1)}, u32[]{:S(2)}) copy-start(bf16[80,1280]{1,0:T(8,128)(2,1)} %out_w_ref.1) | copy-start | bytes 614404
  0.0 37.9 %copy-start.5 = (bf16[3,1280,80]{1,2,0:T(8,128)(2,1)S(1)}, bf16[3,1280,80]{1,2,0:T(8,128)(2,1)}, u32[]{:S(2)}) copy-start(bf16[3,1280,80]{1,2,0:T(8,128)(2,1)} %param.11) | copy-start | bytes 1843204
  1.8 30.9 %all-to-all-start = ((bf16[16,72,80]{2,1,0:T(8,128)(2,1)}), bf16[16,72,80]{2,1,0:T(8,128)(2,1)S(1)}, u32[]{:S(2)}, u32[]{:S(2)}) async-start(bf16[16,72,80]{2,1,0:T(8,128)(2,1)} %pack.1), calls=%async_computation | async-start | bytes 589824 | tf_op jit(solution)/shard_map/all_to_all | solution.py:375
  18.7 33.4 %collective-permute-start.1 = (bf16[1,4,320,128]{3,2,1,0:T(8,128)(2,1)}, bf16[1,4,320,128]{3,2,1,0:T(8,128)(2,1)S(1)}, u32[]{:S(2)}, u32[]{:S(2)}) collective-permute-start(bf16[1,4,320,128]{3,2,1,0:T(8,128)(2,1)} %get-tuple-element.13), channel_id=1, source_target_pairs={{32,0},{64,32},{96,64},{128,96},{160,128},{192,160},{224,192},{256... | collective-permute-start | bytes 983048 | tf_op jit(solution)/shard_map/ppermute | solution.py:379
  20.0 32.2 %collective-permute-start = (bf16[1,4,320,128]{3,2,1,0:T(8,128)(2,1)}, bf16[1,4,320,128]{3,2,1,0:T(8,128)(2,1)}, u32[]{:S(2)}, u32[]{:S(2)}) collective-permute-start(bf16[1,4,320,128]{3,2,1,0:T(8,128)(2,1)} %get-tuple-element.14), channel_id=1, source_target_pairs={{0,32},{32,64},{64,96},{96,128},{128,160},{160,192},{192,224},{224... | collective-permute-start | bytes 983048 | tf_op jit(solution)/shard_map/ppermute | solution.py:378
  33.6 10.0 %all-to-all-start.1 = ((bf16[8,40,80]{2,1,0:T(8,128)(2,1)}), bf16[8,40,80]{2,1,0:T(8,128)(2,1)S(1)}, u32[]{:S(2)}, u32[]{:S(2)}) async-start(bf16[8,40,80]{2,1,0:T(8,128)(2,1)} %get-tuple-element.10), calls=%async_computation.1 | async-start | bytes 163840 | tf_op jit(solution)/shard_map/all_to_all | solution.py:384
  38.0 5.7 %copy-start = (bf16[80,320]{1,0:T(8,128)(2,1)S(1)}, bf16[80,320]{1,0:T(8,128)(2,1)}, u32[]{:S(2)}) copy-start(bf16[80,320]{1,0:T(8,128)(2,1)} %up_ref.1) | copy-start | bytes 153604
  38.0 10.9 %copy-start.6 = (bf16[3,320,320]{2,1,0:T(8,128)(2,1)S(1)}, bf16[3,320,320]{2,1,0:T(8,128)(2,1)}, u32[]{:S(2)}) copy-start(bf16[3,320,320]{2,1,0:T(8,128)(2,1)} %param.17) | copy-start | bytes 1843204
  38.4 3.2 %collective-permute-start.2 = (bf16[2,4,8,80]{3,2,1,0:T(8,128)(2,1)S(1)}, bf16[2,4,8,80]{3,2,1,0:T(8,128)(2,1)S(1)}, u32[]{:S(2)}, u32[]{:S(2)}) collective-permute-start(bf16[2,4,8,80]{3,2,1,0:T(8,128)(2,1)S(1)} %attend.1.mine_ref), channel_id=1, source_target_pairs={{0,1},{1,0},{2,3},{3,2},{4,5},{5,4},{6,7},{7,6},{8,9},{9,8},{10,11... | collective-permute-start | bytes 30728 | tf_op jit(solution)/shard_map/ppermute | solution.py:387
  44.6 22.1 %all-to-all-start.2 = ((bf16[16,2,16,320]{3,2,1,0:T(8,128)(2,1)}), bf16[16,2,16,320]{3,2,1,0:T(8,128)(2,1)}, u32[]{:S(2)}, u32[]{:S(2)}) async-start(bf16[16,2,16,320]{3,2,1,0:T(8,128)(2,1)} %bitcast.3.refs_0_), calls=%async_computation.2 | async-start | bytes 786432 | tf_op jit(solution)/shard_map/all_to_all | solution.py:395
  52.1 22.9 %copy-start.3 = (f32[320]{0:T(512)S(1)}, f32[320]{0:T(512)}, u32[]{:S(2)}) copy-start(f32[320]{0:T(512)} %one_in.1) | copy-start | bytes 3844
  52.2 22.9 %copy-start.4 = (f32[320]{0:T(512)S(1)}, f32[320]{0:T(512)}, u32[]{:S(2)}) copy-start(f32[320]{0:T(512)} %two_in.1) | copy-start | bytes 3844
  58.3 11.4 %collective-permute-start.3 = (bf16[4,320,128]{2,1,0:T(8,128)(2,1)}, bf16[4,320,128]{2,1,0:T(8,128)(2,1)}, u32[]{:S(2)}, u32[]{:S(2)}) collective-permute-start(bf16[4,320,128]{2,1,0:T(8,128)(2,1)} %get-tuple-element.11), channel_id=1, source_target_pairs={{0,1},{1,0},{2,3},{3,2},{4,5},{5,4},{6,7},{7,6},{8,9},{9,8},{10,11... | collective-permute-start | bytes 983048 | tf_op jit(solution)/shard_map/ppermute | solution.py:398
  60.3 10.8 %collective-permute-start.4 = (bf16[4,320,128]{2,1,0:T(8,128)(2,1)}, bf16[4,320,128]{2,1,0:T(8,128)(2,1)}, u32[]{:S(2)}, u32[]{:S(2)}) collective-permute-start(bf16[4,320,128]{2,1,0:T(8,128)(2,1)} %get-tuple-element.12), channel_id=1, source_target_pairs={{1,2},{3,4},{5,6},{7,8},{9,10},{11,12},{13,14},{15,16},{17,18},{19... | collective-permute-start | bytes 983048 | tf_op jit(solution)/shard_map/ppermute | solution.py:399
  67.8 7.3 %collective-permute-start.5 = (bf16[2,16,320]{2,1,0:T(8,128)(2,1)S(1)}, bf16[2,16,320]{2,1,0:T(8,128)(2,1)S(1)}, u32[]{:S(2)}, u32[]{:S(2)}) collective-permute-start(bf16[2,16,320]{2,1,0:T(8,128)(2,1)S(1)} %total.1.up_own), channel_id=1, source_target_pairs={{1,2},{3,4},{5,6},{7,8},{9,10},{11,12},{13,14},{15,16},{17,18},{19... | collective-permute-start | bytes 61448 | tf_op jit(solution)/shard_map/ppermute | solution.py:402

commit v5 on v4

--- a/solution.py
+++ b/solution.py
@@ -197,9 +197,9 @@
         body,
         out_shape=(shape, shape),
         in_specs=[ANY] * (3 + len(earlier)),
-        out_specs=(ANY, ANY),
+        out_specs=(VMEM, VMEM),
         scratch_shapes=[pltpu.SemaphoreType.DMA((8,))],
-        compiler_params=limit(1),
+        compiler_params=limit(2),
         cost_estimate=FREE,
         name="edge_rows",
     )(left, own, right, *earlier)
@@ -224,8 +224,8 @@
 
 
 def fine_kernel(
-    own, left_in, right_in, pair_in, next_in, up_own, up_next, one_in, two_in, space_in, time_in,
-    out, left, right, pair, beyond, space, time, gains, stack, second, merged, sems,
+    own, left_in, right_in, pair_in, next_in, up_own, up_next, one_in, two_in, space, time,
+    out, left, right, pair, beyond, gains, stack, second, merged, mixed, turned, sems, out_sems,
 ):
     channels, width = own.shape[2:]
     cells = up_own.shape[1]
@@ -238,10 +238,9 @@
     valid_before = (frame_index > 0).astype(jnp.float32)
     valid_after = (frame_index < last_frame).astype(jnp.float32)
 
-    moves = []
+    moves, leaving = [], []
     halo = ((left_in, left), (right_in, right), (pair_in, pair), (next_in, beyond))
-    kernels = ((space_in, space), (time_in, time))
-    for place, (source, target) in enumerate((*halo, *kernels)):
+    for place, (source, target) in enumerate(halo):
         moves.append(pltpu.make_async_copy(source, target, sems.at[place]))
     for move in moves:
         move.start()
@@ -279,80 +278,104 @@
         if frame in (1, 2) and 1 <= position <= 4:
             merged[frame - 1, position - 1] = total
         normed = norm(total.astype(jnp.float32), gain_one, scale)
-        before = jnp.where(lane == 0, 0.0, pltpu.roll(normed, 1, 1))
-        after = jnp.where(lane == width - 1, 0.0, pltpu.roll(normed, width - 1, 1))
-        lanes = pl.ds(width * (frame % 2), width)
+        normed = normed.astype(jnp.bfloat16)
+        before = jnp.where(lane == 0, jnp.zeros_like(normed), pltpu.roll(normed, 1, 1))
+        after = jnp.where(lane == width - 1, jnp.zeros_like(normed), pltpu.roll(normed, width - 1, 1))
+        half, side = ((1, 0), (0, 0), (0, 1), (1, 1))[frame]
+        lanes = pl.ds(width * side, width)
         for place, part in enumerate((before, normed, after)):
-            stack[frame // 2, position, pl.ds(place * channels, channels), lanes] = part.astype(
+            stack[half, position, pl.ds(place * channels, channels), lanes] = part
+
+    here, further = spread(up_own), spread(up_next)
+    held = (left.at[0], own.at[0], own.at[1], right.at[0])
+
+    halves = ((1, 2), (0, 3))
+
+    def first_norm(half, position):
+        for frame in halves[half]:
+            if position == 0:
+                pixels = jnp.where(even, beyond[frame], pair[frame])
+                added = jnp.where(even, further[frame], here[frame])
+                keep(frame, 0, pixels, added, valid_above)
+            elif position == 5:
+                pixels = jnp.where(even, pair[frame], beyond[frame])
+                added = jnp.where(even, here[frame], further[frame])
+                keep(frame, 5, pixels, added, valid_below)
+            else:
+                keep(frame, position, held[frame][position - 1], here[frame], None)
+
+    def convolve(half, row_out):
+        window = stack[half, pl.ds(row_out, 3)].reshape(9 * channels, 2 * width)
+        return jnp.dot(space[...], window, preferred_element_type=jnp.float32)
+
+    def second_norm(half, row_out, spatial):
+        for side in range(2):
+            frame = halves[half][side]
+            scale = (valid_before, None, None, valid_after)[frame]
+            normed = norm(spatial[:, side * width : (side + 1) * width], gain_two, scale)
+            second[row_out // 2, frame, :, pl.ds(width * (row_out % 2), width)] = normed.astype(
                 jnp.bfloat16
             )
 
-    here, further = spread(up_own), spread(up_next)
-    for position in range(1, 5):
-        keep(1, position, own[0, position - 1], here[1], None)
-    for move in moves[:4]:
+    for move in moves:
         move.wait()
-
-    def edges(frame):
-        near, far = pair[frame], beyond[frame]
-        keep(
-            frame, 0, jnp.where(even, far, near), jnp.where(even, further[frame], here[frame]), valid_above
-        )
-        keep(
-            frame, 5, jnp.where(even, near, far), jnp.where(even, here[frame], further[frame]), valid_below
-        )
-
-    for position in range(1, 5):
-        keep(0, position, left[0, position - 1], here[0], None)
-    edges(0)
-    edges(1)
-    moves[4].wait()
-    for half in range(2):
-        if half == 1:
-            for position in range(1, 5):
-                keep(2, position, own[1, position - 1], here[2], None)
-                keep(3, position, right[0, position - 1], here[3], None)
-            edges(2)
-            edges(3)
-        for row_out in range(4):
-            window = stack[half, pl.ds(row_out, 3)].reshape(9 * channels, 2 * width)
-            spatial = jnp.dot(space[...], window, preferred_element_type=jnp.float32)
-            for side in range(2):
-                frame = 2 * half + side
-                scale = (valid_before, None, None, valid_after)[frame]
-                normed = norm(spatial[:, side * width : (side + 1) * width], gain_two, scale)
-                second[row_out // 2, frame, :, pl.ds(width * (row_out % 2), width)] = normed.astype(
-                    jnp.bfloat16
-                )
-
-    moves[5].wait()
+    for position in (1, 2, 3):
+        first_norm(0, position)
+    order = ((0, 1), (0, 2), (0, 0), (0, 3), (1, 1), (1, 2), (1, 0), (1, 3))
+    ahead = {
+        (0, 1): ((0, 4), (0, 0)),
+        (0, 2): ((0, 5), (1, 1)),
+        (0, 0): ((1, 2),),
+        (0, 3): ((1, 3),),
+        (1, 1): ((1, 4), (1, 0)),
+        (1, 2): ((1, 5),),
+    }
+    waiting = None
+    for half, row_out in order:
+        current = convolve(half, row_out)
+        for other in ahead.get((half, row_out), ()):
+            first_norm(*other)
+        if waiting is not None:
+            second_norm(*waiting)
+        waiting = (half, row_out, current)
+    second_norm(*waiting)
+
     for frame in range(2):
         for half in range(2):
             window = second[half, pl.ds(frame, 3)].reshape(3 * channels, 2 * width)
             temporal = jnp.dot(time[...], window, preferred_element_type=jnp.float32)
             for side in range(2):
                 row_out = 2 * half + side
-                total = merged[frame, row_out].astype(jnp.float32)
-                total += temporal[:, side * width : (side + 1) * width]
-                out[frame, row_out] = total.astype(jnp.bfloat16)
+                sums = merged[frame, row_out].astype(jnp.float32)
+                sums += temporal[:, side * width : (side + 1) * width]
+                mixed[frame, pl.ds(row_out, channels, stride=4), :] = sums
+        turned[frame] = mixed[frame].reshape(channels, 4, width).astype(jnp.bfloat16)
+        leave = pltpu.make_async_copy(turned.at[frame], out.at[frame], out_sems.at[frame])
+        leave.start()
+        leaving.append(leave)
+    for leave in leaving:
+        leave.wait()
 
 
 def fine_stage(own, left, right, pair, beyond, up_own, up_next, gain_one, gain_two, space, time):
     channels, width = own.shape[2:]
     bf16 = jnp.bfloat16
-    copied = (left, right, pair, beyond, space, time)
+    copied = (left, right, pair, beyond)
     return pl.pallas_call(
         fine_kernel,
-        out_shape=jax.ShapeDtypeStruct(own.shape, bf16),
-        in_specs=[VMEM] + [HBM] * 4 + [VMEM] * 4 + [HBM] * 2,
-        out_specs=VMEM,
+        out_shape=jax.ShapeDtypeStruct((2, channels, 4, width), bf16),
+        in_specs=[VMEM] + [HBM] * 4 + [VMEM] * 6,
+        out_specs=HBM,
         scratch_shapes=[pltpu.VMEM(array.shape, array.dtype) for array in copied]
         + [
             pltpu.VMEM((2, channels, width), jnp.float32),
             pltpu.VMEM((2, 6, 3 * channels, 2 * width), bf16),
             pltpu.VMEM((2, 4, channels, 2 * width), bf16),
             pltpu.VMEM((2, 4, channels, width), bf16),
+            pltpu.VMEM((2, 4 * channels, width), jnp.float32),
+            pltpu.VMEM((2, channels, 4, width), bf16),
             pltpu.SemaphoreType.DMA((len(copied),)),
+            pltpu.SemaphoreType.DMA((2,)),
         ],
         compiler_params=limit(28),
         name="fine_stage",
@@ -400,10 +423,9 @@
 
     up_own = total(summed)
     up_next = lax.ppermute(up_own, "row", across)
-    result = fine_stage(
+    return fine_stage(
         rows_first, left, right, from_pair, from_next, up_own, up_next, gain_one, gain_two, space, time
     )
-    return jnp.swapaxes(result, 1, 2)
 
 
 def solution(mesh):

time: 85.5 us -> 84.2 us (0.985)
  Pallas kernels: 19.7 us -> 15.4 us
  waiting for transfers between devices: 18.4 us -> 22.6 us
  local copies, waits for them, and re-layouts: 6.73 us -> 5.39 us
    pallas_call x1, Pallas kernels: 6.16 us -> 1.88 us  [edge_rows(): pl.pallas_call(body, out_shape=(shape, shape), in_specs=[ANY] * (3 + len(...]
    all_to_all x1, waiting for transfers between devices: 2.79 us -> 7.07 us  [local(): summed = lax.all_to_all(outgoing, 'frame', 0, 0, tiled=True)]
    transpose x1 -> x0, local copies, waits for them, and re-layouts: 1.34 us -> none  [local(): return jnp.swapaxes(result, 1, 2)]
    ppermute x1, waiting for transfers between devices: 1.33 us -> 0.01 us  [local(): from_next = lax.ppermute(to_next, 'row', across)]
    ppermute x1, waiting for transfers between devices: 3.98 us -> 5.31 us  [local(): up_next = lax.ppermute(up_own, 'row', across)]
  transfers between devices with their start and end apart: 9 -> 9, of which waited for: 6 -> 5; matrix products, arithmetic and copies ran while one was open for 6% -> 6% of each run, Pallas kernels for 11% -> 6%
where the time goes in v5:
time: 84.2 us; the launch traced here: 83.5 us
  starting transfers between devices  39.8 us (47%)
  waiting for transfers between devices  22.6 us (27%)
  Pallas kernels  15.4 us (18%)
  local copies, waits for them, and re-layouts  5.39 us (6%)
    all_to_all x1, starting transfers between devices, local(): arrived = lax.all_to_all(message, 'frame', 0, 0, tiled=True)  14.8 us
    pallas_call x1, Pallas kernels, fine_stage(): pl.pallas_call(fine_kernel, out_shape=jax.ShapeDtypeStruct((2, channels,...  8.36 us
    all_to_all x1, waiting for transfers between devices, local(): arrived = lax.all_to_all(message, 'frame', 0, 0, tiled=True)  7.42 us
    all_to_all x1, waiting for transfers between devices, local(): summed = lax.all_to_all(outgoing, 'frame', 0, 0, tiled=True)  7.07 us
    ppermute x1, waiting for transfers between devices, local(): up_next = lax.ppermute(up_own, 'row', across)  5.31 us
    ppermute x1, starting transfers between devices, local(): lax.ppermute(rows_first[1:], 'frame', [(i, i + 1) for i in range(frames -...  5.28 us
    all_to_all x1, starting transfers between devices, local(): lax.all_to_all(copies, 'row', 0, 0, tiled=True, axis_index_groups=groups)  4.3 us
    all_to_all x1, starting transfers between devices, local(): summed = lax.all_to_all(outgoing, 'frame', 0, 0, tiled=True)  4.21 us
  transfers between devices with their start and end apart: 9, of which 5 were waited for; matrix products, arithmetic and copies ran while one was open for 6% of the time, Pallas kernels for 6%

profile of v5, /device:TPU:8, one launch (start us, length us, event | category | flops | bytes accessed | tf_op | source)
XLA Modules:
  0.0 83.5 jit_solution(13411240987682903877)
XLA Ops:
  0.0 0.0 copy-start.2
  0.0 0.0 copy-start.1
  0.0 0.0 copy-start.5
  0.0 1.8 %pack.1 = bf16[16,72,80]{2,1,0:T(8,128)(2,1)} custom-call(bf16[4,8,80]{2,1,0:T(8,128)(2,1)} %coarse_ref.1, bf16[80,320]{1,0:T(8,128)(2,1)} %up_ref.1), custom_call_target="tpu_custom_call" | custom-call | tf_op jit(solution)/shard_map/pack/pallas_call | solution.py:49
  1.8 14.8 %all-to-all-start = ((bf16[16,72,80]{2,1,0:T(8,128)(2,1)}), bf16[16,72,80]{2,1,0:T(8,128)(2,1)S(1)}, u32[]{:S(2)}, u32[]{:S(2)}) async-start(bf16[16,72,80]{2,1,0:T(8,128)(2,1)} %pack.1), calls=%async_computation | async-start | bytes 589824 | tf_op jit(solution)/shard_map/all_to_all | solution.py:398
  16.6 1.2 %copy.19 = bf16[2,320,4,128]{3,1,2,0:T(8,128)(2,1)S(1)} copy(bf16[2,320,4,128]{3,2,1,0:T(4,128)(2,1)} %param.9) | data formatting | bytes 1310720 | tf_op args[0]
  17.8 0.9 %fusion = (bf16[1,4,320,128]{3,2,1,0:T(8,128)(2,1)}, bf16[1,4,320,128]{3,2,1,0:T(8,128)(2,1)}) fusion(bf16[2,4,320,128]{3,2,1,0:T(8,128)(2,1)S(1)} %bitcast.12), kind=kLoop, calls=%fused_computation.1 | loop fusion | bytes 1310720 | tf_op jit(solution)/shard_map/slice | solution.py:402
  18.7 1.3 %collective-permute-start.1 = (bf16[1,4,320,128]{3,2,1,0:T(8,128)(2,1)}, bf16[1,4,320,128]{3,2,1,0:T(8,128)(2,1)S(1)}, u32[]{:S(2)}, u32[]{:S(2)}) collective-permute-start(bf16[1,4,320,128]{3,2,1,0:T(8,128)(2,1)} %get-tuple-element.13), channel_id=1, source_target_pairs={{32,0},{64,32},{96,64},{128,96},{160,128},{192,160},{224,192},{256... | collective-permute-start | bytes 983048 | tf_op jit(solution)/shard_map/ppermute | solution.py:402
  20.0 5.3 %collective-permute-start = (bf16[1,4,320,128]{3,2,1,0:T(8,128)(2,1)}, bf16[1,4,320,128]{3,2,1,0:T(8,128)(2,1)}, u32[]{:S(2)}, u32[]{:S(2)}) collective-permute-start(bf16[1,4,320,128]{3,2,1,0:T(8,128)(2,1)} %get-tuple-element.14), channel_id=1, source_target_pairs={{0,32},{32,64},{64,96},{96,128},{128,160},{160,192},{192,224},{224... | collective-permute-start | bytes 983048 | tf_op jit(solution)/shard_map/ppermute | solution.py:401
  25.3 7.4 %all-to-all-done.arrived_ref = bf16[16,72,80]{2,1,0:T(8,128)(2,1)S(1)} async-done(((bf16[16,72,80]{2,1,0:T(8,128)(2,1)}), bf16[16,72,80]{2,1,0:T(8,128)(2,1)S(1)}, u32[]{:S(2)}, u32[]{:S(2)}) %all-to-all-start) | async-done | bytes 184352 | tf_op jit(solution)/shard_map/all_to_all | solution.py:398
  32.7 0.0 copy-done.1
  32.7 0.9 %fold.1 = (bf16[8,40,80]{2,1,0:T(8,128)(2,1)}, bf16[32,1280]{1,0:T(8,128)(2,1)S(1)}) custom-call(bf16[16,72,80]{2,1,0:T(8,128)(2,1)S(1)} %all-to-all-done.arrived_ref, bf16[80,1280]{1,0:T(8,128)(2,1)S(1)} %copy-done.1), custom_call_target="tpu_custom_call" | custom-call | tf_op jit(solution)/shard_map/fold/pallas_call | solution.py:82
  33.6 4.3 %all-to-all-start.1 = ((bf16[8,40,80]{2,1,0:T(8,128)(2,1)}), bf16[8,40,80]{2,1,0:T(8,128)(2,1)S(1)}, u32[]{:S(2)}, u32[]{:S(2)}) async-start(bf16[8,40,80]{2,1,0:T(8,128)(2,1)} %get-tuple-element.10), calls=%async_computation.1 | async-start | bytes 163840 | tf_op jit(solution)/shard_map/all_to_all | solution.py:407
  37.9 0.0 copy-done.2
  37.9 0.0 copy-done.5
  38.0 0.0 copy-start
  38.0 0.0 copy-start.6
  38.0 0.4 attend.1.mine_ref
  38.4 2.4 %collective-permute-start.2 = (bf16[2,4,8,80]{3,2,1,0:T(8,128)(2,1)S(1)}, bf16[2,4,8,80]{3,2,1,0:T(8,128)(2,1)S(1)}, u32[]{:S(2)}, u32[]{:S(2)}) collective-permute-start(bf16[2,4,8,80]{3,2,1,0:T(8,128)(2,1)S(1)} %attend.1.mine_ref), channel_id=1, source_target_pairs={{0,1},{1,0},{2,3},{3,2},{4,5},{5,4},{6,7},{7,6},{8,9},{9,8},{10,11... | collective-permute-start | bytes 30728 | tf_op jit(solution)/shard_map/ppermute | solution.py:410
  40.8 0.8 collective-permute-done.2.other_ref
  41.6 2.0 %all-to-all-done.1 = bf16[8,40,80]{2,1,0:T(8,128)(2,1)S(1)} async-done(((bf16[8,40,80]{2,1,0:T(8,128)(2,1)}), bf16[8,40,80]{2,1,0:T(8,128)(2,1)S(1)}, u32[]{:S(2)}, u32[]{:S(2)}) %all-to-all-start.1) | async-done | bytes 51232 | tf_op jit(solution)/shard_map/all_to_all | solution.py:407
  43.7 0.0 copy-done
  43.7 1.0 %project.1 = bf16[32,16,320]{2,1,0:T(8,128)(2,1)} custom-call(bf16[2,4,8,80]{3,2,1,0:T(8,128)(2,1)S(1)} %attend.1.mine_ref, bf16[2,4,8,80]{3,2,1,0:T(8,128)(2,1)S(1)} %collective-permute-done.2.other_ref, bf16[320,80]{1,0:T(8,128)(2,1)S(1)} %bitcast.15, bf16[80,320]{1,0:T(8,128)(2,1)S(1)} %copy-done), custom_call_target="tpu_custom_call" | custom-call | tf_op jit(solution)/shard_map/project/pallas_call | solution.py:164
  44.6 4.2 %all-to-all-start.2 = ((bf16[16,2,16,320]{3,2,1,0:T(8,128)(2,1)}), bf16[16,2,16,320]{3,2,1,0:T(8,128)(2,1)}, u32[]{:S(2)}, u32[]{:S(2)}) async-start(bf16[16,2,16,320]{3,2,1,0:T(8,128)(2,1)} %bitcast.3.refs_0_), calls=%async_computation.2 | async-start | bytes 786432 | tf_op jit(solution)/shard_map/all_to_all | solution.py:418
  48.9 0.0 copy-done.6
  48.9 0.3 copy.15.refs_2_.time
  49.2 3.0 %copy.14.refs_1_.space = bf16[320,2880]{1,0:T(8,128)(2,1)S(1)} copy(bf16[320,2880]{0,1:T(8,128)(2,1)} %bitcast.17) | data formatting | bytes 3686400 | tf_op jit(solution)/shard_map/reshape | solution.py:403
  52.1 0.0 copy-start.3
  52.2 0.0 copy-start.4
  52.2 0.0 collective-permute-done.1.right_ref.right_in
  52.2 0.0 collective-permute-done.left_ref.left_in
  52.2 1.9 %edge_rows.1 = (bf16[4,320,128]{2,1,0:T(8,128)(2,1)}, bf16[4,320,128]{2,1,0:T(8,128)(2,1)}) custom-call(bf16[1,4,320,128]{3,2,1,0:T(8,128)(2,1)} %collective-permute-done.left_ref.left_in, bf16[2,4,320,128]{3,2,1,0:T(8,128)(2,1)S(1)} %bitcast.13, bf16[1,4,320,128]{3,2,1,0:T(8,128)(2,1)S(1)} %collective-permute-done.1.right_ref.right_in, ...), custom_call_target="tpu_custom_call" | custom-call | tf_op jit(solution)/shard_map/edge_rows/pallas_call | solution.py:196
  54.1 1.9 %collective-permute-start.3 = (bf16[4,320,128]{2,1,0:T(8,128)(2,1)}, bf16[4,320,128]{2,1,0:T(8,128)(2,1)}, u32[]{:S(2)}, u32[]{:S(2)}) collective-permute-start(bf16[4,320,128]{2,1,0:T(8,128)(2,1)} %get-tuple-element.11), channel_id=1, source_target_pairs={{0,1},{1,0},{2,3},{3,2},{4,5},{5,4},{6,7},{7,6},{8,9},{9,8},{10,11... | collective-permute-start | bytes 983048 | tf_op jit(solution)/shard_map/ppermute | solution.py:421
  56.0 3.7 %collective-permute-start.4 = (bf16[4,320,128]{2,1,0:T(8,128)(2,1)}, bf16[4,320,128]{2,1,0:T(8,128)(2,1)}, u32[]{:S(2)}, u32[]{:S(2)}) collective-permute-start(bf16[4,320,128]{2,1,0:T(8,128)(2,1)} %get-tuple-element.12), channel_id=1, source_target_pairs={{1,2},{3,4},{5,6},{7,8},{9,10},{11,12},{13,14},{15,16},{17,18},{19... | collective-permute-start | bytes 983048 | tf_op jit(solution)/shard_map/ppermute | solution.py:422
  59.7 7.1 %all-to-all-done.2.summed_ref = bf16[16,2,16,320]{3,2,1,0:T(8,128)(2,1)} async-done(((bf16[16,2,16,320]{3,2,1,0:T(8,128)(2,1)}), bf16[16,2,16,320]{3,2,1,0:T(8,128)(2,1)}, u32[]{:S(2)}, u32[]{:S(2)}) %all-to-all-start.2) | async-done | bytes 327712 | tf_op jit(solution)/shard_map/all_to_all | solution.py:418
  66.8 1.1 %total.1.up_own = bf16[2,16,320]{2,1,0:T(8,128)(2,1)S(1)} custom-call(bf16[16,2,16,320]{3,2,1,0:T(8,128)(2,1)} %all-to-all-done.2.summed_ref), custom_call_target="tpu_custom_call" | custom-call | tf_op jit(solution)/shard_map/total/pallas_call | solution.py:215
  67.8 1.9 %collective-permute-start.5 = (bf16[2,16,320]{2,1,0:T(8,128)(2,1)S(1)}, bf16[2,16,320]{2,1,0:T(8,128)(2,1)S(1)}, u32[]{:S(2)}, u32[]{:S(2)}) collective-permute-start(bf16[2,16,320]{2,1,0:T(8,128)(2,1)S(1)} %total.1.up_own), channel_id=1, source_target_pairs={{1,2},{3,4},{5,6},{7,8},{9,10},{11,12},{13,14},{15,16},{17,18},{19... | collective-permute-start | bytes 61448 | tf_op jit(solution)/shard_map/ppermute | solution.py:425
  69.8 0.0 collective-permute-done.3.pair_in
  69.8 0.0 collective-permute-done.4.next_in
  69.8 5.3 %collective-permute-done.5.up_next = bf16[2,16,320]{2,1,0:T(8,128)(2,1)S(1)} collective-permute-done((bf16[2,16,320]{2,1,0:T(8,128)(2,1)S(1)}, bf16[2,16,320]{2,1,0:T(8,128)(2,1)S(1)}, u32[]{:S(2)}, u32[]{:S(2)}) %collective-permute-start.5) | collective-permute-done | bytes 20512 | tf_op jit(solution)/shard_map/ppermute | solution.py:425
  75.1 0.0 copy-done.3
  75.1 0.0 copy-done.4
  75.1 8.4 %fine_stage.1 = bf16[2,320,4,128]{3,2,1,0:T(4,128)(2,1)} custom-call(bf16[2,4,320,128]{3,2,1,0:T(8,128)(2,1)S(1)} %bitcast.14, bf16[1,4,320,128]{3,2,1,0:T(8,128)(2,1)} %collective-permute-done.left_ref.left_in, bf16[1,4,320,128]{3,2,1,0:T(8,128)(2,1)S(1)} %collective-permute-done.1.right_ref.right_in, bf16[4,320,128]{2,1,0:T(8,128)(2,1)} %collective-permute-done.3.pair_in, ...), custom_call_target="tpu_custom_call" | custom-call | tf_op jit(solution)/shard_map/fine_stage/pallas_call | solution.py:364
Async XLA Ops:
  0.0 37.9 %copy-start.2 = (bf16[4,8,80]{2,1,0:T(8,128)(2,1)S(1)}, bf16[4,8,80]{2,1,0:T(8,128)(2,1)}, u32[]{:S(2)}) copy-start(bf16[4,8,80]{2,1,0:T(8,128)(2,1)} %coarse_ref.1) | copy-start | bytes 15364
  0.0 32.7 %copy-start.1 = (bf16[80,1280]{1,0:T(8,128)(2,1)S(1)}, bf16[80,1280]{1,0:T(8,128)(2,1)}, u32[]{:S(2)}) copy-start(bf16[80,1280]{1,0:T(8,128)(2,1)} %out_w_ref.1) | copy-start | bytes 614404
  0.0 37.9 %copy-start.5 = (bf16[3,1280,80]{1,2,0:T(8,128)(2,1)S(1)}, bf16[3,1280,80]{1,2,0:T(8,128)(2,1)}, u32[]{:S(2)}) copy-start(bf16[3,1280,80]{1,2,0:T(8,128)(2,1)} %param.11) | copy-start | bytes 1843204
  1.8 30.9 %all-to-all-start = ((bf16[16,72,80]{2,1,0:T(8,128)(2,1)}), bf16[16,72,80]{2,1,0:T(8,128)(2,1)S(1)}, u32[]{:S(2)}, u32[]{:S(2)}) async-start(bf16[16,72,80]{2,1,0:T(8,128)(2,1)} %pack.1), calls=%async_computation | async-start | bytes 589824 | tf_op jit(solution)/shard_map/all_to_all | solution.py:398
  18.7 33.4 %collective-permute-start.1 = (bf16[1,4,320,128]{3,2,1,0:T(8,128)(2,1)}, bf16[1,4,320,128]{3,2,1,0:T(8,128)(2,1)S(1)}, u32[]{:S(2)}, u32[]{:S(2)}) collective-permute-start(bf16[1,4,320,128]{3,2,1,0:T(8,128)(2,1)} %get-tuple-element.13), channel_id=1, source_target_pairs={{32,0},{64,32},{96,64},{128,96},{160,128},{192,160},{224,192},{256... | collective-permute-start | bytes 983048 | tf_op jit(solution)/shard_map/ppermute | solution.py:402
  20.0 32.2 %collective-permute-start = (bf16[1,4,320,128]{3,2,1,0:T(8,128)(2,1)}, bf16[1,4,320,128]{3,2,1,0:T(8,128)(2,1)}, u32[]{:S(2)}, u32[]{:S(2)}) collective-permute-start(bf16[1,4,320,128]{3,2,1,0:T(8,128)(2,1)} %get-tuple-element.14), channel_id=1, source_target_pairs={{0,32},{32,64},{64,96},{96,128},{128,160},{160,192},{192,224},{224... | collective-permute-start | bytes 983048 | tf_op jit(solution)/shard_map/ppermute | solution.py:401
  33.6 10.0 %all-to-all-start.1 = ((bf16[8,40,80]{2,1,0:T(8,128)(2,1)}), bf16[8,40,80]{2,1,0:T(8,128)(2,1)S(1)}, u32[]{:S(2)}, u32[]{:S(2)}) async-start(bf16[8,40,80]{2,1,0:T(8,128)(2,1)} %get-tuple-element.10), calls=%async_computation.1 | async-start | bytes 163840 | tf_op jit(solution)/shard_map/all_to_all | solution.py:407
  38.0 5.7 %copy-start = (bf16[80,320]{1,0:T(8,128)(2,1)S(1)}, bf16[80,320]{1,0:T(8,128)(2,1)}, u32[]{:S(2)}) copy-start(bf16[80,320]{1,0:T(8,128)(2,1)} %up_ref.1) | copy-start | bytes 153604
  38.0 10.9 %copy-start.6 = (bf16[3,320,320]{2,1,0:T(8,128)(2,1)S(1)}, bf16[3,320,320]{2,1,0:T(8,128)(2,1)}, u32[]{:S(2)}) copy-start(bf16[3,320,320]{2,1,0:T(8,128)(2,1)} %param.17) | copy-start | bytes 1843204
  38.4 3.2 %collective-permute-start.2 = (bf16[2,4,8,80]{3,2,1,0:T(8,128)(2,1)S(1)}, bf16[2,4,8,80]{3,2,1,0:T(8,128)(2,1)S(1)}, u32[]{:S(2)}, u32[]{:S(2)}) collective-permute-start(bf16[2,4,8,80]{3,2,1,0:T(8,128)(2,1)S(1)} %attend.1.mine_ref), channel_id=1, source_target_pairs={{0,1},{1,0},{2,3},{3,2},{4,5},{5,4},{6,7},{7,6},{8,9},{9,8},{10,11... | collective-permute-start | bytes 30728 | tf_op jit(solution)/shard_map/ppermute | solution.py:410
  44.6 22.1 %all-to-all-start.2 = ((bf16[16,2,16,320]{3,2,1,0:T(8,128)(2,1)}), bf16[16,2,16,320]{3,2,1,0:T(8,128)(2,1)}, u32[]{:S(2)}, u32[]{:S(2)}) async-start(bf16[16,2,16,320]{3,2,1,0:T(8,128)(2,1)} %bitcast.3.refs_0_), calls=%async_computation.2 | async-start | bytes 786432 | tf_op jit(solution)/shard_map/all_to_all | solution.py:418
  52.1 22.9 %copy-start.3 = (f32[320]{0:T(512)S(1)}, f32[320]{0:T(512)}, u32[]{:S(2)}) copy-start(f32[320]{0:T(512)} %one_in.1) | copy-start | bytes 3844
  52.2 22.9 %copy-start.4 = (f32[320]{0:T(512)S(1)}, f32[320]{0:T(512)}, u32[]{:S(2)}) copy-start(f32[320]{0:T(512)} %two_in.1) | copy-start | bytes 3844
  54.1 15.7 %collective-permute-start.3 = (bf16[4,320,128]{2,1,0:T(8,128)(2,1)}, bf16[4,320,128]{2,1,0:T(8,128)(2,1)}, u32[]{:S(2)}, u32[]{:S(2)}) collective-permute-start(bf16[4,320,128]{2,1,0:T(8,128)(2,1)} %get-tuple-element.11), channel_id=1, source_target_pairs={{0,1},{1,0},{2,3},{3,2},{4,5},{5,4},{6,7},{7,6},{8,9},{9,8},{10,11... | collective-permute-start | bytes 983048 | tf_op jit(solution)/shard_map/ppermute | solution.py:421
  56.0 13.8 %collective-permute-start.4 = (bf16[4,320,128]{2,1,0:T(8,128)(2,1)}, bf16[4,320,128]{2,1,0:T(8,128)(2,1)}, u32[]{:S(2)}, u32[]{:S(2)}) collective-permute-start(bf16[4,320,128]{2,1,0:T(8,128)(2,1)} %get-tuple-element.12), channel_id=1, source_target_pairs={{1,2},{3,4},{5,6},{7,8},{9,10},{11,12},{13,14},{15,16},{17,18},{19... | collective-permute-start | bytes 983048 | tf_op jit(solution)/shard_map/ppermute | solution.py:422
  67.8 7.3 %collective-permute-start.5 = (bf16[2,16,320]{2,1,0:T(8,128)(2,1)S(1)}, bf16[2,16,320]{2,1,0:T(8,128)(2,1)S(1)}, u32[]{:S(2)}, u32[]{:S(2)}) collective-permute-start(bf16[2,16,320]{2,1,0:T(8,128)(2,1)S(1)} %total.1.up_own), channel_id=1, source_target_pairs={{1,2},{3,4},{5,6},{7,8},{9,10},{11,12},{13,14},{15,16},{17,18},{19... | collective-permute-start | bytes 61448 | tf_op jit(solution)/shard_map/ppermute | solution.py:425

commit v6 on v5

--- a/solution.py
+++ b/solution.py
@@ -138,38 +138,31 @@
     )(whole, w_qkv_t, coarse)
 
 
-def project(mine, other, folded, w_up, wanted):
+def project(mine, folded, w_up, wanted):
     cf, cells, width = mine.shape[1:]
 
-    def body(mine_ref, other_ref, folded_ref, up_ref, out_ref):
-        even = lax.rem(lax.axis_index("row"), 2) == 0
-
-        def through(ref):
-            attn = ref[0].reshape(cf * cells, width)
-            inputs = ref[1].reshape(cf * cells, width)
-            partial = lax.dot_general(
-                attn, folded_ref[...], (((1,), (1,)), ((), ())), preferred_element_type=jnp.float32
-            )
-            return partial + jnp.dot(inputs, up_ref[...], preferred_element_type=jnp.float32)
-
-        own, far = through(mine_ref), through(other_ref)
-        first, second = jnp.where(even, own, far), jnp.where(even, far, own)
+    def body(mine_ref, folded_ref, up_ref, out_ref):
+        attn = mine_ref[0].reshape(cf * cells, width)
+        inputs = mine_ref[1].reshape(cf * cells, width)
+        partial = lax.dot_general(
+            attn, folded_ref[...], (((1,), (1,)), ((), ())), preferred_element_type=jnp.float32
+        )
+        partial += jnp.dot(inputs, up_ref[...], preferred_element_type=jnp.float32)
         for f in range(cf):
-            part = slice(cells * f, cells * (f + 1))
-            block = jnp.concatenate([first[part], second[part]], axis=0).astype(jnp.bfloat16)
+            block = partial[cells * f : cells * (f + 1)].astype(jnp.bfloat16)
             for place, source in enumerate(wanted):
                 if source == f:
                     out_ref[place] = block
 
     return pl.pallas_call(
         body,
-        out_shape=jax.ShapeDtypeStruct((len(wanted), 2 * cells, w_up.shape[1]), jnp.bfloat16),
-        in_specs=[VMEM] * 4,
+        out_shape=jax.ShapeDtypeStruct((len(wanted), cells, w_up.shape[1]), jnp.bfloat16),
+        in_specs=[VMEM] * 3,
         out_specs=VMEM,
         compiler_params=limit(2),
         cost_estimate=FREE,
         name="project",
-    )(mine, other, folded, w_up)
+    )(mine, folded, w_up)
 
 
 def edge_rows(left, own, right, earlier):
@@ -218,17 +211,17 @@
         in_specs=[VMEM],
         out_specs=VMEM,
         compiler_params=limit(2),
-        cost_estimate=FREE,
+        cost_estimate=pl.CostEstimate(flops=10000000000, bytes_accessed=0, transcendentals=0),
         name="total",
     )(summed)
 
 
 def fine_kernel(
-    own, left_in, right_in, pair_in, next_in, up_own, up_next, one_in, two_in, space, time,
+    own, left_in, right_in, pair_in, next_in, up_own, up_pair, up_near, up_far, one_in, two_in, space, time,
     out, left, right, pair, beyond, gains, stack, second, merged, mixed, turned, sems, out_sems,
 ):
     channels, width = own.shape[2:]
-    cells = up_own.shape[1]
+    cells = 2 * up_own.shape[1]
     row, frame_index = lax.axis_index("row"), lax.axis_index("frame")
     last_row, last_frame = lax.axis_size("row") - 1, lax.axis_size("frame") - 1
     even = lax.rem(row, 2) == 0
@@ -249,19 +242,29 @@
         gains[place] = jnp.broadcast_to(0.5 * gain[...].reshape(1, channels), (width, channels)).T
     gain_one, gain_two = gains.at[0], gains.at[1]
 
-    across = width // cells
-    column = lax.broadcasted_iota(jnp.int32, (cells, width), 1)
-    cell = lax.broadcasted_iota(jnp.int32, (cells, width), 0) * across
-    expand = ((column >= cell) & (column < cell + across)).astype(jnp.float32).astype(jnp.bfloat16)
+    def columns_of(odd):
+        cell = lax.broadcasted_iota(jnp.int32, (cells, width), 0) + odd * (cells // 2)
+        cell = jnp.where(cell >= cells, cell - cells, cell) * (width // cells)
+        column = lax.broadcasted_iota(jnp.int32, (cells, width), 1)
+        inside = (column >= cell) & (column < cell + width // cells)
+        return inside.astype(jnp.float32).astype(jnp.bfloat16)
+
     lane = lax.broadcasted_iota(jnp.int32, (channels, width), 1)
 
-    def spread(source):
-        by_slot = [
-            lax.dot_general(
-                source[slot], expand, (((0,), (0,)), ((), ())), preferred_element_type=jnp.float32
+    def spread(first, then, expand):
+        by_slot = []
+        for slot in range(2):
+            both = jnp.concatenate(
+                [first[slot].astype(jnp.float32), then[slot].astype(jnp.float32)], axis=0
             )
-            for slot in range(2)
-        ]
+            by_slot.append(
+                lax.dot_general(
+                    both.astype(jnp.bfloat16),
+                    expand,
+                    (((0,), (0,)), ((), ())),
+                    preferred_element_type=jnp.float32,
+                )
+            )
         middle = jnp.where(first_slot, by_slot[1], by_slot[0])
         return [by_slot[0], middle, middle, by_slot[1]]
 
@@ -286,7 +289,9 @@
         for place, part in enumerate((before, normed, after)):
             stack[half, position, pl.ds(place * channels, channels), lanes] = part
 
-    here, further = spread(up_own), spread(up_next)
+    odd = lax.rem(row, 2)
+    here = spread(up_own, up_pair, columns_of(odd))
+    further = spread(up_near, up_far, columns_of(1 - odd))
     held = (left.at[0], own.at[0], own.at[1], right.at[0])
 
     halves = ((1, 2), (0, 3))
@@ -357,14 +362,14 @@
         leave.wait()
 
 
-def fine_stage(own, left, right, pair, beyond, up_own, up_next, gain_one, gain_two, space, time):
+def fine_stage(own, left, right, pair, beyond, up_own, up_pair, up_near, up_far, gain_one, gain_two, space, time):
     channels, width = own.shape[2:]
     bf16 = jnp.bfloat16
     copied = (left, right, pair, beyond)
     return pl.pallas_call(
         fine_kernel,
         out_shape=jax.ShapeDtypeStruct((2, channels, 4, width), bf16),
-        in_specs=[VMEM] + [HBM] * 4 + [VMEM] * 6,
+        in_specs=[VMEM] + [HBM] * 4 + [VMEM] * 8,
         out_specs=HBM,
         scratch_shapes=[pltpu.VMEM(array.shape, array.dtype) for array in copied]
         + [
@@ -379,7 +384,7 @@
         ],
         compiler_params=limit(28),
         name="fine_stage",
-    )(own, left, right, pair, beyond, up_own, up_next, gain_one, gain_two, space, time)
+    )(own, left, right, pair, beyond, up_own, up_pair, up_near, up_far, gain_one, gain_two, space, time)
 
 
 def local(fine, coarse, w_qkv, w_out, w_up, gain_one, conv_space, gain_two, conv_time):
@@ -393,6 +398,7 @@
     partner = [(i, i ^ 1) for i in range(rows)]
     across = [(i, i + 1) for i in range(1, rows - 1, 2)]
     across += [(b, a) for a, b in across]
+    beyond = [(i, i + 2) for i in range(0, rows - 2, 2)] + [(i + 2, i) for i in range(1, rows - 2, 2)]
 
     message = pack(coarse, w_up, share, frames)
     arrived = lax.all_to_all(message, "frame", 0, 0, tiled=True)
@@ -400,31 +406,33 @@
     rows_first = jnp.swapaxes(fine, 1, 2)
     left = lax.ppermute(rows_first[1:], "frame", [(i, i + 1) for i in range(frames - 1)])
     right = lax.ppermute(rows_first[:1], "frame", [(i + 1, i) for i in range(frames - 1)])
-    space = jnp.transpose(conv_space, (3, 0, 1, 2)).reshape(fine_c, 9 * fine_c)
-    time = jnp.transpose(conv_time, (2, 0, 1)).reshape(fine_c, 3 * fine_c)
 
     copies, whole = fold(arrived, w_out, tokens, share)
     folded = lax.all_to_all(copies, "row", 0, 0, tiled=True, axis_index_groups=groups)
     folded = folded.reshape(fine_c, w_out.shape[0])
     mine = attend(whole, jnp.swapaxes(w_qkv, 1, 2), coarse)
-    other = lax.ppermute(mine, "row", partner)
 
     per = frames // cf
     wanted = []
     for f in range(frames):
         wanted.append(max(f - 1, 0) // per)
         wanted.append(min(f + 1, frames - 1) // per)
-    outgoing = project(mine, other, folded, w_up, wanted).reshape(frames, 2, 2 * cells, fine_c)
+    outgoing = project(mine, folded, w_up, wanted).reshape(frames, 2, cells, fine_c)
     summed = lax.all_to_all(outgoing, "frame", 0, 0, tiled=True)
 
+    conv_space, conv_time, _ = lax.optimization_barrier((conv_space, conv_time, outgoing))
+    space = jnp.transpose(conv_space, (3, 0, 1, 2)).reshape(fine_c, 9 * fine_c)
+    time = jnp.transpose(conv_time, (2, 0, 1)).reshape(fine_c, 3 * fine_c)
     to_pair, to_next = edge_rows(left, rows_first, right, (outgoing, space, time))
     from_pair = lax.ppermute(to_pair, "row", partner)
     from_next = lax.ppermute(to_next, "row", across)
 
     up_own = total(summed)
-    up_next = lax.ppermute(up_own, "row", across)
+    up_pair = lax.ppermute(up_own, "row", partner)
+    up_near = lax.ppermute(up_own, "row", across)
+    up_far = lax.ppermute(up_own, "row", beyond)
     return fine_stage(
-        rows_first, left, right, from_pair, from_next, up_own, up_next, gain_one, gain_two, space, time
+        rows_first, left, right, from_pair, from_next, up_own, up_pair, up_near, up_far, gain_one, gain_two, space, time
     )
 
 

time: 84.2 us -> 82.7 us (0.982)
  the two profiles are of different devices: /device:TPU:8 before, /device:TPU:5 now
where the time goes in v6:
time: 82.7 us; the launch traced here: 82 us
  starting transfers between devices  53.4 us (65%)
  Pallas kernels  15.2 us (18%)
  waiting for transfers between devices  7.83 us (9%)
  local copies, waits for them, and re-layouts  5.38 us (7%)
    all_to_all x1, starting transfers between devices, local(): arrived = lax.all_to_all(message, 'frame', 0, 0, tiled=True)  15.4 us
    pallas_call x1, Pallas kernels, fine_stage(): pl.pallas_call(fine_kernel, out_shape=jax.ShapeDtypeStruct((2, channels,...  8.39 us
    ppermute x1, starting transfers between devices, local(): up_near = lax.ppermute(up_own, 'row', across)  7.77 us
    all_to_all x1, starting transfers between devices, local(): lax.all_to_all(copies, 'row', 0, 0, tiled=True, axis_index_groups=groups)  6.62 us
    all_to_all x1, starting transfers between devices, local(): summed = lax.all_to_all(outgoing, 'frame', 0, 0, tiled=True)  6.57 us
    ppermute x1, starting transfers between devices, local(): lax.ppermute(rows_first[1:], 'frame', [(i, i + 1) for i in range(frames -...  4.72 us
    all_to_all x1, waiting for transfers between devices, local(): arrived = lax.all_to_all(message, 'frame', 0, 0, tiled=True)  4.03 us
    ppermute x1, starting transfers between devices, local(): from_next = lax.ppermute(to_next, 'row', across)  3.21 us
  transfers between devices with their start and end apart: 10, of which 4 were waited for; matrix products, arithmetic and copies ran while one was open for 7% of the time, Pallas kernels for 6%

profile of v6, /device:TPU:5, one launch (start us, length us, event | category | flops | bytes accessed | tf_op | source)
XLA Modules:
  0.0 82.0 jit_solution(9102536833098582362)
XLA Ops:
  0.0 0.0 copy-start.2
  0.0 0.0 copy-start.1
  0.0 0.0 copy-start.5
  0.0 1.8 %pack.1 = bf16[16,72,80]{2,1,0:T(8,128)(2,1)} custom-call(bf16[4,8,80]{2,1,0:T(8,128)(2,1)} %coarse_ref.1, bf16[80,320]{1,0:T(8,128)(2,1)} %up_ref.1), custom_call_target="tpu_custom_call" | custom-call | tf_op jit(solution)/shard_map/pack/pallas_call | solution.py:49
  1.8 15.4 %all-to-all-start = ((bf16[16,72,80]{2,1,0:T(8,128)(2,1)}), bf16[16,72,80]{2,1,0:T(8,128)(2,1)S(1)}, u32[]{:S(2)}, u32[]{:S(2)}) async-start(bf16[16,72,80]{2,1,0:T(8,128)(2,1)} %pack.1), calls=%async_computation | async-start | bytes 589824 | tf_op jit(solution)/shard_map/all_to_all | solution.py:404
  17.3 1.2 %copy.19 = bf16[2,320,4,128]{3,1,2,0:T(8,128)(2,1)S(1)} copy(bf16[2,320,4,128]{3,2,1,0:T(4,128)(2,1)} %param.9) | data formatting | bytes 1310720 | tf_op args[0]
  18.4 0.9 %fusion = (bf16[1,4,320,128]{3,2,1,0:T(8,128)(2,1)}, bf16[1,4,320,128]{3,2,1,0:T(8,128)(2,1)}) fusion(bf16[2,4,320,128]{3,2,1,0:T(8,128)(2,1)S(1)} %bitcast.12), kind=kLoop, calls=%fused_computation.1 | loop fusion | bytes 1310720 | tf_op jit(solution)/shard_map/slice | solution.py:408
  19.3 1.3 %collective-permute-start.1 = (bf16[1,4,320,128]{3,2,1,0:T(8,128)(2,1)}, bf16[1,4,320,128]{3,2,1,0:T(8,128)(2,1)S(1)}, u32[]{:S(2)}, u32[]{:S(2)}) collective-permute-start(bf16[1,4,320,128]{3,2,1,0:T(8,128)(2,1)} %get-tuple-element.17), channel_id=1, source_target_pairs={{32,0},{64,32},{96,64},{128,96},{160,128},{192,160},{224,192},{256... | collective-permute-start | bytes 983048 | tf_op jit(solution)/shard_map/ppermute | solution.py:408
  20.6 4.7 %collective-permute-start = (bf16[1,4,320,128]{3,2,1,0:T(8,128)(2,1)}, bf16[1,4,320,128]{3,2,1,0:T(8,128)(2,1)}, u32[]{:S(2)}, u32[]{:S(2)}) collective-permute-start(bf16[1,4,320,128]{3,2,1,0:T(8,128)(2,1)} %get-tuple-element.18), channel_id=1, source_target_pairs={{0,32},{32,64},{64,96},{96,128},{128,160},{160,192},{192,224},{224... | collective-permute-start | bytes 983048 | tf_op jit(solution)/shard_map/ppermute | solution.py:407
  25.3 4.0 %all-to-all-done.arrived_ref = bf16[16,72,80]{2,1,0:T(8,128)(2,1)S(1)} async-done(((bf16[16,72,80]{2,1,0:T(8,128)(2,1)}), bf16[16,72,80]{2,1,0:T(8,128)(2,1)S(1)}, u32[]{:S(2)}, u32[]{:S(2)}) %all-to-all-start) | async-done | bytes 184352 | tf_op jit(solution)/shard_map/all_to_all | solution.py:404
  29.4 0.0 copy-done.1
  29.4 0.9 %fold.1 = (bf16[8,40,80]{2,1,0:T(8,128)(2,1)}, bf16[32,1280]{1,0:T(8,128)(2,1)S(1)}) custom-call(bf16[16,72,80]{2,1,0:T(8,128)(2,1)S(1)} %all-to-all-done.arrived_ref, bf16[80,1280]{1,0:T(8,128)(2,1)S(1)} %copy-done.1), custom_call_target="tpu_custom_call" | custom-call | tf_op jit(solution)/shard_map/fold/pallas_call | solution.py:82
  30.3 6.6 %all-to-all-start.1 = ((bf16[8,40,80]{2,1,0:T(8,128)(2,1)}), bf16[8,40,80]{2,1,0:T(8,128)(2,1)S(1)}, u32[]{:S(2)}, u32[]{:S(2)}) async-start(bf16[8,40,80]{2,1,0:T(8,128)(2,1)} %get-tuple-element.12), calls=%async_computation.1 | async-start | bytes 163840 | tf_op jit(solution)/shard_map/all_to_all | solution.py:411
  36.9 0.0 copy-done.2
  36.9 0.0 copy-done.5
  36.9 0.0 copy-start
  36.9 0.0 copy-start.6
  36.9 0.4 attend.1.mine_ref
  37.4 2.2 %all-to-all-done.1 = bf16[8,40,80]{2,1,0:T(8,128)(2,1)S(1)} async-done(((bf16[8,40,80]{2,1,0:T(8,128)(2,1)}), bf16[8,40,80]{2,1,0:T(8,128)(2,1)S(1)}, u32[]{:S(2)}, u32[]{:S(2)}) %all-to-all-start.1) | async-done | bytes 51232 | tf_op jit(solution)/shard_map/all_to_all | solution.py:411
  39.6 0.0 copy-done
  39.6 0.9 %project.1 = bf16[32,8,320]{2,1,0:T(8,128)(2,1)} custom-call(bf16[2,4,8,80]{3,2,1,0:T(8,128)(2,1)S(1)} %attend.1.mine_ref, bf16[320,80]{1,0:T(8,128)(2,1)S(1)} %bitcast.15, bf16[80,320]{1,0:T(8,128)(2,1)S(1)} %copy-done), custom_call_target="tpu_custom_call" | custom-call | tf_op jit(solution)/shard_map/project/pallas_call | solution.py:157
  40.5 6.6 %all-to-all-start.2 = ((bf16[16,2,8,320]{3,2,1,0:T(8,128)(2,1)}), bf16[16,2,8,320]{3,2,1,0:T(8,128)(2,1)}, u32[]{:S(2)}, u32[]{:S(2)}) async-start(bf16[16,2,8,320]{3,2,1,0:T(8,128)(2,1)} %bitcast.3.refs_0_), calls=%async_computation.2 | async-start | bytes 393216 | tf_op jit(solution)/shard_map/all_to_all | solution.py:421
  47.1 0.0 copy-done.6
  47.1 0.3 copy.15.refs_2_.time
  47.4 3.0 %copy.14.refs_1_.space = bf16[320,2880]{1,0:T(8,128)(2,1)S(1)} copy(bf16[320,2880]{0,1:T(8,128)(2,1)} %bitcast.17) | data formatting | bytes 3686400 | tf_op jit(solution)/shard_map/reshape | solution.py:424
  50.3 0.0 collective-permute-done.1.right_ref.right_in
  50.4 0.0 collective-permute-done.left_ref.left_in
  50.4 1.9 %edge_rows.1 = (bf16[4,320,128]{2,1,0:T(8,128)(2,1)}, bf16[4,320,128]{2,1,0:T(8,128)(2,1)}) custom-call(bf16[1,4,320,128]{3,2,1,0:T(8,128)(2,1)} %collective-permute-done.left_ref.left_in, bf16[2,4,320,128]{3,2,1,0:T(8,128)(2,1)S(1)} %bitcast.13, bf16[1,4,320,128]{3,2,1,0:T(8,128)(2,1)S(1)} %collective-permute-done.1.right_ref.right_in, ...), custom_call_target="tpu_custom_call" | custom-call | tf_op jit(solution)/shard_map/edge_rows/pallas_call | solution.py:189
  52.2 2.8 %collective-permute-start.2 = (bf16[4,320,128]{2,1,0:T(8,128)(2,1)}, bf16[4,320,128]{2,1,0:T(8,128)(2,1)}, u32[]{:S(2)}, u32[]{:S(2)}) collective-permute-start(bf16[4,320,128]{2,1,0:T(8,128)(2,1)} %get-tuple-element.15), channel_id=1, source_target_pairs={{0,1},{1,0},{2,3},{3,2},{4,5},{5,4},{6,7},{7,6},{8,9},{9,8},{10,11... | collective-permute-start | bytes 983048 | tf_op jit(solution)/shard_map/ppermute | solution.py:427
  55.0 0.0 copy-start.3
  55.1 0.0 copy-start.4
  55.1 3.2 %collective-permute-start.3 = (bf16[4,320,128]{2,1,0:T(8,128)(2,1)}, bf16[4,320,128]{2,1,0:T(8,128)(2,1)}, u32[]{:S(2)}, u32[]{:S(2)}) collective-permute-start(bf16[4,320,128]{2,1,0:T(8,128)(2,1)} %get-tuple-element.16), channel_id=1, source_target_pairs={{1,2},{3,4},{5,6},{7,8},{9,10},{11,12},{13,14},{15,16},{17,18},{19... | collective-permute-start | bytes 983048 | tf_op jit(solution)/shard_map/ppermute | solution.py:428
  58.3 0.4 all-to-all-done.2.summed_ref
  58.7 1.0 %total.1.up_own = bf16[2,8,320]{2,1,0:T(8,128)(2,1)S(1)} custom-call(bf16[16,2,8,320]{3,2,1,0:T(8,128)(2,1)} %all-to-all-done.2.summed_ref), custom_call_target="tpu_custom_call" | custom-call | flops 10000000000 | tf_op jit(solution)/shard_map/total/pallas_call | solution.py:208
  59.7 3.0 %collective-permute-start.6 = (bf16[2,8,320]{2,1,0:T(8,128)(2,1)S(1)}, bf16[2,8,320]{2,1,0:T(8,128)(2,1)S(1)}, u32[]{:S(2)}, u32[]{:S(2)}) collective-permute-start(bf16[2,8,320]{2,1,0:T(8,128)(2,1)S(1)} %total.1.up_own), channel_id=1, source_target_pairs={{0,2},{2,4},{4,6},{6,8},{8,10},{10,12},{12,14},{14,16},{16,18},{18... | collective-permute-start | bytes 30728 | tf_op jit(solution)/shard_map/ppermute | solution.py:433
  62.7 7.8 %collective-permute-start.5 = (bf16[2,8,320]{2,1,0:T(8,128)(2,1)S(1)}, bf16[2,8,320]{2,1,0:T(8,128)(2,1)S(1)}, u32[]{:S(2)}, u32[]{:S(2)}) collective-permute-start(bf16[2,8,320]{2,1,0:T(8,128)(2,1)S(1)} %total.1.up_own), channel_id=1, source_target_pairs={{1,2},{3,4},{5,6},{7,8},{9,10},{11,12},{13,14},{15,16},{17,18},{19... | collective-permute-start | bytes 30728 | tf_op jit(solution)/shard_map/ppermute | solution.py:432
  70.5 1.9 %collective-permute-start.4 = (bf16[2,8,320]{2,1,0:T(8,128)(2,1)S(1)}, bf16[2,8,320]{2,1,0:T(8,128)(2,1)S(1)}, u32[]{:S(2)}, u32[]{:S(2)}) collective-permute-start(bf16[2,8,320]{2,1,0:T(8,128)(2,1)S(1)} %total.1.up_own), channel_id=1, source_target_pairs={{0,1},{1,0},{2,3},{3,2},{4,5},{5,4},{6,7},{7,6},{8,9},{9,8},{10,11... | collective-permute-start | bytes 30728 | tf_op jit(solution)/shard_map/ppermute | solution.py:431
  72.4 0.0 collective-permute-done.6.up_far
  72.4 0.0 collective-permute-done.5.up_near
  72.4 1.1 %collective-permute-done.4.up_pair = bf16[2,8,320]{2,1,0:T(8,128)(2,1)S(1)} collective-permute-done((bf16[2,8,320]{2,1,0:T(8,128)(2,1)S(1)}, bf16[2,8,320]{2,1,0:T(8,128)(2,1)S(1)}, u32[]{:S(2)}, u32[]{:S(2)}) %collective-permute-start.4) | collective-permute-done | bytes 10272 | tf_op jit(solution)/shard_map/ppermute | solution.py:431
  73.6 0.0 collective-permute-done.2.pair_in
  73.6 0.0 collective-permute-done.3.next_in
  73.6 0.0 copy-done.3
  73.6 0.0 copy-done.4
  73.6 8.4 %fine_stage.1 = bf16[2,320,4,128]{3,2,1,0:T(4,128)(2,1)} custom-call(bf16[2,4,320,128]{3,2,1,0:T(8,128)(2,1)S(1)} %bitcast.14, bf16[1,4,320,128]{3,2,1,0:T(8,128)(2,1)} %collective-permute-done.left_ref.left_in, bf16[1,4,320,128]{3,2,1,0:T(8,128)(2,1)S(1)} %collective-permute-done.1.right_ref.right_in, bf16[4,320,128]{2,1,0:T(8,128)(2,1)} %collective-permute-done.2.pair_in, ...), custom_call_target="tpu_custom_call" | custom-call | tf_op jit(solution)/shard_map/fine_stage/pallas_call | solution.py:369
Async XLA Ops:
  0.0 36.9 %copy-start.2 = (bf16[4,8,80]{2,1,0:T(8,128)(2,1)S(1)}, bf16[4,8,80]{2,1,0:T(8,128)(2,1)}, u32[]{:S(2)}) copy-start(bf16[4,8,80]{2,1,0:T(8,128)(2,1)} %coarse_ref.1) | copy-start | bytes 15364
  0.0 29.4 %copy-start.1 = (bf16[80,1280]{1,0:T(8,128)(2,1)S(1)}, bf16[80,1280]{1,0:T(8,128)(2,1)}, u32[]{:S(2)}) copy-start(bf16[80,1280]{1,0:T(8,128)(2,1)} %out_w_ref.1) | copy-start | bytes 614404
  0.0 36.9 %copy-start.5 = (bf16[3,1280,80]{1,2,0:T(8,128)(2,1)S(1)}, bf16[3,1280,80]{1,2,0:T(8,128)(2,1)}, u32[]{:S(2)}) copy-start(bf16[3,1280,80]{1,2,0:T(8,128)(2,1)} %param.11) | copy-start | bytes 1843204
  1.8 27.5 %all-to-all-start = ((bf16[16,72,80]{2,1,0:T(8,128)(2,1)}), bf16[16,72,80]{2,1,0:T(8,128)(2,1)S(1)}, u32[]{:S(2)}, u32[]{:S(2)}) async-start(bf16[16,72,80]{2,1,0:T(8,128)(2,1)} %pack.1), calls=%async_computation | async-start | bytes 589824 | tf_op jit(solution)/shard_map/all_to_all | solution.py:404
  19.3 31.0 %collective-permute-start.1 = (bf16[1,4,320,128]{3,2,1,0:T(8,128)(2,1)}, bf16[1,4,320,128]{3,2,1,0:T(8,128)(2,1)S(1)}, u32[]{:S(2)}, u32[]{:S(2)}) collective-permute-start(bf16[1,4,320,128]{3,2,1,0:T(8,128)(2,1)} %get-tuple-element.17), channel_id=1, source_target_pairs={{32,0},{64,32},{96,64},{128,96},{160,128},{192,160},{224,192},{256... | collective-permute-start | bytes 983048 | tf_op jit(solution)/shard_map/ppermute | solution.py:408
  20.6 29.7 %collective-permute-start = (bf16[1,4,320,128]{3,2,1,0:T(8,128)(2,1)}, bf16[1,4,320,128]{3,2,1,0:T(8,128)(2,1)}, u32[]{:S(2)}, u32[]{:S(2)}) collective-permute-start(bf16[1,4,320,128]{3,2,1,0:T(8,128)(2,1)} %get-tuple-element.18), channel_id=1, source_target_pairs={{0,32},{32,64},{64,96},{96,128},{128,160},{160,192},{192,224},{224... | collective-permute-start | bytes 983048 | tf_op jit(solution)/shard_map/ppermute | solution.py:407
  30.3 9.3 %all-to-all-start.1 = ((bf16[8,40,80]{2,1,0:T(8,128)(2,1)}), bf16[8,40,80]{2,1,0:T(8,128)(2,1)S(1)}, u32[]{:S(2)}, u32[]{:S(2)}) async-start(bf16[8,40,80]{2,1,0:T(8,128)(2,1)} %get-tuple-element.12), calls=%async_computation.1 | async-start | bytes 163840 | tf_op jit(solution)/shard_map/all_to_all | solution.py:411
  36.9 2.7 %copy-start = (bf16[80,320]{1,0:T(8,128)(2,1)S(1)}, bf16[80,320]{1,0:T(8,128)(2,1)}, u32[]{:S(2)}) copy-start(bf16[80,320]{1,0:T(8,128)(2,1)} %up_ref.1) | copy-start | bytes 153604
  36.9 10.1 %copy-start.6 = (bf16[3,320,320]{2,1,0:T(8,128)(2,1)S(1)}, bf16[3,320,320]{2,1,0:T(8,128)(2,1)}, u32[]{:S(2)}) copy-start(bf16[3,320,320]{2,1,0:T(8,128)(2,1)} %param.17) | copy-start | bytes 1843204
  40.5 18.2 %all-to-all-start.2 = ((bf16[16,2,8,320]{3,2,1,0:T(8,128)(2,1)}), bf16[16,2,8,320]{3,2,1,0:T(8,128)(2,1)}, u32[]{:S(2)}, u32[]{:S(2)}) async-start(bf16[16,2,8,320]{3,2,1,0:T(8,128)(2,1)} %bitcast.3.refs_0_), calls=%async_computation.2 | async-start | bytes 393216 | tf_op jit(solution)/shard_map/all_to_all | solution.py:421
  52.2 21.3 %collective-permute-start.2 = (bf16[4,320,128]{2,1,0:T(8,128)(2,1)}, bf16[4,320,128]{2,1,0:T(8,128)(2,1)}, u32[]{:S(2)}, u32[]{:S(2)}) collective-permute-start(bf16[4,320,128]{2,1,0:T(8,128)(2,1)} %get-tuple-element.15), channel_id=1, source_target_pairs={{0,1},{1,0},{2,3},{3,2},{4,5},{5,4},{6,7},{7,6},{8,9},{9,8},{10,11... | collective-permute-start | bytes 983048 | tf_op jit(solution)/shard_map/ppermute | solution.py:427
  55.0 18.5 %copy-start.3 = (f32[320]{0:T(512)S(1)}, f32[320]{0:T(512)}, u32[]{:S(2)}) copy-start(f32[320]{0:T(512)} %one_in.1) | copy-start | bytes 3844
  55.1 18.5 %copy-start.4 = (f32[320]{0:T(512)S(1)}, f32[320]{0:T(512)}, u32[]{:S(2)}) copy-start(f32[320]{0:T(512)} %two_in.1) | copy-start | bytes 3844
  55.1 18.5 %collective-permute-start.3 = (bf16[4,320,128]{2,1,0:T(8,128)(2,1)}, bf16[4,320,128]{2,1,0:T(8,128)(2,1)}, u32[]{:S(2)}, u32[]{:S(2)}) collective-permute-start(bf16[4,320,128]{2,1,0:T(8,128)(2,1)} %get-tuple-element.16), channel_id=1, source_target_pairs={{1,2},{3,4},{5,6},{7,8},{9,10},{11,12},{13,14},{15,16},{17,18},{19... | collective-permute-start | bytes 983048 | tf_op jit(solution)/shard_map/ppermute | solution.py:428
  59.7 12.8 %collective-permute-start.6 = (bf16[2,8,320]{2,1,0:T(8,128)(2,1)S(1)}, bf16[2,8,320]{2,1,0:T(8,128)(2,1)S(1)}, u32[]{:S(2)}, u32[]{:S(2)}) collective-permute-start(bf16[2,8,320]{2,1,0:T(8,128)(2,1)S(1)} %total.1.up_own), channel_id=1, source_target_pairs={{0,2},{2,4},{4,6},{6,8},{8,10},{10,12},{12,14},{14,16},{16,18},{18... | collective-permute-start | bytes 30728 | tf_op jit(solution)/shard_map/ppermute | solution.py:433
  62.7 9.7 %collective-permute-start.5 = (bf16[2,8,320]{2,1,0:T(8,128)(2,1)S(1)}, bf16[2,8,320]{2,1,0:T(8,128)(2,1)S(1)}, u32[]{:S(2)}, u32[]{:S(2)}) collective-permute-start(bf16[2,8,320]{2,1,0:T(8,128)(2,1)S(1)} %total.1.up_own), channel_id=1, source_target_pairs={{1,2},{3,4},{5,6},{7,8},{9,10},{11,12},{13,14},{15,16},{17,18},{19... | collective-permute-start | bytes 30728 | tf_op jit(solution)/shard_map/ppermute | solution.py:432
  70.5 3.1 %collective-permute-start.4 = (bf16[2,8,320]{2,1,0:T(8,128)(2,1)S(1)}, bf16[2,8,320]{2,1,0:T(8,128)(2,1)S(1)}, u32[]{:S(2)}, u32[]{:S(2)}) collective-permute-start(bf16[2,8,320]{2,1,0:T(8,128)(2,1)S(1)} %total.1.up_own), channel_id=1, source_target_pairs={{0,1},{1,0},{2,3},{3,2},{4,5},{5,4},{6,7},{7,6},{8,9},{9,8},{10,11... | collective-permute-start | bytes 30728 | tf_op jit(solution)/shard_map/ppermute | solution.py:431

commit v7 on v6

--- a/solution.py
+++ b/solution.py
@@ -138,10 +138,10 @@
     )(whole, w_qkv_t, coarse)
 
 
-def project(mine, folded, w_up, wanted):
+def project(mine, folded, w_up, earlier, wanted):
     cf, cells, width = mine.shape[1:]
 
-    def body(mine_ref, folded_ref, up_ref, out_ref):
+    def body(mine_ref, folded_ref, up_ref, _, out_ref):
         attn = mine_ref[0].reshape(cf * cells, width)
         inputs = mine_ref[1].reshape(cf * cells, width)
         partial = lax.dot_general(
@@ -157,21 +157,21 @@
     return pl.pallas_call(
         body,
         out_shape=jax.ShapeDtypeStruct((len(wanted), cells, w_up.shape[1]), jnp.bfloat16),
-        in_specs=[VMEM] * 3,
+        in_specs=[VMEM] * 3 + [ANY],
         out_specs=VMEM,
         compiler_params=limit(2),
         cost_estimate=FREE,
         name="project",
-    )(mine, folded, w_up)
-
-
-def edge_rows(left, own, right, earlier):
-    rows, channels, width = own.shape[1:]
-
-    def body(left_ref, own_ref, right_ref, *refs):
+    )(mine, folded, w_up, earlier)
+
+
+def edge_rows(left, one, two, right, earlier):
+    rows, channels, width = one.shape[1:]
+
+    def body(left_ref, one_ref, two_ref, right_ref, *refs):
         pair_ref, next_ref, sems = refs[-3:]
         odd = lax.rem(lax.axis_index("row"), 2)
-        frames = (left_ref.at[0], own_ref.at[0], own_ref.at[1], right_ref.at[0])
+        frames = (left_ref.at[0], one_ref.at[0], two_ref.at[0], right_ref.at[0])
         moves = []
         for place, frame in enumerate(frames):
             for side, (out, row) in enumerate(((pair_ref, 1 - odd), (next_ref, odd))):
@@ -189,13 +189,13 @@
     return pl.pallas_call(
         body,
         out_shape=(shape, shape),
-        in_specs=[ANY] * (3 + len(earlier)),
+        in_specs=[ANY] * (4 + len(earlier)),
         out_specs=(VMEM, VMEM),
         scratch_shapes=[pltpu.SemaphoreType.DMA((8,))],
         compiler_params=limit(2),
         cost_estimate=FREE,
         name="edge_rows",
-    )(left, own, right, *earlier)
+    )(left, one, two, right, *earlier)
 
 
 def total(summed):
@@ -217,10 +217,10 @@
 
 
 def fine_kernel(
-    own, left_in, right_in, pair_in, next_in, up_own, up_pair, up_near, up_far, one_in, two_in, space, time,
+    one, two, left_in, right_in, pair_in, next_in, up_own, up_pair, up_near, up_far, one_in, two_in, space, time,
     out, left, right, pair, beyond, gains, stack, second, merged, mixed, turned, sems, out_sems,
 ):
-    channels, width = own.shape[2:]
+    channels, width = one.shape[2:]
     cells = 2 * up_own.shape[1]
     row, frame_index = lax.axis_index("row"), lax.axis_index("frame")
     last_row, last_frame = lax.axis_size("row") - 1, lax.axis_size("frame") - 1
@@ -292,7 +292,7 @@
     odd = lax.rem(row, 2)
     here = spread(up_own, up_pair, columns_of(odd))
     further = spread(up_near, up_far, columns_of(1 - odd))
-    held = (left.at[0], own.at[0], own.at[1], right.at[0])
+    held = (left.at[0], one.at[0], two.at[0], right.at[0])
 
     halves = ((1, 2), (0, 3))
 
@@ -362,14 +362,14 @@
         leave.wait()
 
 
-def fine_stage(own, left, right, pair, beyond, up_own, up_pair, up_near, up_far, gain_one, gain_two, space, time):
-    channels, width = own.shape[2:]
+def fine_stage(one, two, left, right, pair, beyond, up_own, up_pair, up_near, up_far, gain_one, gain_two, space, time):
+    channels, width = one.shape[2:]
     bf16 = jnp.bfloat16
     copied = (left, right, pair, beyond)
     return pl.pallas_call(
         fine_kernel,
         out_shape=jax.ShapeDtypeStruct((2, channels, 4, width), bf16),
-        in_specs=[VMEM] + [HBM] * 4 + [VMEM] * 8,
+        in_specs=[VMEM] * 2 + [HBM] * 4 + [VMEM] * 8,
         out_specs=HBM,
         scratch_shapes=[pltpu.VMEM(array.shape, array.dtype) for array in copied]
         + [
@@ -384,7 +384,7 @@
         ],
         compiler_params=limit(28),
         name="fine_stage",
-    )(own, left, right, pair, beyond, up_own, up_pair, up_near, up_far, gain_one, gain_two, space, time)
+    )(one, two, left, right, pair, beyond, up_own, up_pair, up_near, up_far, gain_one, gain_two, space, time)
 
 
 def local(fine, coarse, w_qkv, w_out, w_up, gain_one, conv_space, gain_two, conv_time):
@@ -403,13 +403,15 @@
     message = pack(coarse, w_up, share, frames)
     arrived = lax.all_to_all(message, "frame", 0, 0, tiled=True)
 
-    rows_first = jnp.swapaxes(fine, 1, 2)
-    left = lax.ppermute(rows_first[1:], "frame", [(i, i + 1) for i in range(frames - 1)])
-    right = lax.ppermute(rows_first[:1], "frame", [(i + 1, i) for i in range(frames - 1)])
+    first, second = jnp.swapaxes(fine[:1], 1, 2), jnp.swapaxes(fine[1:], 1, 2)
+    left = lax.ppermute(second, "frame", [(i, i + 1) for i in range(frames - 1)])
+    right = lax.ppermute(first, "frame", [(i + 1, i) for i in range(frames - 1)])
 
     copies, whole = fold(arrived, w_out, tokens, share)
     folded = lax.all_to_all(copies, "row", 0, 0, tiled=True, axis_index_groups=groups)
     folded = folded.reshape(fine_c, w_out.shape[0])
+    conv_space, _ = lax.optimization_barrier((conv_space, copies))
+    space = jnp.transpose(conv_space, (3, 0, 1, 2)).reshape(fine_c, 9 * fine_c)
     mine = attend(whole, jnp.swapaxes(w_qkv, 1, 2), coarse)
 
     per = frames // cf
@@ -417,13 +419,12 @@
     for f in range(frames):
         wanted.append(max(f - 1, 0) // per)
         wanted.append(min(f + 1, frames - 1) // per)
-    outgoing = project(mine, folded, w_up, wanted).reshape(frames, 2, cells, fine_c)
+    outgoing = project(mine, folded, w_up, space, wanted).reshape(frames, 2, cells, fine_c)
     summed = lax.all_to_all(outgoing, "frame", 0, 0, tiled=True)
 
-    conv_space, conv_time, _ = lax.optimization_barrier((conv_space, conv_time, outgoing))
-    space = jnp.transpose(conv_space, (3, 0, 1, 2)).reshape(fine_c, 9 * fine_c)
+    conv_time, _ = lax.optimization_barrier((conv_time, outgoing))
     time = jnp.transpose(conv_time, (2, 0, 1)).reshape(fine_c, 3 * fine_c)
-    to_pair, to_next = edge_rows(left, rows_first, right, (outgoing, space, time))
+    to_pair, to_next = edge_rows(left, first, second, right, (outgoing, time))
     from_pair = lax.ppermute(to_pair, "row", partner)
     from_next = lax.ppermute(to_next, "row", across)
 
@@ -432,7 +433,7 @@
     up_near = lax.ppermute(up_own, "row", across)
     up_far = lax.ppermute(up_own, "row", beyond)
     return fine_stage(
-        rows_first, left, right, from_pair, from_next, up_own, up_pair, up_near, up_far, gain_one, gain_two, space, time
+        first, second, left, right, from_pair, from_next, up_own, up_pair, up_near, up_far, gain_one, gain_two, space, time
     )
 
 

time: 82.7 us -> 85.1 us (1.029)
  waiting for transfers between devices: 7.83 us -> 8.74 us
  starting transfers between devices: 53.4 us -> 54.3 us
    ppermute x1, starting transfers between devices: 7.77 us -> 10.6 us  [local(): up_near = lax.ppermute(up_own, 'row', across)]
    all_to_all x1, waiting for transfers between devices: 0.41 us -> 2.92 us  [local(): summed = lax.all_to_all(outgoing, 'frame', 0, 0, tiled=True)]
    all_to_all x1, waiting for transfers between devices: 2.25 us -> 0.01 us  [local(): lax.all_to_all(copies, 'row', 0, 0, tiled=True, axis_index_groups=groups)]
    unnamed x15 -> x14, local copies, waits for them, and re-layouts: 1.21 us -> 0.12 us
    reshape x1, local copies, waits for them, and re-layouts: 0.28 us -> 1.37 us  [local(): time = jnp.transpose(conv_time, (2, 0, 1)).reshape(fine_c, 3 * fine_c)]
  transfers between devices with their start and end apart: 10 -> 10, of which waited for: 4 -> 3; matrix products, arithmetic and copies ran while one was open for 7% -> 7% of each run, Pallas kernels for 6% -> 6%
where the time goes in v7:
time: 85.1 us; the launch traced here: 84.3 us
  starting transfers between devices  54.3 us (64%)
  Pallas kernels  15.2 us (18%)
  waiting for transfers between devices  8.74 us (10%)
  local copies, waits for them, and re-layouts  5.79 us (7%)
    all_to_all x1, starting transfers between devices, local(): arrived = lax.all_to_all(message, 'frame', 0, 0, tiled=True)  15.4 us
    ppermute x1, starting transfers between devices, local(): up_near = lax.ppermute(up_own, 'row', across)  10.6 us
    pallas_call x1, Pallas kernels, fine_stage(): pl.pallas_call(fine_kernel, out_shape=jax.ShapeDtypeStruct((2, channels,...  8.4 us
    all_to_all x1, starting transfers between devices, local(): lax.all_to_all(copies, 'row', 0, 0, tiled=True, axis_index_groups=groups)  6.57 us
    all_to_all x1, starting transfers between devices, local(): summed = lax.all_to_all(outgoing, 'frame', 0, 0, tiled=True)  5.84 us
    ppermute x1, starting transfers between devices, local(): lax.ppermute(second, 'frame', [(i, i + 1) for i in range(frames - 1)])  4.73 us
    all_to_all x1, waiting for transfers between devices, local(): arrived = lax.all_to_all(message, 'frame', 0, 0, tiled=True)  4.68 us
    reshape x1, local copies, waits for them, and re-layouts, local(): space = jnp.transpose(conv_space, (3, 0, 1, 2)).reshape(fine_c, 9 * fine_c)  2.99 us
  transfers between devices with their start and end apart: 10, of which 3 were waited for; matrix products, arithmetic and copies ran while one was open for 7% of the time, Pallas kernels for 6%

profile of v7, /device:TPU:5, one launch (start us, length us, event | category | flops | bytes accessed | tf_op | source)
XLA Modules:
  0.0 84.3 jit_solution(15927519138683083547)
XLA Ops:
  0.0 0.0 copy-start.2
  0.0 0.0 copy-start.1
  0.0 0.0 copy-start.5
  0.0 1.8 %pack.1 = bf16[16,72,80]{2,1,0:T(8,128)(2,1)} custom-call(bf16[4,8,80]{2,1,0:T(8,128)(2,1)} %coarse_ref.1, bf16[80,320]{1,0:T(8,128)(2,1)} %up_ref.1), custom_call_target="tpu_custom_call" | custom-call | tf_op jit(solution)/shard_map/pack/pallas_call | solution.py:49
  1.8 15.4 %all-to-all-start = ((bf16[16,72,80]{2,1,0:T(8,128)(2,1)}), bf16[16,72,80]{2,1,0:T(8,128)(2,1)S(1)}, u32[]{:S(2)}, u32[]{:S(2)}) async-start(bf16[16,72,80]{2,1,0:T(8,128)(2,1)} %pack.1), calls=%async_computation | async-start | bytes 589824 | tf_op jit(solution)/shard_map/all_to_all | solution.py:404
  17.2 1.3 %fusion = (bf16[1,320,4,128]{3,2,1,0:T(4,128)(2,1)S(1)}, bf16[1,320,4,128]{3,2,1,0:T(4,128)(2,1)S(1)}) fusion(bf16[2,320,4,128]{3,2,1,0:T(4,128)(2,1)} %param.9), kind=kLoop, calls=%fused_computation.2 | loop fusion | bytes 1310720 | tf_op jit(solution)/shard_map/slice | solution.py:406
  18.6 1.3 %collective-permute-start.1 = (bf16[1,4,320,128]{3,2,1,0:T(8,128)(2,1)S(1)}, bf16[1,4,320,128]{3,2,1,0:T(8,128)(2,1)S(1)}, u32[]{:S(2)}, u32[]{:S(2)}) collective-permute-start(bf16[1,4,320,128]{3,2,1,0:T(8,128)(2,1)S(1)} %bitcast.15), channel_id=1, source_target_pairs={{32,0},{64,32},{96,64},{128,96},{160,128},{192,160},{224,192},{256... | collective-permute-start | bytes 983048 | tf_op jit(solution)/shard_map/ppermute | solution.py:408
  20.0 4.7 %collective-permute-start = (bf16[1,4,320,128]{3,2,1,0:T(8,128)(2,1)S(1)}, bf16[1,4,320,128]{3,2,1,0:T(8,128)(2,1)}, u32[]{:S(2)}, u32[]{:S(2)}) collective-permute-start(bf16[1,4,320,128]{3,2,1,0:T(8,128)(2,1)S(1)} %bitcast.18), channel_id=1, source_target_pairs={{0,32},{32,64},{64,96},{96,128},{128,160},{160,192},{192,224},{224... | collective-permute-start | bytes 983048 | tf_op jit(solution)/shard_map/ppermute | solution.py:407
  24.7 4.7 %all-to-all-done.arrived_ref = bf16[16,72,80]{2,1,0:T(8,128)(2,1)S(1)} async-done(((bf16[16,72,80]{2,1,0:T(8,128)(2,1)}), bf16[16,72,80]{2,1,0:T(8,128)(2,1)S(1)}, u32[]{:S(2)}, u32[]{:S(2)}) %all-to-all-start) | async-done | bytes 184352 | tf_op jit(solution)/shard_map/all_to_all | solution.py:404
  29.4 0.0 copy-done.1
  29.4 0.9 %fold.1 = (bf16[8,40,80]{2,1,0:T(8,128)(2,1)}, bf16[32,1280]{1,0:T(8,128)(2,1)S(1)}) custom-call(bf16[16,72,80]{2,1,0:T(8,128)(2,1)S(1)} %all-to-all-done.arrived_ref, bf16[80,1280]{1,0:T(8,128)(2,1)S(1)} %copy-done.1), custom_call_target="tpu_custom_call" | custom-call | tf_op jit(solution)/shard_map/fold/pallas_call | solution.py:82
  30.3 6.6 %all-to-all-start.1 = ((bf16[8,40,80]{2,1,0:T(8,128)(2,1)}), bf16[8,40,80]{2,1,0:T(8,128)(2,1)S(1)}, u32[]{:S(2)}, u32[]{:S(2)}) async-start(bf16[8,40,80]{2,1,0:T(8,128)(2,1)} %get-tuple-element.12), calls=%async_computation.1 | async-start | bytes 163840 | tf_op jit(solution)/shard_map/all_to_all | solution.py:411
  36.9 0.0 copy-done.2
  36.9 0.0 copy-done.5
  36.9 0.4 attend.1.mine_ref
  37.3 0.0 copy-start
  37.3 3.0 %copy.16._.space = bf16[320,2880]{1,0:T(8,128)(2,1)S(1)} copy(bf16[320,2880]{0,1:T(8,128)(2,1)} %bitcast.23) | data formatting | bytes 3686400 | tf_op jit(solution)/shard_map/reshape | solution.py:414
  40.3 0.0 all-to-all-done.1
  40.3 0.0 copy-done
  40.3 0.9 %project.1 = bf16[32,8,320]{2,1,0:T(8,128)(2,1)} custom-call(bf16[2,4,8,80]{3,2,1,0:T(8,128)(2,1)S(1)} %attend.1.mine_ref, bf16[320,80]{1,0:T(8,128)(2,1)S(1)} %bitcast.21, bf16[80,320]{1,0:T(8,128)(2,1)S(1)} %copy-done, bf16[320,2880]{1,0:T(8,128)(2,1)S(1)} %copy.16._.space), custom_call_target="tpu_custom_call" | custom-call | tf_op jit(solution)/shard_map/project/pallas_call | solution.py:157
  41.2 5.8 %all-to-all-start.2 = ((bf16[16,2,8,320]{3,2,1,0:T(8,128)(2,1)}), bf16[16,2,8,320]{3,2,1,0:T(8,128)(2,1)}, u32[]{:S(2)}, u32[]{:S(2)}) async-start(bf16[16,2,8,320]{3,2,1,0:T(8,128)(2,1)} %bitcast.6.refs_0_), calls=%async_computation.2 | async-start | bytes 393216 | tf_op jit(solution)/shard_map/all_to_all | solution.py:423
  47.0 1.4 %copy.17.refs_1_.time = bf16[320,960]{1,0:T(8,128)(2,1)S(1)} copy(bf16[320,960]{0,1:T(8,128)(2,1)} %bitcast.24) | data formatting | bytes 1228800 | tf_op jit(solution)/shard_map/reshape | solution.py:426
  48.4 0.0 collective-permute-done.1.right_ref.right_in
  48.4 0.0 collective-permute-done.left_ref.left_in
  48.4 1.9 %edge_rows.1 = (bf16[4,320,128]{2,1,0:T(8,128)(2,1)}, bf16[4,320,128]{2,1,0:T(8,128)(2,1)}) custom-call(bf16[1,4,320,128]{3,2,1,0:T(8,128)(2,1)} %collective-permute-done.left_ref.left_in, bf16[1,4,320,128]{3,2,1,0:T(8,128)(2,1)S(1)} %bitcast.16, bf16[1,4,320,128]{3,2,1,0:T(8,128)(2,1)S(1)} %bitcast.19, ...), custom_call_target="tpu_custom_call" | custom-call | tf_op jit(solution)/shard_map/edge_rows/pallas_call | solution.py:189
  50.3 2.6 %collective-permute-start.2 = (bf16[4,320,128]{2,1,0:T(8,128)(2,1)}, bf16[4,320,128]{2,1,0:T(8,128)(2,1)}, u32[]{:S(2)}, u32[]{:S(2)}) collective-permute-start(bf16[4,320,128]{2,1,0:T(8,128)(2,1)} %get-tuple-element.15), channel_id=1, source_target_pairs={{0,1},{1,0},{2,3},{3,2},{4,5},{5,4},{6,7},{7,6},{8,9},{9,8},{10,11... | collective-permute-start | bytes 983048 | tf_op jit(solution)/shard_map/ppermute | solution.py:428
  52.9 0.0 copy-start.3
  52.9 0.0 copy-start.4
  52.9 2.9 %collective-permute-start.3 = (bf16[4,320,128]{2,1,0:T(8,128)(2,1)}, bf16[4,320,128]{2,1,0:T(8,128)(2,1)}, u32[]{:S(2)}, u32[]{:S(2)}) collective-permute-start(bf16[4,320,128]{2,1,0:T(8,128)(2,1)} %get-tuple-element.16), channel_id=1, source_target_pairs={{1,2},{3,4},{5,6},{7,8},{9,10},{11,12},{13,14},{15,16},{17,18},{19... | collective-permute-start | bytes 983048 | tf_op jit(solution)/shard_map/ppermute | solution.py:429
  55.8 2.9 %all-to-all-done.2.summed_ref = bf16[16,2,8,320]{3,2,1,0:T(8,128)(2,1)} async-done(((bf16[16,2,8,320]{3,2,1,0:T(8,128)(2,1)}), bf16[16,2,8,320]{3,2,1,0:T(8,128)(2,1)}, u32[]{:S(2)}, u32[]{:S(2)}) %all-to-all-start.2) | async-done | bytes 163872 | tf_op jit(solution)/shard_map/all_to_all | solution.py:423
  58.7 1.0 %total.1.up_own = bf16[2,8,320]{2,1,0:T(8,128)(2,1)S(1)} custom-call(bf16[16,2,8,320]{3,2,1,0:T(8,128)(2,1)} %all-to-all-done.2.summed_ref), custom_call_target="tpu_custom_call" | custom-call | flops 10000000000 | tf_op jit(solution)/shard_map/total/pallas_call | solution.py:208
  59.7 2.6 %collective-permute-start.6 = (bf16[2,8,320]{2,1,0:T(8,128)(2,1)S(1)}, bf16[2,8,320]{2,1,0:T(8,128)(2,1)S(1)}, u32[]{:S(2)}, u32[]{:S(2)}) collective-permute-start(bf16[2,8,320]{2,1,0:T(8,128)(2,1)S(1)} %total.1.up_own), channel_id=1, source_target_pairs={{0,2},{2,4},{4,6},{6,8},{8,10},{10,12},{12,14},{14,16},{16,18},{18... | collective-permute-start | bytes 30728 | tf_op jit(solution)/shard_map/ppermute | solution.py:434
  62.2 10.6 %collective-permute-start.5 = (bf16[2,8,320]{2,1,0:T(8,128)(2,1)S(1)}, bf16[2,8,320]{2,1,0:T(8,128)(2,1)S(1)}, u32[]{:S(2)}, u32[]{:S(2)}) collective-permute-start(bf16[2,8,320]{2,1,0:T(8,128)(2,1)S(1)} %total.1.up_own), channel_id=1, source_target_pairs={{1,2},{3,4},{5,6},{7,8},{9,10},{11,12},{13,14},{15,16},{17,18},{19... | collective-permute-start | bytes 30728 | tf_op jit(solution)/shard_map/ppermute | solution.py:433
  72.8 1.9 %collective-permute-start.4 = (bf16[2,8,320]{2,1,0:T(8,128)(2,1)S(1)}, bf16[2,8,320]{2,1,0:T(8,128)(2,1)S(1)}, u32[]{:S(2)}, u32[]{:S(2)}) collective-permute-start(bf16[2,8,320]{2,1,0:T(8,128)(2,1)S(1)} %total.1.up_own), channel_id=1, source_target_pairs={{0,1},{1,0},{2,3},{3,2},{4,5},{5,4},{6,7},{7,6},{8,9},{9,8},{10,11... | collective-permute-start | bytes 30728 | tf_op jit(solution)/shard_map/ppermute | solution.py:432
  74.7 0.0 collective-permute-done.6.up_far
  74.7 0.0 collective-permute-done.5.up_near
  74.7 1.1 %collective-permute-done.4.up_pair = bf16[2,8,320]{2,1,0:T(8,128)(2,1)S(1)} collective-permute-done((bf16[2,8,320]{2,1,0:T(8,128)(2,1)S(1)}, bf16[2,8,320]{2,1,0:T(8,128)(2,1)S(1)}, u32[]{:S(2)}, u32[]{:S(2)}) %collective-permute-start.4) | collective-permute-done | bytes 10272 | tf_op jit(solution)/shard_map/ppermute | solution.py:432
  75.9 0.0 collective-permute-done.2.pair_in
  75.9 0.0 collective-permute-done.3.next_in
  75.9 0.0 copy-done.3
  75.9 0.0 copy-done.4
  75.9 8.4 %fine_stage.1 = bf16[2,320,4,128]{3,2,1,0:T(4,128)(2,1)} custom-call(bf16[1,4,320,128]{3,2,1,0:T(8,128)(2,1)S(1)} %bitcast.17, bf16[1,4,320,128]{3,2,1,0:T(8,128)(2,1)S(1)} %bitcast.20, bf16[1,4,320,128]{3,2,1,0:T(8,128)(2,1)} %collective-permute-done.left_ref.left_in, bf16[1,4,320,128]{3,2,1,0:T(8,128)(2,1)S(1)} %collective-permute-done.1.right_ref.right_in, ...), custom_call_target="tpu_custom_call" | custom-call | tf_op jit(solution)/shard_map/fine_stage/pallas_call | solution.py:369
  (2 shorter events, 0.1 us)
Async XLA Ops:
  0.0 36.9 %copy-start.2 = (bf16[4,8,80]{2,1,0:T(8,128)(2,1)S(1)}, bf16[4,8,80]{2,1,0:T(8,128)(2,1)}, u32[]{:S(2)}) copy-start(bf16[4,8,80]{2,1,0:T(8,128)(2,1)} %coarse_ref.1) | copy-start | bytes 15364
  0.0 29.4 %copy-start.1 = (bf16[80,1280]{1,0:T(8,128)(2,1)S(1)}, bf16[80,1280]{1,0:T(8,128)(2,1)}, u32[]{:S(2)}) copy-start(bf16[80,1280]{1,0:T(8,128)(2,1)} %out_w_ref.1) | copy-start | bytes 614404
  0.0 36.9 %copy-start.5 = (bf16[3,1280,80]{1,2,0:T(8,128)(2,1)S(1)}, bf16[3,1280,80]{1,2,0:T(8,128)(2,1)}, u32[]{:S(2)}) copy-start(bf16[3,1280,80]{1,2,0:T(8,128)(2,1)} %param.11) | copy-start | bytes 1843204
  1.8 27.5 %all-to-all-start = ((bf16[16,72,80]{2,1,0:T(8,128)(2,1)}), bf16[16,72,80]{2,1,0:T(8,128)(2,1)S(1)}, u32[]{:S(2)}, u32[]{:S(2)}) async-start(bf16[16,72,80]{2,1,0:T(8,128)(2,1)} %pack.1), calls=%async_computation | async-start | bytes 589824 | tf_op jit(solution)/shard_map/all_to_all | solution.py:404
  18.6 29.8 %collective-permute-start.1 = (bf16[1,4,320,128]{3,2,1,0:T(8,128)(2,1)S(1)}, bf16[1,4,320,128]{3,2,1,0:T(8,128)(2,1)S(1)}, u32[]{:S(2)}, u32[]{:S(2)}) collective-permute-start(bf16[1,4,320,128]{3,2,1,0:T(8,128)(2,1)S(1)} %bitcast.15), channel_id=1, source_target_pairs={{32,0},{64,32},{96,64},{128,96},{160,128},{192,160},{224,192},{256... | collective-permute-start | bytes 983048 | tf_op jit(solution)/shard_map/ppermute | solution.py:408
  20.0 28.5 %collective-permute-start = (bf16[1,4,320,128]{3,2,1,0:T(8,128)(2,1)S(1)}, bf16[1,4,320,128]{3,2,1,0:T(8,128)(2,1)}, u32[]{:S(2)}, u32[]{:S(2)}) collective-permute-start(bf16[1,4,320,128]{3,2,1,0:T(8,128)(2,1)S(1)} %bitcast.18), channel_id=1, source_target_pairs={{0,32},{32,64},{64,96},{96,128},{128,160},{160,192},{192,224},{224... | collective-permute-start | bytes 983048 | tf_op jit(solution)/shard_map/ppermute | solution.py:407
  30.3 10.0 %all-to-all-start.1 = ((bf16[8,40,80]{2,1,0:T(8,128)(2,1)}), bf16[8,40,80]{2,1,0:T(8,128)(2,1)S(1)}, u32[]{:S(2)}, u32[]{:S(2)}) async-start(bf16[8,40,80]{2,1,0:T(8,128)(2,1)} %get-tuple-element.12), calls=%async_computation.1 | async-start | bytes 163840 | tf_op jit(solution)/shard_map/all_to_all | solution.py:411
  37.3 3.0 %copy-start = (bf16[80,320]{1,0:T(8,128)(2,1)S(1)}, bf16[80,320]{1,0:T(8,128)(2,1)}, u32[]{:S(2)}) copy-start(bf16[80,320]{1,0:T(8,128)(2,1)} %up_ref.1) | copy-start | bytes 153604
  41.2 17.5 %all-to-all-start.2 = ((bf16[16,2,8,320]{3,2,1,0:T(8,128)(2,1)}), bf16[16,2,8,320]{3,2,1,0:T(8,128)(2,1)}, u32[]{:S(2)}, u32[]{:S(2)}) async-start(bf16[16,2,8,320]{3,2,1,0:T(8,128)(2,1)} %bitcast.6.refs_0_), calls=%async_computation.2 | async-start | bytes 393216 | tf_op jit(solution)/shard_map/all_to_all | solution.py:423
  50.3 25.6 %collective-permute-start.2 = (bf16[4,320,128]{2,1,0:T(8,128)(2,1)}, bf16[4,320,128]{2,1,0:T(8,128)(2,1)}, u32[]{:S(2)}, u32[]{:S(2)}) collective-permute-start(bf16[4,320,128]{2,1,0:T(8,128)(2,1)} %get-tuple-element.15), channel_id=1, source_target_pairs={{0,1},{1,0},{2,3},{3,2},{4,5},{5,4},{6,7},{7,6},{8,9},{9,8},{10,11... | collective-permute-start | bytes 983048 | tf_op jit(solution)/shard_map/ppermute | solution.py:428
  52.9 23.0 %copy-start.3 = (f32[320]{0:T(512)S(1)}, f32[320]{0:T(512)}, u32[]{:S(2)}) copy-start(f32[320]{0:T(512)} %one_in.1) | copy-start | bytes 3844
  52.9 23.0 %copy-start.4 = (f32[320]{0:T(512)S(1)}, f32[320]{0:T(512)}, u32[]{:S(2)}) copy-start(f32[320]{0:T(512)} %two_in.1) | copy-start | bytes 3844
  52.9 23.0 %collective-permute-start.3 = (bf16[4,320,128]{2,1,0:T(8,128)(2,1)}, bf16[4,320,128]{2,1,0:T(8,128)(2,1)}, u32[]{:S(2)}, u32[]{:S(2)}) collective-permute-start(bf16[4,320,128]{2,1,0:T(8,128)(2,1)} %get-tuple-element.16), channel_id=1, source_target_pairs={{1,2},{3,4},{5,6},{7,8},{9,10},{11,12},{13,14},{15,16},{17,18},{19... | collective-permute-start | bytes 983048 | tf_op jit(solution)/shard_map/ppermute | solution.py:429
  59.7 15.1 %collective-permute-start.6 = (bf16[2,8,320]{2,1,0:T(8,128)(2,1)S(1)}, bf16[2,8,320]{2,1,0:T(8,128)(2,1)S(1)}, u32[]{:S(2)}, u32[]{:S(2)}) collective-permute-start(bf16[2,8,320]{2,1,0:T(8,128)(2,1)S(1)} %total.1.up_own), channel_id=1, source_target_pairs={{0,2},{2,4},{4,6},{6,8},{8,10},{10,12},{12,14},{14,16},{16,18},{18... | collective-permute-start | bytes 30728 | tf_op jit(solution)/shard_map/ppermute | solution.py:434
  62.2 12.5 %collective-permute-start.5 = (bf16[2,8,320]{2,1,0:T(8,128)(2,1)S(1)}, bf16[2,8,320]{2,1,0:T(8,128)(2,1)S(1)}, u32[]{:S(2)}, u32[]{:S(2)}) collective-permute-start(bf16[2,8,320]{2,1,0:T(8,128)(2,1)S(1)} %total.1.up_own), channel_id=1, source_target_pairs={{1,2},{3,4},{5,6},{7,8},{9,10},{11,12},{13,14},{15,16},{17,18},{19... | collective-permute-start | bytes 30728 | tf_op jit(solution)/shard_map/ppermute | solution.py:433
  72.8 3.1 %collective-permute-start.4 = (bf16[2,8,320]{2,1,0:T(8,128)(2,1)S(1)}, bf16[2,8,320]{2,1,0:T(8,128)(2,1)S(1)}, u32[]{:S(2)}, u32[]{:S(2)}) collective-permute-start(bf16[2,8,320]{2,1,0:T(8,128)(2,1)S(1)} %total.1.up_own), channel_id=1, source_target_pairs={{0,1},{1,0},{2,3},{3,2},{4,5},{5,4},{6,7},{7,6},{8,9},{9,8},{10,11... | collective-permute-start | bytes 30728 | tf_op jit(solution)/shard_map/ppermute | solution.py:432

commit v8 on v7

--- a/solution.py
+++ b/solution.py
@@ -225,11 +225,14 @@
     row, frame_index = lax.axis_index("row"), lax.axis_index("frame")
     last_row, last_frame = lax.axis_size("row") - 1, lax.axis_size("frame") - 1
     even = lax.rem(row, 2) == 0
-    first_slot = lax.rem(frame_index, 4) == 0
     valid_above = (row > 0).astype(jnp.float32)
     valid_below = (row < last_row).astype(jnp.float32)
-    valid_before = (frame_index > 0).astype(jnp.float32)
-    valid_after = (frame_index < last_frame).astype(jnp.float32)
+    valid_beyond = jnp.logical_and(frame_index > 0, frame_index < last_frame).astype(jnp.float32)
+    in_time = lax.rem(frame_index, 2) == 1
+
+    def time_of(frame):
+        return jnp.where(in_time, frame, 3 - frame)
+
 
     moves, leaving = [], []
     halo = ((left_in, left), (right_in, right), (pair_in, pair), (next_in, beyond))
@@ -265,8 +268,7 @@
                     preferred_element_type=jnp.float32,
                 )
             )
-        middle = jnp.where(first_slot, by_slot[1], by_slot[0])
-        return [by_slot[0], middle, middle, by_slot[1]]
+        return [by_slot[0]] * 3 + [by_slot[1]]
 
     def norm(values, gain, scale):
         square = jnp.sum(values * values, axis=0, keepdims=True) * (1.0 / channels)
@@ -279,7 +281,7 @@
     def keep(frame, position, pixels, added, scale):
         total = (pixels.astype(jnp.float32) + added).astype(jnp.bfloat16)
         if frame in (1, 2) and 1 <= position <= 4:
-            merged[frame - 1, position - 1] = total
+            merged[time_of(frame) - 1, position - 1] = total
         normed = norm(total.astype(jnp.float32), gain_one, scale)
         normed = normed.astype(jnp.bfloat16)
         before = jnp.where(lane == 0, jnp.zeros_like(normed), pltpu.roll(normed, 1, 1))
@@ -316,11 +318,10 @@
     def second_norm(half, row_out, spatial):
         for side in range(2):
             frame = halves[half][side]
-            scale = (valid_before, None, None, valid_after)[frame]
+            scale = (None, None, None, valid_beyond)[frame]
             normed = norm(spatial[:, side * width : (side + 1) * width], gain_two, scale)
-            second[row_out // 2, frame, :, pl.ds(width * (row_out % 2), width)] = normed.astype(
-                jnp.bfloat16
-            )
+            lanes = pl.ds(width * (row_out % 2), width)
+            second[row_out // 2, time_of(frame), :, lanes] = normed.astype(jnp.bfloat16)
 
     for move in moves:
         move.wait()
@@ -403,9 +404,13 @@
     message = pack(coarse, w_up, share, frames)
     arrived = lax.all_to_all(message, "frame", 0, 0, tiled=True)
 
-    first, second = jnp.swapaxes(fine[:1], 1, 2), jnp.swapaxes(fine[1:], 1, 2)
-    left = lax.ppermute(second, "frame", [(i, i + 1) for i in range(frames - 1)])
-    right = lax.ppermute(first, "frame", [(i + 1, i) for i in range(frames - 1)])
+    odd_frame = lax.axis_index("frame") % 2
+    near_one = jnp.swapaxes(lax.dynamic_slice_in_dim(fine, 1 - odd_frame, 1, 0), 1, 2)
+    near_two = jnp.swapaxes(lax.dynamic_slice_in_dim(fine, odd_frame, 1, 0), 1, 2)
+    second_pairs = [(i, i + 1) for i in range(1, frames - 1, 2)]
+    second_pairs += [(b, a) for a, b in second_pairs]
+    beyond_one = lax.ppermute(near_one, "frame", [(i, i ^ 1) for i in range(frames)])
+    beyond_two = lax.ppermute(near_two, "frame", second_pairs)
 
     copies, whole = fold(arrived, w_out, tokens, share)
     folded = lax.all_to_all(copies, "row", 0, 0, tiled=True, axis_index_groups=groups)
@@ -417,14 +422,14 @@
     per = frames // cf
     wanted = []
     for f in range(frames):
-        wanted.append(max(f - 1, 0) // per)
-        wanted.append(min(f + 1, frames - 1) // per)
+        wanted.append(f // per)
+        wanted.append(min(max(f + 2 * (f % 2) - 1, 0), frames - 1) // per)
     outgoing = project(mine, folded, w_up, space, wanted).reshape(frames, 2, cells, fine_c)
     summed = lax.all_to_all(outgoing, "frame", 0, 0, tiled=True)
 
     conv_time, _ = lax.optimization_barrier((conv_time, outgoing))
     time = jnp.transpose(conv_time, (2, 0, 1)).reshape(fine_c, 3 * fine_c)
-    to_pair, to_next = edge_rows(left, first, second, right, (outgoing, time))
+    to_pair, to_next = edge_rows(beyond_one, near_one, near_two, beyond_two, (outgoing, time))
     from_pair = lax.ppermute(to_pair, "row", partner)
     from_next = lax.ppermute(to_next, "row", across)
 
@@ -433,7 +438,7 @@
     up_near = lax.ppermute(up_own, "row", across)
     up_far = lax.ppermute(up_own, "row", beyond)
     return fine_stage(
-        first, second, left, right, from_pair, from_next, up_own, up_pair, up_near, up_far, gain_one, gain_two, space, time
+        near_one, near_two, beyond_one, beyond_two, from_pair, from_next, up_own, up_pair, up_near, up_far, gain_one, gain_two, space, time
     )
 
 

time: 85.1 us -> 82.6 us (0.971)
  starting transfers between devices: 54.3 us -> 50.2 us
  Pallas kernels: 15.2 us -> 16.1 us
    ppermute x1, starting transfers between devices: 10.6 us -> 7.63 us  [local(): up_near = lax.ppermute(up_own, 'row', across)]
    ppermute x2, starting transfers between devices: 6.02 us -> 4.65 us  [the longest x1 3.25 us: local(): lax.ppermute(near_one, 'frame', [(i, i ^ 1) for i in range(frames)])]
    all_to_all x1, waiting for transfers between devices: 4.68 us -> 6.04 us  [local(): arrived = lax.all_to_all(message, 'frame', 0, 0, tiled=True)]
    dynamic_slice x0 -> x1, local copies, waits for them, and re-layouts: none -> 1.3 us  [local(): lax.dynamic_slice_in_dim(fine, odd_frame, 1, 0)]
    slice x1 -> x0, local copies, waits for them, and re-layouts: 1.3 us -> none  [local(): first, second = (jnp.swapaxes(fine[:1], 1, 2), jnp.swapaxes(fine[1:], 1, 2))]
  transfers between devices with their start and end apart: 10 -> 10, of which waited for: 3 -> 3; matrix products, arithmetic and copies ran while one was open for 7% -> 7% of each run, Pallas kernels for 6% -> 7%
where the time goes in v8:
time: 82.6 us; the launch traced here: 81.8 us
  starting transfers between devices  50.2 us (61%)
  Pallas kernels  16.1 us (19%)
  waiting for transfers between devices  9.47 us (11%)
  local copies, waits for them, and re-layouts  5.79 us (7%)
    all_to_all x1, starting transfers between devices, local(): arrived = lax.all_to_all(message, 'frame', 0, 0, tiled=True)  15.4 us
    pallas_call x1, Pallas kernels, fine_stage(): pl.pallas_call(fine_kernel, out_shape=jax.ShapeDtypeStruct((2, channels,...  8.67 us
    ppermute x1, starting transfers between devices, local(): up_near = lax.ppermute(up_own, 'row', across)  7.63 us
    all_to_all x1, starting transfers between devices, local(): lax.all_to_all(copies, 'row', 0, 0, tiled=True, axis_index_groups=groups)  6.56 us
    all_to_all x1, waiting for transfers between devices, local(): arrived = lax.all_to_all(message, 'frame', 0, 0, tiled=True)  6.04 us
    all_to_all x1, starting transfers between devices, local(): summed = lax.all_to_all(outgoing, 'frame', 0, 0, tiled=True)  6.02 us
    ppermute x1, starting transfers between devices, local(): lax.ppermute(near_one, 'frame', [(i, i ^ 1) for i in range(frames)])  3.25 us
    reshape x1, local copies, waits for them, and re-layouts, local(): space = jnp.transpose(conv_space, (3, 0, 1, 2)).reshape(fine_c, 9 * fine_c)  2.99 us
  transfers between devices with their start and end apart: 10, of which 3 were waited for; matrix products, arithmetic and copies ran while one was open for 7% of the time, Pallas kernels for 7%

profile of v8, /device:TPU:5, one launch (start us, length us, event | category | flops | bytes accessed | tf_op | source)
XLA Modules:
  0.0 81.8 jit_solution(12589313851090364561)
XLA Ops:
  0.0 0.0 copy-start.2
  0.0 0.0 copy-start.1
  0.0 0.0 copy-start.5
  0.0 1.8 %pack.1 = bf16[16,72,80]{2,1,0:T(8,128)(2,1)} custom-call(bf16[4,8,80]{2,1,0:T(8,128)(2,1)} %coarse_ref.1, bf16[80,320]{1,0:T(8,128)(2,1)} %up_ref.1), custom_call_target="tpu_custom_call" | custom-call | tf_op jit(solution)/shard_map/pack/pallas_call | solution.py:49
  1.8 15.4 %all-to-all-start = ((bf16[16,72,80]{2,1,0:T(8,128)(2,1)}), bf16[16,72,80]{2,1,0:T(8,128)(2,1)S(1)}, u32[]{:S(2)}, u32[]{:S(2)}) async-start(bf16[16,72,80]{2,1,0:T(8,128)(2,1)} %pack.1), calls=%async_computation | async-start | bytes 589824 | tf_op jit(solution)/shard_map/all_to_all | solution.py:405
  17.3 1.3 %constant_dynamic-slice_fusion = (bf16[1,320,4,128]{3,2,1,0:T(4,128)(2,1)S(1)}, bf16[1,320,4,128]{3,2,1,0:T(4,128)(2,1)S(1)}) fusion(bf16[2,320,4,128]{3,2,1,0:T(4,128)(2,1)} %param.9, s32[]{:T(128)S(6)} %select_n.15, s32[]{:T(128)S(6)} %select_n.14), kind=kLoop, calls=%fused_computation.2 | loop fusion | bytes 1310728 | tf_op jit(solution)/shard_map/dynamic_slice | solution.py:409
  18.6 3.2 %collective-permute-start = (bf16[1,4,320,128]{3,2,1,0:T(8,128)(2,1)S(1)}, bf16[1,4,320,128]{3,2,1,0:T(8,128)(2,1)S(1)}, u32[]{:S(2)}, u32[]{:S(2)}) collective-permute-start(bf16[1,4,320,128]{3,2,1,0:T(8,128)(2,1)S(1)} %bitcast.15), channel_id=1, source_target_pairs={{0,32},{32,0},{64,96},{96,64},{128,160},{160,128},{192,224},{224,1... | collective-permute-start | bytes 983048 | tf_op jit(solution)/shard_map/ppermute | solution.py:412
  21.9 1.4 %collective-permute-start.1 = (bf16[1,4,320,128]{3,2,1,0:T(8,128)(2,1)S(1)}, bf16[1,4,320,128]{3,2,1,0:T(8,128)(2,1)}, u32[]{:S(2)}, u32[]{:S(2)}) collective-permute-start(bf16[1,4,320,128]{3,2,1,0:T(8,128)(2,1)S(1)} %bitcast.18), channel_id=1, source_target_pairs={{32,64},{96,128},{160,192},{224,256},{288,320},{352,384},{416,448}... | collective-permute-start | bytes 983048 | tf_op jit(solution)/shard_map/ppermute | solution.py:413
  23.3 6.0 %all-to-all-done.arrived_ref = bf16[16,72,80]{2,1,0:T(8,128)(2,1)S(1)} async-done(((bf16[16,72,80]{2,1,0:T(8,128)(2,1)}), bf16[16,72,80]{2,1,0:T(8,128)(2,1)S(1)}, u32[]{:S(2)}, u32[]{:S(2)}) %all-to-all-start) | async-done | bytes 184352 | tf_op jit(solution)/shard_map/all_to_all | solution.py:405
  29.4 0.0 copy-done.1
  29.4 0.9 %fold.1 = (bf16[8,40,80]{2,1,0:T(8,128)(2,1)}, bf16[32,1280]{1,0:T(8,128)(2,1)S(1)}) custom-call(bf16[16,72,80]{2,1,0:T(8,128)(2,1)S(1)} %all-to-all-done.arrived_ref, bf16[80,1280]{1,0:T(8,128)(2,1)S(1)} %copy-done.1), custom_call_target="tpu_custom_call" | custom-call | tf_op jit(solution)/shard_map/fold/pallas_call | solution.py:82
  30.3 6.6 %all-to-all-start.1 = ((bf16[8,40,80]{2,1,0:T(8,128)(2,1)}), bf16[8,40,80]{2,1,0:T(8,128)(2,1)S(1)}, u32[]{:S(2)}, u32[]{:S(2)}) async-start(bf16[8,40,80]{2,1,0:T(8,128)(2,1)} %get-tuple-element.12), calls=%async_computation.1 | async-start | bytes 163840 | tf_op jit(solution)/shard_map/all_to_all | solution.py:416
  36.9 0.0 copy-done.2
  36.9 0.0 copy-done.5
  36.9 0.4 attend.1.mine_ref
  37.3 0.0 copy-start
  37.3 3.0 %copy.16._.space = bf16[320,2880]{1,0:T(8,128)(2,1)S(1)} copy(bf16[320,2880]{0,1:T(8,128)(2,1)} %bitcast.23) | data formatting | bytes 3686400 | tf_op jit(solution)/shard_map/reshape | solution.py:419
  40.3 0.0 all-to-all-done.1
  40.3 0.0 copy-done
  40.3 0.9 %project.1 = bf16[32,8,320]{2,1,0:T(8,128)(2,1)} custom-call(bf16[2,4,8,80]{3,2,1,0:T(8,128)(2,1)S(1)} %attend.1.mine_ref, bf16[320,80]{1,0:T(8,128)(2,1)S(1)} %bitcast.21, bf16[80,320]{1,0:T(8,128)(2,1)S(1)} %copy-done, bf16[320,2880]{1,0:T(8,128)(2,1)S(1)} %copy.16._.space), custom_call_target="tpu_custom_call" | custom-call | tf_op jit(solution)/shard_map/project/pallas_call | solution.py:157
  41.2 6.0 %all-to-all-start.2 = ((bf16[16,2,8,320]{3,2,1,0:T(8,128)(2,1)}), bf16[16,2,8,320]{3,2,1,0:T(8,128)(2,1)}, u32[]{:S(2)}, u32[]{:S(2)}) async-start(bf16[16,2,8,320]{3,2,1,0:T(8,128)(2,1)} %bitcast.6.refs_0_), calls=%async_computation.2 | async-start | bytes 393216 | tf_op jit(solution)/shard_map/all_to_all | solution.py:428
  47.2 1.4 %copy.17.refs_1_.time = bf16[320,960]{1,0:T(8,128)(2,1)S(1)} copy(bf16[320,960]{0,1:T(8,128)(2,1)} %bitcast.24) | data formatting | bytes 1228800 | tf_op jit(solution)/shard_map/reshape | solution.py:431
  48.6 0.0 collective-permute-done.left_ref.left_in
  48.6 0.0 collective-permute-done.1.right_ref.right_in
  48.6 2.5 %edge_rows.1 = (bf16[4,320,128]{2,1,0:T(8,128)(2,1)}, bf16[4,320,128]{2,1,0:T(8,128)(2,1)}) custom-call(bf16[1,4,320,128]{3,2,1,0:T(8,128)(2,1)S(1)} %collective-permute-done.left_ref.left_in, bf16[1,4,320,128]{3,2,1,0:T(8,128)(2,1)S(1)} %bitcast.16, bf16[1,4,320,128]{3,2,1,0:T(8,128)(2,1)S(1)} %bitcast.19, ...), custom_call_target="tpu_custom_call" | custom-call | tf_op jit(solution)/shard_map/edge_rows/pallas_call | solution.py:189
  51.1 2.5 %collective-permute-start.2 = (bf16[4,320,128]{2,1,0:T(8,128)(2,1)}, bf16[4,320,128]{2,1,0:T(8,128)(2,1)}, u32[]{:S(2)}, u32[]{:S(2)}) collective-permute-start(bf16[4,320,128]{2,1,0:T(8,128)(2,1)} %get-tuple-element.15), channel_id=1, source_target_pairs={{0,1},{1,0},{2,3},{3,2},{4,5},{5,4},{6,7},{7,6},{8,9},{9,8},{10,11... | collective-permute-start | bytes 983048 | tf_op jit(solution)/shard_map/ppermute | solution.py:433
  53.7 0.0 copy-start.3
  53.7 0.0 copy-start.4
  53.7 2.9 %collective-permute-start.3 = (bf16[4,320,128]{2,1,0:T(8,128)(2,1)}, bf16[4,320,128]{2,1,0:T(8,128)(2,1)}, u32[]{:S(2)}, u32[]{:S(2)}) collective-permute-start(bf16[4,320,128]{2,1,0:T(8,128)(2,1)} %get-tuple-element.16), channel_id=1, source_target_pairs={{1,2},{3,4},{5,6},{7,8},{9,10},{11,12},{13,14},{15,16},{17,18},{19... | collective-permute-start | bytes 983048 | tf_op jit(solution)/shard_map/ppermute | solution.py:434
  56.6 2.3 %all-to-all-done.2.summed_ref = bf16[16,2,8,320]{3,2,1,0:T(8,128)(2,1)} async-done(((bf16[16,2,8,320]{3,2,1,0:T(8,128)(2,1)}), bf16[16,2,8,320]{3,2,1,0:T(8,128)(2,1)}, u32[]{:S(2)}, u32[]{:S(2)}) %all-to-all-start.2) | async-done | bytes 163872 | tf_op jit(solution)/shard_map/all_to_all | solution.py:428
  58.9 1.0 %total.1.up_own = bf16[2,8,320]{2,1,0:T(8,128)(2,1)S(1)} custom-call(bf16[16,2,8,320]{3,2,1,0:T(8,128)(2,1)} %all-to-all-done.2.summed_ref), custom_call_target="tpu_custom_call" | custom-call | flops 10000000000 | tf_op jit(solution)/shard_map/total/pallas_call | solution.py:208
  59.8 2.6 %collective-permute-start.6 = (bf16[2,8,320]{2,1,0:T(8,128)(2,1)S(1)}, bf16[2,8,320]{2,1,0:T(8,128)(2,1)S(1)}, u32[]{:S(2)}, u32[]{:S(2)}) collective-permute-start(bf16[2,8,320]{2,1,0:T(8,128)(2,1)S(1)} %total.1.up_own), channel_id=1, source_target_pairs={{0,2},{2,4},{4,6},{6,8},{8,10},{10,12},{12,14},{14,16},{16,18},{18... | collective-permute-start | bytes 30728 | tf_op jit(solution)/shard_map/ppermute | solution.py:439
  62.4 7.6 %collective-permute-start.5 = (bf16[2,8,320]{2,1,0:T(8,128)(2,1)S(1)}, bf16[2,8,320]{2,1,0:T(8,128)(2,1)S(1)}, u32[]{:S(2)}, u32[]{:S(2)}) collective-permute-start(bf16[2,8,320]{2,1,0:T(8,128)(2,1)S(1)} %total.1.up_own), channel_id=1, source_target_pairs={{1,2},{3,4},{5,6},{7,8},{9,10},{11,12},{13,14},{15,16},{17,18},{19... | collective-permute-start | bytes 30728 | tf_op jit(solution)/shard_map/ppermute | solution.py:438
  70.1 1.9 %collective-permute-start.4 = (bf16[2,8,320]{2,1,0:T(8,128)(2,1)S(1)}, bf16[2,8,320]{2,1,0:T(8,128)(2,1)S(1)}, u32[]{:S(2)}, u32[]{:S(2)}) collective-permute-start(bf16[2,8,320]{2,1,0:T(8,128)(2,1)S(1)} %total.1.up_own), channel_id=1, source_target_pairs={{0,1},{1,0},{2,3},{3,2},{4,5},{5,4},{6,7},{7,6},{8,9},{9,8},{10,11... | collective-permute-start | bytes 30728 | tf_op jit(solution)/shard_map/ppermute | solution.py:437
  72.0 0.0 collective-permute-done.6.up_far
  72.0 0.0 collective-permute-done.5.up_near
  72.0 1.1 %collective-permute-done.4.up_pair = bf16[2,8,320]{2,1,0:T(8,128)(2,1)S(1)} collective-permute-done((bf16[2,8,320]{2,1,0:T(8,128)(2,1)S(1)}, bf16[2,8,320]{2,1,0:T(8,128)(2,1)S(1)}, u32[]{:S(2)}, u32[]{:S(2)}) %collective-permute-start.4) | collective-permute-done | bytes 10272 | tf_op jit(solution)/shard_map/ppermute | solution.py:437
  73.1 0.0 collective-permute-done.2.pair_in
  73.1 0.0 collective-permute-done.3.next_in
  73.1 0.0 copy-done.3
  73.1 0.0 copy-done.4
  73.1 8.7 %fine_stage.1 = bf16[2,320,4,128]{3,2,1,0:T(4,128)(2,1)} custom-call(bf16[1,4,320,128]{3,2,1,0:T(8,128)(2,1)S(1)} %bitcast.17, bf16[1,4,320,128]{3,2,1,0:T(8,128)(2,1)S(1)} %bitcast.20, bf16[1,4,320,128]{3,2,1,0:T(8,128)(2,1)S(1)} %collective-permute-done.left_ref.left_in, bf16[1,4,320,128]{3,2,1,0:T(8,128)(2,1)} %collective-permute-done.1.right_ref.right_in, ...), custom_call_target="tpu_custom_call" | custom-call | tf_op jit(solution)/shard_map/fine_stage/pallas_call | solution.py:370
  (2 shorter events, 0.1 us)
Async XLA Ops:
  0.0 36.9 %copy-start.2 = (bf16[4,8,80]{2,1,0:T(8,128)(2,1)S(1)}, bf16[4,8,80]{2,1,0:T(8,128)(2,1)}, u32[]{:S(2)}) copy-start(bf16[4,8,80]{2,1,0:T(8,128)(2,1)} %coarse_ref.1) | copy-start | bytes 15364
  0.0 29.4 %copy-start.1 = (bf16[80,1280]{1,0:T(8,128)(2,1)S(1)}, bf16[80,1280]{1,0:T(8,128)(2,1)}, u32[]{:S(2)}) copy-start(bf16[80,1280]{1,0:T(8,128)(2,1)} %out_w_ref.1) | copy-start | bytes 614404
  0.0 36.9 %copy-start.5 = (bf16[3,1280,80]{1,2,0:T(8,128)(2,1)S(1)}, bf16[3,1280,80]{1,2,0:T(8,128)(2,1)}, u32[]{:S(2)}) copy-start(bf16[3,1280,80]{1,2,0:T(8,128)(2,1)} %param.11) | copy-start | bytes 1843204
  1.8 27.6 %all-to-all-start = ((bf16[16,72,80]{2,1,0:T(8,128)(2,1)}), bf16[16,72,80]{2,1,0:T(8,128)(2,1)S(1)}, u32[]{:S(2)}, u32[]{:S(2)}) async-start(bf16[16,72,80]{2,1,0:T(8,128)(2,1)} %pack.1), calls=%async_computation | async-start | bytes 589824 | tf_op jit(solution)/shard_map/all_to_all | solution.py:405
  18.6 30.0 %collective-permute-start = (bf16[1,4,320,128]{3,2,1,0:T(8,128)(2,1)S(1)}, bf16[1,4,320,128]{3,2,1,0:T(8,128)(2,1)S(1)}, u32[]{:S(2)}, u32[]{:S(2)}) collective-permute-start(bf16[1,4,320,128]{3,2,1,0:T(8,128)(2,1)S(1)} %bitcast.15), channel_id=1, source_target_pairs={{0,32},{32,0},{64,96},{96,64},{128,160},{160,128},{192,224},{224,1... | collective-permute-start | bytes 983048 | tf_op jit(solution)/shard_map/ppermute | solution.py:412
  21.9 26.7 %collective-permute-start.1 = (bf16[1,4,320,128]{3,2,1,0:T(8,128)(2,1)S(1)}, bf16[1,4,320,128]{3,2,1,0:T(8,128)(2,1)}, u32[]{:S(2)}, u32[]{:S(2)}) collective-permute-start(bf16[1,4,320,128]{3,2,1,0:T(8,128)(2,1)S(1)} %bitcast.18), channel_id=1, source_target_pairs={{32,64},{96,128},{160,192},{224,256},{288,320},{352,384},{416,448}... | collective-permute-start | bytes 983048 | tf_op jit(solution)/shard_map/ppermute | solution.py:413
  30.3 10.0 %all-to-all-start.1 = ((bf16[8,40,80]{2,1,0:T(8,128)(2,1)}), bf16[8,40,80]{2,1,0:T(8,128)(2,1)S(1)}, u32[]{:S(2)}, u32[]{:S(2)}) async-start(bf16[8,40,80]{2,1,0:T(8,128)(2,1)} %get-tuple-element.12), calls=%async_computation.1 | async-start | bytes 163840 | tf_op jit(solution)/shard_map/all_to_all | solution.py:416
  37.3 3.0 %copy-start = (bf16[80,320]{1,0:T(8,128)(2,1)S(1)}, bf16[80,320]{1,0:T(8,128)(2,1)}, u32[]{:S(2)}) copy-start(bf16[80,320]{1,0:T(8,128)(2,1)} %up_ref.1) | copy-start | bytes 153604
  41.2 17.7 %all-to-all-start.2 = ((bf16[16,2,8,320]{3,2,1,0:T(8,128)(2,1)}), bf16[16,2,8,320]{3,2,1,0:T(8,128)(2,1)}, u32[]{:S(2)}, u32[]{:S(2)}) async-start(bf16[16,2,8,320]{3,2,1,0:T(8,128)(2,1)} %bitcast.6.refs_0_), calls=%async_computation.2 | async-start | bytes 393216 | tf_op jit(solution)/shard_map/all_to_all | solution.py:428
  51.1 22.0 %collective-permute-start.2 = (bf16[4,320,128]{2,1,0:T(8,128)(2,1)}, bf16[4,320,128]{2,1,0:T(8,128)(2,1)}, u32[]{:S(2)}, u32[]{:S(2)}) collective-permute-start(bf16[4,320,128]{2,1,0:T(8,128)(2,1)} %get-tuple-element.15), channel_id=1, source_target_pairs={{0,1},{1,0},{2,3},{3,2},{4,5},{5,4},{6,7},{7,6},{8,9},{9,8},{10,11... | collective-permute-start | bytes 983048 | tf_op jit(solution)/shard_map/ppermute | solution.py:433
  53.7 19.5 %copy-start.3 = (f32[320]{0:T(512)S(1)}, f32[320]{0:T(512)}, u32[]{:S(2)}) copy-start(f32[320]{0:T(512)} %one_in.1) | copy-start | bytes 3844
  53.7 19.5 %copy-start.4 = (f32[320]{0:T(512)S(1)}, f32[320]{0:T(512)}, u32[]{:S(2)}) copy-start(f32[320]{0:T(512)} %two_in.1) | copy-start | bytes 3844
  53.7 19.5 %collective-permute-start.3 = (bf16[4,320,128]{2,1,0:T(8,128)(2,1)}, bf16[4,320,128]{2,1,0:T(8,128)(2,1)}, u32[]{:S(2)}, u32[]{:S(2)}) collective-permute-start(bf16[4,320,128]{2,1,0:T(8,128)(2,1)} %get-tuple-element.16), channel_id=1, source_target_pairs={{1,2},{3,4},{5,6},{7,8},{9,10},{11,12},{13,14},{15,16},{17,18},{19... | collective-permute-start | bytes 983048 | tf_op jit(solution)/shard_map/ppermute | solution.py:434
  59.8 12.2 %collective-permute-start.6 = (bf16[2,8,320]{2,1,0:T(8,128)(2,1)S(1)}, bf16[2,8,320]{2,1,0:T(8,128)(2,1)S(1)}, u32[]{:S(2)}, u32[]{:S(2)}) collective-permute-start(bf16[2,8,320]{2,1,0:T(8,128)(2,1)S(1)} %total.1.up_own), channel_id=1, source_target_pairs={{0,2},{2,4},{4,6},{6,8},{8,10},{10,12},{12,14},{14,16},{16,18},{18... | collective-permute-start | bytes 30728 | tf_op jit(solution)/shard_map/ppermute | solution.py:439
  62.4 9.6 %collective-permute-start.5 = (bf16[2,8,320]{2,1,0:T(8,128)(2,1)S(1)}, bf16[2,8,320]{2,1,0:T(8,128)(2,1)S(1)}, u32[]{:S(2)}, u32[]{:S(2)}) collective-permute-start(bf16[2,8,320]{2,1,0:T(8,128)(2,1)S(1)} %total.1.up_own), channel_id=1, source_target_pairs={{1,2},{3,4},{5,6},{7,8},{9,10},{11,12},{13,14},{15,16},{17,18},{19... | collective-permute-start | bytes 30728 | tf_op jit(solution)/shard_map/ppermute | solution.py:438
  70.1 3.1 %collective-permute-start.4 = (bf16[2,8,320]{2,1,0:T(8,128)(2,1)S(1)}, bf16[2,8,320]{2,1,0:T(8,128)(2,1)S(1)}, u32[]{:S(2)}, u32[]{:S(2)}) collective-permute-start(bf16[2,8,320]{2,1,0:T(8,128)(2,1)S(1)} %total.1.up_own), channel_id=1, source_target_pairs={{0,1},{1,0},{2,3},{3,2},{4,5},{5,4},{6,7},{7,6},{8,9},{9,8},{10,11... | collective-permute-start | bytes 30728 | tf_op jit(solution)/shard_map/ppermute | solution.py:437

commit v9 on v8

--- a/solution.py
+++ b/solution.py
@@ -217,7 +217,7 @@
 
 
 def fine_kernel(
-    one, two, left_in, right_in, pair_in, next_in, up_own, up_pair, up_near, up_far, one_in, two_in, space, time,
+    one, two, left_in, right_in, pair_in, next_in, up_own, up_pair, up_next, one_in, two_in, space, time,
     out, left, right, pair, beyond, gains, stack, second, merged, mixed, turned, sems, out_sems,
 ):
     channels, width = one.shape[2:]
@@ -293,7 +293,7 @@
 
     odd = lax.rem(row, 2)
     here = spread(up_own, up_pair, columns_of(odd))
-    further = spread(up_near, up_far, columns_of(1 - odd))
+    further = spread(up_next.at[0], up_next.at[1], columns_of(1 - odd))
     held = (left.at[0], one.at[0], two.at[0], right.at[0])
 
     halves = ((1, 2), (0, 3))
@@ -363,14 +363,14 @@
         leave.wait()
 
 
-def fine_stage(one, two, left, right, pair, beyond, up_own, up_pair, up_near, up_far, gain_one, gain_two, space, time):
+def fine_stage(one, two, left, right, pair, beyond, up_own, up_pair, up_next, gain_one, gain_two, space, time):
     channels, width = one.shape[2:]
     bf16 = jnp.bfloat16
     copied = (left, right, pair, beyond)
     return pl.pallas_call(
         fine_kernel,
         out_shape=jax.ShapeDtypeStruct((2, channels, 4, width), bf16),
-        in_specs=[VMEM] * 2 + [HBM] * 4 + [VMEM] * 8,
+        in_specs=[VMEM] * 2 + [HBM] * 4 + [VMEM] * 7,
         out_specs=HBM,
         scratch_shapes=[pltpu.VMEM(array.shape, array.dtype) for array in copied]
         + [
@@ -385,7 +385,7 @@
         ],
         compiler_params=limit(28),
         name="fine_stage",
-    )(one, two, left, right, pair, beyond, up_own, up_pair, up_near, up_far, gain_one, gain_two, space, time)
+    )(one, two, left, right, pair, beyond, up_own, up_pair, up_next, gain_one, gain_two, space, time)
 
 
 def local(fine, coarse, w_qkv, w_out, w_up, gain_one, conv_space, gain_two, conv_time):
@@ -399,7 +399,6 @@
     partner = [(i, i ^ 1) for i in range(rows)]
     across = [(i, i + 1) for i in range(1, rows - 1, 2)]
     across += [(b, a) for a, b in across]
-    beyond = [(i, i + 2) for i in range(0, rows - 2, 2)] + [(i + 2, i) for i in range(1, rows - 2, 2)]
 
     message = pack(coarse, w_up, share, frames)
     arrived = lax.all_to_all(message, "frame", 0, 0, tiled=True)
@@ -435,10 +434,9 @@
 
     up_own = total(summed)
     up_pair = lax.ppermute(up_own, "row", partner)
-    up_near = lax.ppermute(up_own, "row", across)
-    up_far = lax.ppermute(up_own, "row", beyond)
+    up_next = lax.ppermute(jnp.stack([up_own, up_pair]), "row", across)
     return fine_stage(
-        near_one, near_two, beyond_one, beyond_two, from_pair, from_next, up_own, up_pair, up_near, up_far, gain_one, gain_two, space, time
+        near_one, near_two, beyond_one, beyond_two, from_pair, from_next, up_own, up_pair, up_next, gain_one, gain_two, space, time
     )
 
 

time: 82.6 us -> 83 us (level)
  the two profiles are of different devices: /device:TPU:5 before, /device:TPU:8 now
where the time goes in v9:
time: 83 us; the launch traced here: 82.2 us
  starting transfers between devices  37.8 us (46%)
  waiting for transfers between devices  22.3 us (27%)
  Pallas kernels  16.1 us (19%)
  local copies, waits for them, and re-layouts  5.79 us (7%)
    all_to_all x1, starting transfers between devices, local(): arrived = lax.all_to_all(message, 'frame', 0, 0, tiled=True)  14.8 us
    all_to_all x1, waiting for transfers between devices, local(): arrived = lax.all_to_all(message, 'frame', 0, 0, tiled=True)  9.43 us
    pallas_call x1, Pallas kernels, fine_stage(): pl.pallas_call(fine_kernel, out_shape=jax.ShapeDtypeStruct((2, channels,...  8.63 us
    ppermute x1, waiting for transfers between devices, local(): up_next = lax.ppermute(jnp.stack([up_own, up_pair]), 'row', across)  5.02 us
    all_to_all x1, waiting for transfers between devices, local(): summed = lax.all_to_all(outgoing, 'frame', 0, 0, tiled=True)  4.43 us
    all_to_all x1, starting transfers between devices, local(): lax.all_to_all(copies, 'row', 0, 0, tiled=True, axis_index_groups=groups)  4.3 us
    all_to_all x1, starting transfers between devices, local(): summed = lax.all_to_all(outgoing, 'frame', 0, 0, tiled=True)  4.17 us
    ppermute x1, starting transfers between devices, local(): lax.ppermute(near_one, 'frame', [(i, i ^ 1) for i in range(frames)])  3.81 us
  transfers between devices with their start and end apart: 9, of which 5 were waited for; matrix products, arithmetic and copies ran while one was open for 7% of the time, Pallas kernels for 7%

profile of v9, /device:TPU:8, one launch (start us, length us, event | category | flops | bytes accessed | tf_op | source)
XLA Modules:
  0.0 82.2 jit_solution(13396635446378072265)
XLA Ops:
  0.0 0.0 copy-start.2
  0.0 0.0 copy-start.1
  0.0 0.0 copy-start.5
  0.0 1.8 %pack.1 = bf16[16,72,80]{2,1,0:T(8,128)(2,1)} custom-call(bf16[4,8,80]{2,1,0:T(8,128)(2,1)} %coarse_ref.1, bf16[80,320]{1,0:T(8,128)(2,1)} %up_ref.1), custom_call_target="tpu_custom_call" | custom-call | tf_op jit(solution)/shard_map/pack/pallas_call | solution.py:49
  1.8 14.8 %all-to-all-start = ((bf16[16,72,80]{2,1,0:T(8,128)(2,1)}), bf16[16,72,80]{2,1,0:T(8,128)(2,1)S(1)}, u32[]{:S(2)}, u32[]{:S(2)}) async-start(bf16[16,72,80]{2,1,0:T(8,128)(2,1)} %pack.1), calls=%async_computation | async-start | bytes 589824 | tf_op jit(solution)/shard_map/all_to_all | solution.py:404
  16.6 1.3 %constant_dynamic-slice_fusion = (bf16[1,320,4,128]{3,2,1,0:T(4,128)(2,1)S(1)}, bf16[1,320,4,128]{3,2,1,0:T(4,128)(2,1)S(1)}) fusion(bf16[2,320,4,128]{3,2,1,0:T(4,128)(2,1)} %param.9, s32[]{:T(128)S(6)} %select_n.15, s32[]{:T(128)S(6)} %select_n.14), kind=kLoop, calls=%fused_computation.3 | loop fusion | bytes 1310728 | tf_op jit(solution)/shard_map/dynamic_slice | solution.py:408
  18.0 3.8 %collective-permute-start = (bf16[1,4,320,128]{3,2,1,0:T(8,128)(2,1)S(1)}, bf16[1,4,320,128]{3,2,1,0:T(8,128)(2,1)S(1)}, u32[]{:S(2)}, u32[]{:S(2)}) collective-permute-start(bf16[1,4,320,128]{3,2,1,0:T(8,128)(2,1)S(1)} %bitcast.17), channel_id=1, source_target_pairs={{0,32},{32,0},{64,96},{96,64},{128,160},{160,128},{192,224},{224,1... | collective-permute-start | bytes 983048 | tf_op jit(solution)/shard_map/ppermute | solution.py:411
  21.9 1.4 %collective-permute-start.1 = (bf16[1,4,320,128]{3,2,1,0:T(8,128)(2,1)S(1)}, bf16[1,4,320,128]{3,2,1,0:T(8,128)(2,1)}, u32[]{:S(2)}, u32[]{:S(2)}) collective-permute-start(bf16[1,4,320,128]{3,2,1,0:T(8,128)(2,1)S(1)} %bitcast.20), channel_id=1, source_target_pairs={{32,64},{96,128},{160,192},{224,256},{288,320},{352,384},{416,448}... | collective-permute-start | bytes 983048 | tf_op jit(solution)/shard_map/ppermute | solution.py:412
  23.3 9.4 %all-to-all-done.arrived_ref = bf16[16,72,80]{2,1,0:T(8,128)(2,1)S(1)} async-done(((bf16[16,72,80]{2,1,0:T(8,128)(2,1)}), bf16[16,72,80]{2,1,0:T(8,128)(2,1)S(1)}, u32[]{:S(2)}, u32[]{:S(2)}) %all-to-all-start) | async-done | bytes 184352 | tf_op jit(solution)/shard_map/all_to_all | solution.py:404
  32.7 0.0 copy-done.1
  32.7 0.9 %fold.1 = (bf16[8,40,80]{2,1,0:T(8,128)(2,1)}, bf16[32,1280]{1,0:T(8,128)(2,1)S(1)}) custom-call(bf16[16,72,80]{2,1,0:T(8,128)(2,1)S(1)} %all-to-all-done.arrived_ref, bf16[80,1280]{1,0:T(8,128)(2,1)S(1)} %copy-done.1), custom_call_target="tpu_custom_call" | custom-call | tf_op jit(solution)/shard_map/fold/pallas_call | solution.py:82
  33.6 4.3 %all-to-all-start.1 = ((bf16[8,40,80]{2,1,0:T(8,128)(2,1)}), bf16[8,40,80]{2,1,0:T(8,128)(2,1)S(1)}, u32[]{:S(2)}, u32[]{:S(2)}) async-start(bf16[8,40,80]{2,1,0:T(8,128)(2,1)} %get-tuple-element.12), calls=%async_computation.1 | async-start | bytes 163840 | tf_op jit(solution)/shard_map/all_to_all | solution.py:415
  37.9 0.0 copy-done.2
  37.9 0.0 copy-done.5
  38.0 0.4 attend.1.mine_ref
  38.4 0.0 copy-start
  38.4 3.0 %copy.16._.space = bf16[320,2880]{1,0:T(8,128)(2,1)S(1)} copy(bf16[320,2880]{0,1:T(8,128)(2,1)} %bitcast.27) | data formatting | bytes 3686400 | tf_op jit(solution)/shard_map/reshape | solution.py:418
  41.4 2.3 %all-to-all-done.1 = bf16[8,40,80]{2,1,0:T(8,128)(2,1)S(1)} async-done(((bf16[8,40,80]{2,1,0:T(8,128)(2,1)}), bf16[8,40,80]{2,1,0:T(8,128)(2,1)S(1)}, u32[]{:S(2)}, u32[]{:S(2)}) %all-to-all-start.1) | async-done | bytes 51232 | tf_op jit(solution)/shard_map/all_to_all | solution.py:415
  43.6 0.0 copy-done
  43.6 0.9 %project.1 = bf16[32,8,320]{2,1,0:T(8,128)(2,1)} custom-call(bf16[2,4,8,80]{3,2,1,0:T(8,128)(2,1)S(1)} %attend.1.mine_ref, bf16[320,80]{1,0:T(8,128)(2,1)S(1)} %bitcast.23, bf16[80,320]{1,0:T(8,128)(2,1)S(1)} %copy-done, bf16[320,2880]{1,0:T(8,128)(2,1)S(1)} %copy.16._.space), custom_call_target="tpu_custom_call" | custom-call | tf_op jit(solution)/shard_map/project/pallas_call | solution.py:157
  44.5 4.2 %all-to-all-start.2 = ((bf16[16,2,8,320]{3,2,1,0:T(8,128)(2,1)}), bf16[16,2,8,320]{3,2,1,0:T(8,128)(2,1)}, u32[]{:S(2)}, u32[]{:S(2)}) async-start(bf16[16,2,8,320]{3,2,1,0:T(8,128)(2,1)} %bitcast.6.refs_0_), calls=%async_computation.2 | async-start | bytes 393216 | tf_op jit(solution)/shard_map/all_to_all | solution.py:427
  48.7 1.4 %copy.17.refs_1_.time = bf16[320,960]{1,0:T(8,128)(2,1)S(1)} copy(bf16[320,960]{0,1:T(8,128)(2,1)} %bitcast.28) | data formatting | bytes 1228800 | tf_op jit(solution)/shard_map/reshape | solution.py:430
  50.1 0.0 collective-permute-done.left_ref.left_in
  50.1 0.0 collective-permute-done.1.right_ref.right_in
  50.1 2.5 %edge_rows.1 = (bf16[4,320,128]{2,1,0:T(8,128)(2,1)}, bf16[4,320,128]{2,1,0:T(8,128)(2,1)}) custom-call(bf16[1,4,320,128]{3,2,1,0:T(8,128)(2,1)S(1)} %collective-permute-done.left_ref.left_in, bf16[1,4,320,128]{3,2,1,0:T(8,128)(2,1)S(1)} %bitcast.18, bf16[1,4,320,128]{3,2,1,0:T(8,128)(2,1)S(1)} %bitcast.21, ...), custom_call_target="tpu_custom_call" | custom-call | tf_op jit(solution)/shard_map/edge_rows/pallas_call | solution.py:189
  52.6 1.9 %collective-permute-start.2 = (bf16[4,320,128]{2,1,0:T(8,128)(2,1)}, bf16[4,320,128]{2,1,0:T(8,128)(2,1)}, u32[]{:S(2)}, u32[]{:S(2)}) collective-permute-start(bf16[4,320,128]{2,1,0:T(8,128)(2,1)} %get-tuple-element.15), channel_id=1, source_target_pairs={{0,1},{1,0},{2,3},{3,2},{4,5},{5,4},{6,7},{7,6},{8,9},{9,8},{10,11... | collective-permute-start | bytes 983048 | tf_op jit(solution)/shard_map/ppermute | solution.py:432
  54.5 0.0 copy-start.3
  54.5 0.0 copy-start.4
  54.5 3.3 %collective-permute-start.3 = (bf16[4,320,128]{2,1,0:T(8,128)(2,1)}, bf16[4,320,128]{2,1,0:T(8,128)(2,1)}, u32[]{:S(2)}, u32[]{:S(2)}) collective-permute-start(bf16[4,320,128]{2,1,0:T(8,128)(2,1)} %get-tuple-element.16), channel_id=1, source_target_pairs={{1,2},{3,4},{5,6},{7,8},{9,10},{11,12},{13,14},{15,16},{17,18},{19... | collective-permute-start | bytes 983048 | tf_op jit(solution)/shard_map/ppermute | solution.py:433
  57.9 4.4 %all-to-all-done.2.summed_ref = bf16[16,2,8,320]{3,2,1,0:T(8,128)(2,1)} async-done(((bf16[16,2,8,320]{3,2,1,0:T(8,128)(2,1)}), bf16[16,2,8,320]{3,2,1,0:T(8,128)(2,1)}, u32[]{:S(2)}, u32[]{:S(2)}) %all-to-all-start.2) | async-done | bytes 163872 | tf_op jit(solution)/shard_map/all_to_all | solution.py:427
  62.3 1.0 %total.1.up_own = bf16[2,8,320]{2,1,0:T(8,128)(2,1)S(1)} custom-call(bf16[16,2,8,320]{3,2,1,0:T(8,128)(2,1)} %all-to-all-done.2.summed_ref), custom_call_target="tpu_custom_call" | custom-call | flops 10000000000 | tf_op jit(solution)/shard_map/total/pallas_call | solution.py:208
  63.3 1.9 %collective-permute-start.4 = (bf16[2,8,320]{2,1,0:T(8,128)(2,1)S(1)}, bf16[2,8,320]{2,1,0:T(8,128)(2,1)S(1)}, u32[]{:S(2)}, u32[]{:S(2)}) collective-permute-start(bf16[2,8,320]{2,1,0:T(8,128)(2,1)S(1)} %total.1.up_own), channel_id=1, source_target_pairs={{0,1},{1,0},{2,3},{3,2},{4,5},{5,4},{6,7},{7,6},{8,9},{9,8},{10,11... | collective-permute-start | bytes 30728 | tf_op jit(solution)/shard_map/ppermute | solution.py:436
  65.2 1.1 %collective-permute-done.4.up_pair = bf16[2,8,320]{2,1,0:T(8,128)(2,1)S(1)} collective-permute-done((bf16[2,8,320]{2,1,0:T(8,128)(2,1)S(1)}, bf16[2,8,320]{2,1,0:T(8,128)(2,1)S(1)}, u32[]{:S(2)}, u32[]{:S(2)}) %collective-permute-start.4) | collective-permute-done | bytes 10272 | tf_op jit(solution)/shard_map/ppermute | solution.py:436
  66.3 2.2 %collective-permute-start.5 = (bf16[2,2,8,320]{3,2,1,0:T(8,128)(2,1)S(1)}, bf16[2,2,8,320]{3,2,1,0:T(8,128)(2,1)S(1)}, u32[]{:S(2)}, u32[]{:S(2)}) collective-permute-start(bf16[2,2,8,320]{3,2,1,0:T(8,128)(2,1)S(1)} %pad_maximum_fusion), channel_id=1, source_target_pairs={{1,2},{3,4},{5,6},{7,8},{9,10},{11,12},{13,14},{15,16},{17,18},{19... | collective-permute-start | bytes 61448 | tf_op jit(solution)/shard_map/ppermute | solution.py:437
  68.5 0.0 collective-permute-done.2.pair_in
  68.6 0.0 collective-permute-done.3.next_in
  68.6 5.0 %collective-permute-done.5.up_next = bf16[2,2,8,320]{3,2,1,0:T(8,128)(2,1)S(1)} collective-permute-done((bf16[2,2,8,320]{3,2,1,0:T(8,128)(2,1)S(1)}, bf16[2,2,8,320]{3,2,1,0:T(8,128)(2,1)S(1)}, u32[]{:S(2)}, u32[]{:S(2)}) %collective-permute-start.5) | collective-permute-done | bytes 20512 | tf_op jit(solution)/shard_map/ppermute | solution.py:437
  73.6 0.0 copy-done.3
  73.6 0.0 copy-done.4
  73.6 8.6 %fine_stage.1 = bf16[2,320,4,128]{3,2,1,0:T(4,128)(2,1)} custom-call(bf16[1,4,320,128]{3,2,1,0:T(8,128)(2,1)S(1)} %bitcast.19, bf16[1,4,320,128]{3,2,1,0:T(8,128)(2,1)S(1)} %bitcast.22, bf16[1,4,320,128]{3,2,1,0:T(8,128)(2,1)S(1)} %collective-permute-done.left_ref.left_in, bf16[1,4,320,128]{3,2,1,0:T(8,128)(2,1)} %collective-permute-done.1.right_ref.right_in, ...), custom_call_target="tpu_custom_call" | custom-call | tf_op jit(solution)/shard_map/fine_stage/pallas_call | solution.py:370
  (3 shorter events, 0.1 us)
Async XLA Ops:
  0.0 37.9 %copy-start.2 = (bf16[4,8,80]{2,1,0:T(8,128)(2,1)S(1)}, bf16[4,8,80]{2,1,0:T(8,128)(2,1)}, u32[]{:S(2)}) copy-start(bf16[4,8,80]{2,1,0:T(8,128)(2,1)} %coarse_ref.1) | copy-start | bytes 15364
  0.0 32.7 %copy-start.1 = (bf16[80,1280]{1,0:T(8,128)(2,1)S(1)}, bf16[80,1280]{1,0:T(8,128)(2,1)}, u32[]{:S(2)}) copy-start(bf16[80,1280]{1,0:T(8,128)(2,1)} %out_w_ref.1) | copy-start | bytes 614404
  0.0 37.9 %copy-start.5 = (bf16[3,1280,80]{1,2,0:T(8,128)(2,1)S(1)}, bf16[3,1280,80]{1,2,0:T(8,128)(2,1)}, u32[]{:S(2)}) copy-start(bf16[3,1280,80]{1,2,0:T(8,128)(2,1)} %param.11) | copy-start | bytes 1843204
  1.8 30.9 %all-to-all-start = ((bf16[16,72,80]{2,1,0:T(8,128)(2,1)}), bf16[16,72,80]{2,1,0:T(8,128)(2,1)S(1)}, u32[]{:S(2)}, u32[]{:S(2)}) async-start(bf16[16,72,80]{2,1,0:T(8,128)(2,1)} %pack.1), calls=%async_computation | async-start | bytes 589824 | tf_op jit(solution)/shard_map/all_to_all | solution.py:404
  18.0 32.1 %collective-permute-start = (bf16[1,4,320,128]{3,2,1,0:T(8,128)(2,1)S(1)}, bf16[1,4,320,128]{3,2,1,0:T(8,128)(2,1)S(1)}, u32[]{:S(2)}, u32[]{:S(2)}) collective-permute-start(bf16[1,4,320,128]{3,2,1,0:T(8,128)(2,1)S(1)} %bitcast.17), channel_id=1, source_target_pairs={{0,32},{32,0},{64,96},{96,64},{128,160},{160,128},{192,224},{224,1... | collective-permute-start | bytes 983048 | tf_op jit(solution)/shard_map/ppermute | solution.py:411
  21.9 28.2 %collective-permute-start.1 = (bf16[1,4,320,128]{3,2,1,0:T(8,128)(2,1)S(1)}, bf16[1,4,320,128]{3,2,1,0:T(8,128)(2,1)}, u32[]{:S(2)}, u32[]{:S(2)}) collective-permute-start(bf16[1,4,320,128]{3,2,1,0:T(8,128)(2,1)S(1)} %bitcast.20), channel_id=1, source_target_pairs={{32,64},{96,128},{160,192},{224,256},{288,320},{352,384},{416,448}... | collective-permute-start | bytes 983048 | tf_op jit(solution)/shard_map/ppermute | solution.py:412
  33.6 10.0 %all-to-all-start.1 = ((bf16[8,40,80]{2,1,0:T(8,128)(2,1)}), bf16[8,40,80]{2,1,0:T(8,128)(2,1)S(1)}, u32[]{:S(2)}, u32[]{:S(2)}) async-start(bf16[8,40,80]{2,1,0:T(8,128)(2,1)} %get-tuple-element.12), calls=%async_computation.1 | async-start | bytes 163840 | tf_op jit(solution)/shard_map/all_to_all | solution.py:415
  38.4 5.3 %copy-start = (bf16[80,320]{1,0:T(8,128)(2,1)S(1)}, bf16[80,320]{1,0:T(8,128)(2,1)}, u32[]{:S(2)}) copy-start(bf16[80,320]{1,0:T(8,128)(2,1)} %up_ref.1) | copy-start | bytes 153604
  44.5 17.8 %all-to-all-start.2 = ((bf16[16,2,8,320]{3,2,1,0:T(8,128)(2,1)}), bf16[16,2,8,320]{3,2,1,0:T(8,128)(2,1)}, u32[]{:S(2)}, u32[]{:S(2)}) async-start(bf16[16,2,8,320]{3,2,1,0:T(8,128)(2,1)} %bitcast.6.refs_0_), calls=%async_computation.2 | async-start | bytes 393216 | tf_op jit(solution)/shard_map/all_to_all | solution.py:427
  52.6 16.0 %collective-permute-start.2 = (bf16[4,320,128]{2,1,0:T(8,128)(2,1)}, bf16[4,320,128]{2,1,0:T(8,128)(2,1)}, u32[]{:S(2)}, u32[]{:S(2)}) collective-permute-start(bf16[4,320,128]{2,1,0:T(8,128)(2,1)} %get-tuple-element.15), channel_id=1, source_target_pairs={{0,1},{1,0},{2,3},{3,2},{4,5},{5,4},{6,7},{7,6},{8,9},{9,8},{10,11... | collective-permute-start | bytes 983048 | tf_op jit(solution)/shard_map/ppermute | solution.py:432
  54.5 19.1 %copy-start.3 = (f32[320]{0:T(512)S(1)}, f32[320]{0:T(512)}, u32[]{:S(2)}) copy-start(f32[320]{0:T(512)} %one_in.1) | copy-start | bytes 3844
  54.5 19.1 %copy-start.4 = (f32[320]{0:T(512)S(1)}, f32[320]{0:T(512)}, u32[]{:S(2)}) copy-start(f32[320]{0:T(512)} %two_in.1) | copy-start | bytes 3844
  54.5 14.0 %collective-permute-start.3 = (bf16[4,320,128]{2,1,0:T(8,128)(2,1)}, bf16[4,320,128]{2,1,0:T(8,128)(2,1)}, u32[]{:S(2)}, u32[]{:S(2)}) collective-permute-start(bf16[4,320,128]{2,1,0:T(8,128)(2,1)} %get-tuple-element.16), channel_id=1, source_target_pairs={{1,2},{3,4},{5,6},{7,8},{9,10},{11,12},{13,14},{15,16},{17,18},{19... | collective-permute-start | bytes 983048 | tf_op jit(solution)/shard_map/ppermute | solution.py:433
  63.3 3.1 %collective-permute-start.4 = (bf16[2,8,320]{2,1,0:T(8,128)(2,1)S(1)}, bf16[2,8,320]{2,1,0:T(8,128)(2,1)S(1)}, u32[]{:S(2)}, u32[]{:S(2)}) collective-permute-start(bf16[2,8,320]{2,1,0:T(8,128)(2,1)S(1)} %total.1.up_own), channel_id=1, source_target_pairs={{0,1},{1,0},{2,3},{3,2},{4,5},{5,4},{6,7},{7,6},{8,9},{9,8},{10,11... | collective-permute-start | bytes 30728 | tf_op jit(solution)/shard_map/ppermute | solution.py:436
  66.3 7.3 %collective-permute-start.5 = (bf16[2,2,8,320]{3,2,1,0:T(8,128)(2,1)S(1)}, bf16[2,2,8,320]{3,2,1,0:T(8,128)(2,1)S(1)}, u32[]{:S(2)}, u32[]{:S(2)}) collective-permute-start(bf16[2,2,8,320]{3,2,1,0:T(8,128)(2,1)S(1)} %pad_maximum_fusion), channel_id=1, source_target_pairs={{1,2},{3,4},{5,6},{7,8},{9,10},{11,12},{13,14},{15,16},{17,18},{19... | collective-permute-start | bytes 61448 | tf_op jit(solution)/shard_map/ppermute | solution.py:437
